TPU v7x, 32 devices: a whole 2x2x4 slice. The times are simulated.
32 devices in a mesh: groups: 2 (over y), region: 16 (over z, x, core).
Axes of the slice: x: 2, y: 2, z: 4, core: 2. Of those that a mesh axis runs over, the one named last changes fastest.
Arguments:
- ray_code: bfloat16 [8192, 128], P(('groups', 'region')), parts along dimension 0, may hold values from -6 to 6
- seg_region: int32 [8192, 4], P(('groups', 'region')), parts along dimension 0, may hold values from 0 to 15, all different within a row; in each aligned block of 256 rows (0 to 255, 256 to 511, ...) at most 128 rows name the same one
- seg_count: int32 [8192, 4], P(('groups', 'region')), parts along dimension 0, may hold values from 1 to 16
- pixel_of_ray: int32 [8192], P(('groups', 'region')), parts along dimension 0, may hold values from 0 to 4095, as said below
- sample_code: bfloat16 [16, 16, 128], P('region'), may hold values from -5 to 5
- w_hidden: bfloat16 [16, 128, 128], P('region'), may hold values from -0.5 to 0.5
- w_feat: bfloat16 [16, 128, 64], P('region'), may hold values from -0.5 to 0.5
- w_density: bfloat16 [16, 128], P('region'), may hold values from -0.5 to 0.5
- decoder: bfloat16 [576, 384], replicated, may hold values from -0.25 to 0.25
- target: bfloat16 [8192, 384], P(('groups', 'region')), parts along dimension 0, may hold values from -6 to 6
Outputs:
- hidden_grad: float32 [16, 256, 128], P('region', 'groups'), parts along dimension 1
- feat_grad: float32 [16, 256, 64], P('region', 'groups'), parts along dimension 1
- density_grad: float32 [16, 256], P('region', 'groups'), parts along dimension 1
- code_grad: float32 [16, 32, 128], P('region', 'groups'), parts along dimension 1
There are 2 independent parts, one for each index of `groups`. A program takes and returns all parts, laid end to end along the dimension named above; an argument that names none is the same for every part. Nothing has to cross between parts.
Inputs may be any that keep to these rules, and one draw needn't show every extreme that they name: `seg_region`: each ray lists 4 different regions, front to back. Among the rays of one device no region is listed more than 128 times, a bound that some block reaches. `pixel_of_ray`: every pixel is named by exactly one ray. The rays of one device name exactly 16 pixels in each block of 256 consecutive pixels.
All inputs are finite; a program needn't handle non-finite values.
Results may differ from a plain program's by a relative error of at most 0.0085.
The roundings to bfloat16 on the way count: a program that leaves them out, or rounds other values in their place, can miss the bound.
Values may be sent and summed in bfloat16 or wider, within the bound.
No kernel may reach another device: no remote copies, remote signals or barrier semaphores. Data moves between devices by JAX's collectives and lax.ppermute only.
A program may use at most 192 MiB of HBM per device.

v0:
```python
import functools

import jax
import jax.numpy as jnp
from jax import lax
from jax.experimental import pallas as pl
from jax.experimental.pallas import tpu as pltpu
from jax.sharding import PartitionSpec as P

IW = 128
STEP = 0.08
F32 = jnp.float32
BF16 = jnp.bfloat16
LANES = 128

WF_AT = 128
SAMPLE_AT = 192
META_AT = 208
RAYS_AT = 224
G2_AT = 192
DG_AT = 208
PART_ROWS = 224

PARAMS = pltpu.CompilerParams(vmem_limit_bytes=52 << 20)


def iota(shape, dim):
    return lax.broadcasted_iota(jnp.int32, shape, dim)


def dot(lhs, rhs, left=1, right=0):
    return lax.dot_general(lhs, rhs, (((left,), (right,)), ((), ())), preferred_element_type=F32)


def split(values):
    high = values.astype(BF16)
    return high, (values - high.astype(F32)).astype(BF16)


def running_sum(values):
    rows = values.shape[0]
    row = iota(values.shape, 0)
    step = 1
    while step < rows:
        values = values + jnp.where(row >= step, pltpu.roll(values, step, 0), 0.0)
        step *= 2
    return values


def pack_kernel(half, group, room, pix_ref, reg_ref, cnt_ref, code_ref, samp_ref, wh_ref, wf_ref, wd_ref, out_ref, meta_ref):
    rays = code_ref.shape[0]
    regions = 2 * half
    shift = rays.bit_length() - 1
    pix = pix_ref[...]
    tile = lax.shift_right_logical(pix, shift)
    spot = pix & (rays - 1)
    mine = iota((regions, rays), 0) == tile
    mine_f = jnp.where(mine, 1.0, 0.0)
    earlier = jnp.where(iota((rays, rays), 0) < iota((rays, rays), 1), 1.0, 0.0).astype(BF16)
    counts = dot(mine_f.astype(BF16), earlier)
    rank = jnp.sum(counts * mine_f, axis=0, keepdims=True).astype(jnp.int32)
    row_place = lax.shift_right_logical(tile, 1) * room + (tile & 1) * group + rank
    lane_place = tile * group + rank
    meta_ref[...] = jnp.zeros(meta_ref.shape, F32)
    meta_ref[1:2, :] = spot.astype(F32)
    meta_ref[2:6, :] = reg_ref[...].astype(F32)
    meta_ref[6:10, :] = cnt_ref[...].astype(F32)
    row_hot = jnp.where(iota((half * room, rays), 0) == row_place, 1.0, 0.0).astype(BF16)
    codes = dot(row_hot, code_ref[...]).astype(BF16)
    lane_hot = jnp.where(iota((rays, rays), 0) == lane_place, 1.0, 0.0).astype(BF16)
    meta = dot(meta_ref[...].astype(BF16), lane_hot, 1, 1)
    meta_ref[...] = meta
    wh_t = wh_ref[0].astype(F32).T.astype(BF16)
    wf_t = wf_ref[0].astype(F32).T.astype(BF16)
    samples = samp_ref[0]
    density = wd_ref[...].astype(F32)
    first = iota((16, LANES), 0) == 0
    for chip in range(half):
        out_ref[chip, 0:WF_AT] = wh_t
        out_ref[chip, WF_AT:SAMPLE_AT] = wf_t
        out_ref[chip, SAMPLE_AT:META_AT] = samples
        here = pltpu.roll(meta, (rays - chip * 2 * group) % rays, 1)[:, :LANES]
        out_ref[chip, META_AT:RAYS_AT] = jnp.where(first, density, here).astype(BF16)
        out_ref[chip, RAYS_AT : RAYS_AT + room] = codes[chip * room : (chip + 1) * room]


def pick(source_ref, wanted, out_ref):
    regions = source_ref.shape[0]
    segs = len(wanted)
    for part in range(2):
        lanes = slice(part * LANES, (part + 1) * LANES)
        rel = [jnp.broadcast_to(row[:, lanes], (8, LANES)) for row in wanted]

        def step(index, carry):
            rows = pl.ds(pl.multiple_of(index * 8, 8), 8)
            found = [jnp.zeros((8, LANES), F32)] * segs
            for region in range(regions):
                value = source_ref[region, rows, lanes]
                found = [jnp.where(rel[k] == region, value, found[k]) for k in range(segs)]
            for k in range(segs):
                out_ref[2 * k + part, rows, :] = found[k]
            return carry

        lax.fori_loop(0, 16, step, 0)


def spread(source_ref, wanted, region):
    segs = len(wanted)
    pieces = []
    for part in range(2):
        lanes = slice(part * LANES, (part + 1) * LANES)
        total = jnp.zeros((LANES, LANES), F32)
        for k in range(segs):
            total = jnp.where(wanted[k][:, lanes] == region, source_ref[2 * k + part], total)
        pieces.append(total)
    return jnp.concatenate(pieces, axis=1)


def block_of(a_ref, b_ref, half, region):
    return (a_ref, region) if region < half else (b_ref, region - half)


def seg_hot(wanted, regions):
    return jnp.concatenate(
        [jnp.where(iota((regions, row.shape[1]), 0) == row, 1.0, 0.0) for row in wanted], axis=1
    )


def expand_samples(table_ref, hot2, base_ref):
    tiles = base_ref.shape[0]

    def one(sample):
        values = dot(table_ref[sample], hot2, 0, 0)
        at = slice(sample * LANES, (sample + 1) * LANES)
        for tile in range(tiles):
            base_ref[tile, at, :] = values[:, tile * LANES : (tile + 1) * LANES]

    for sample in range(table_ref.shape[0]):
        one(sample)


def forward_kernel(
    half, group, room, a_ref, b_ref,
    image_ref, a_out, table_ref, att_hw_ref, weight_ref, pass_ref, slope_ref, att_ref, rel_ref, codes_ref,
    meta_ref, plain_ref, proj_ref, base_ref, h_ref, row_ref, ahead_ref,
):
    regions = 2 * half
    rays = codes_ref.shape[0]
    segs = rel_ref.shape[0]
    samples = weight_ref.shape[1]
    core = lax.axis_index("region") & 1
    per_tile = LANES // room
    lane = iota((16, LANES), 1)
    chunk = lax.div(lane, room)
    inside = lane - chunk * room
    mine = (inside < 2 * group) & (lax.div(inside, group) == core)
    for tile in range(regions // per_tile):
        total = jnp.zeros((16, LANES), F32)
        for spot in range(per_tile):
            ref, at = block_of(a_ref, b_ref, half, tile * per_tile + spot)
            block = ref[at, META_AT:RAYS_AT].astype(F32)
            total = jnp.where(chunk == spot, pltpu.roll(block, spot * room, 1), total)
        meta_ref[:, tile * LANES : (tile + 1) * LANES] = jnp.where(mine, total, -1.0)
    meta_src = meta_ref[...]
    places = regions * room
    to_pixel = jnp.where(
        iota((rays, places), 0).astype(F32) == meta_src[1:2, :], 1.0, 0.0
    ).astype(BF16)
    sources = jnp.concatenate(
        [a_ref[i, RAYS_AT : RAYS_AT + room] for i in range(half)]
        + [b_ref[i, RAYS_AT : RAYS_AT + room] for i in range(half)],
        axis=0,
    )
    codes = dot(to_pixel, sources)
    codes_ref[...] = codes.astype(BF16)
    codes_t = codes.T.astype(BF16)
    meta = dot(meta_src.astype(BF16), to_pixel, 1, 1)
    region = meta[2 : 2 + segs].astype(jnp.int32)
    rel = jnp.bitwise_xor(region & 1, core) * half + lax.shift_right_logical(region, 1)
    rel_ref[...] = rel
    for k in range(segs):
        for part in range(2):
            row_ref[2 * k + part] = meta[6 + k : 7 + k, part * LANES : (part + 1) * LANES]
    wanted = [rel_ref[k : k + 1, :] for k in range(segs)]
    for r in range(regions):
        ref, at = block_of(a_ref, b_ref, half, r)
        w_t = ref[at, 0:WF_AT]
        proj_ref[r] = dot(w_t, codes_t)
        own = dot(ref[at, SAMPLE_AT:META_AT], w_t, 1, 1)
        plain_ref[0:samples, r, :] = own
        plain_ref[samples, r : r + 1, :] = ref[at, META_AT:RAYS_AT].astype(F32)[0:1, :]
    for s in range(samples + 1):
        high, low = split(plain_ref[s])
        table_ref[s] = jnp.concatenate([high, low], axis=0)
    pick(proj_ref, wanted, a_out)
    hot = seg_hot(wanted, regions).astype(BF16)
    expand_samples(table_ref, jnp.concatenate([hot, hot], axis=0), base_ref)
    ahead_ref[...] = jnp.zeros(ahead_ref.shape, F32)
    order = iota((samples, LANES), 0).astype(F32)

    def step(tile, carry):
        sums = [jnp.zeros((8, LANES), F32)] * samples
        for ht in range(16):
            rows = slice(ht * 8, ht * 8 + 8)
            a = a_out[tile, rows, :]
            wd = base_ref[tile, samples * LANES + ht * 8 : samples * LANES + ht * 8 + 8, :]
            for s in range(samples):
                h = jnp.maximum(a + base_ref[tile, s * LANES + ht * 8 : s * LANES + ht * 8 + 8, :], 0.0)
                h_ref[ht * samples + s] = h
                sums[s] = sums[s] + h * wd
        density = jnp.concatenate([jnp.sum(v, axis=0, keepdims=True) for v in sums], axis=0)
        part = tile & 1
        live = order < row_ref[tile]
        soft = jnp.maximum(density, 0.0) + jnp.log1p(jnp.exp(-jnp.abs(density)))
        thick = jnp.where(live, STEP * soft, 0.0)
        through = running_sum(thick)
        passing = jnp.exp(-(through - thick))
        keeping = jnp.exp(-thick)
        weight = passing * (1.0 - keeping)
        weight_ref[tile] = weight
        pass_ref[tile] = passing * keeping
        slope_ref[tile] = jnp.where(live, STEP / (1.0 + jnp.exp(-density)), 0.0)
        before = ahead_ref[part]
        att = jnp.exp(-before)
        ahead_ref[part] = before + through[samples - 1 : samples, :]
        att_ref[tile] = att
        scale = [jnp.broadcast_to(weight[s : s + 1, :] * att, (8, LANES)) for s in range(samples)]
        for ht in range(16):
            total = scale[0] * h_ref[ht * samples]
            for s in range(1, samples):
                total = total + scale[s] * h_ref[ht * samples + s]
            att_hw_ref[tile, ht * 8 : ht * 8 + 8, :] = total
        return carry

    lax.fori_loop(0, 2 * segs, step, 0)
    feat = jnp.zeros(image_ref.shape, F32)
    for r in range(regions):
        ref, at = block_of(a_ref, b_ref, half, r)
        high, low = split(spread(att_hw_ref, wanted, r))
        wf_t = ref[at, WF_AT:SAMPLE_AT]
        feat = feat + dot(wf_t, high) + dot(wf_t, low)
    image_ref[...] = feat.astype(BF16)


def shifted(values, by):
    lane = iota(values.shape, 1)
    if by == 0:
        return values
    if by > 0:
        return jnp.where(lane == 0, 0.0, pltpu.roll(values, 1, 1))
    return jnp.where(lane == LANES - 1, 0.0, pltpu.roll(values, LANES - 1, 1))


def backward_kernel(
    half, own_ref, inner_ref, cross_ref, tgt_ref, tin_ref, tcr_ref, dec_ref, dect_ref,
    wa_ref, wb_ref, a_ref, table_ref, att_hw_ref, weight_ref, pass_ref, slope_ref, att_ref, rel_ref, codes_ref,
    mine_ref, other_ref,
    patch_ref, proj_ref, q_ref, base_ref, h_ref, gp_ref, g1_ref, hd_ref, tail_ref, row_ref,
):
    regions = 2 * half
    feats, rays = own_ref.shape
    segs = rel_ref.shape[0]
    samples = weight_ref.shape[1]
    me = lax.axis_index("region")
    core = me & 1
    own = own_ref[...].astype(F32)
    inner = inner_ref[...].astype(F32)
    cross = cross_ref[...].astype(F32)
    top = jnp.where(core == 0, cross, inner)
    bottom = jnp.where(core == 0, inner, cross)
    rows = [v[:, i * IW : (i + 1) * IW] for v in (top, own, bottom) for i in range(2)]
    for at, row in enumerate(rows):
        for dx in range(3):
            piece = shifted(row, 1 - dx).astype(BF16)
            for dy in range(3):
                if 0 <= at - dy < 4:
                    patch_ref[(3 * dy + dx) * feats : (3 * dy + dx + 1) * feats, (at - dy) * IW : (at - dy + 1) * IW] = piece
    tin = tin_ref[...].astype(F32)
    tcr = tcr_ref[...].astype(F32)
    t_top = jnp.where(core == 0, tcr, tin)
    t_bottom = jnp.where(core == 0, tin, tcr)
    decoded = dot(dect_ref[...], patch_ref[...])
    tgt = tgt_ref[...].astype(F32)
    g_top = jnp.where(me > 0, decoded[:, 0:IW] - t_top, 0.0)
    g_own = decoded[:, IW : 3 * IW] - tgt
    g_bottom = jnp.where(me < regions - 1, decoded[:, 3 * IW :] - t_bottom, 0.0)
    grad_dec = jnp.concatenate([g_top, g_own, g_bottom], axis=1).astype(BF16)
    grad_patch = dot(dec_ref[...], grad_dec)
    image_rows = []
    for i in range(2):
        total = jnp.zeros((feats, IW), F32)
        for dx in range(3):
            term = jnp.zeros((feats, IW), F32)
            for dy in range(3):
                at = (3 * dy + dx) * feats
                term = term + grad_patch[at : at + feats, (i - dy + 2) * IW : (i - dy + 3) * IW]
            total = total + shifted(term, dx - 1)
        image_rows.append(total)
    grad_ray = jnp.concatenate(image_rows, axis=1)
    g_high, g_low = split(grad_ray)
    g_both = jnp.concatenate([g_high, g_low], axis=0)
    wanted = [rel_ref[k : k + 1, :] for k in range(segs)]

    for r in range(regions):
        ref, at = block_of(wa_ref, wb_ref, half, r)
        out, to = block_of(mine_ref, other_ref, half, r)
        wf_t = ref[at]
        proj_ref[r] = dot(jnp.concatenate([wf_t, wf_t], axis=0), g_both, 0, 0)
        held = spread(att_hw_ref, wanted, r).astype(BF16)
        out[to, WF_AT:G2_AT] = dot(g_high, held, 1, 1).astype(BF16)
    pick(proj_ref, wanted, q_ref)
    hot = seg_hot(wanted, regions).astype(BF16)
    expand_samples(table_ref, jnp.concatenate([hot, hot], axis=0), base_ref)
    for part in range(2):
        later = jnp.zeros((1, LANES), F32)
        for k in reversed(range(segs)):
            row_ref[2 * k + part] = -later
            pulled = jnp.sum(att_hw_ref[2 * k + part] * q_ref[2 * k + part], axis=0, keepdims=True)
            later = later + pulled

    def step(tile, carry):
        att = jnp.broadcast_to(att_ref[tile], (8, LANES))
        sums = [jnp.zeros((8, LANES), F32)] * samples
        for ht in range(16):
            rows = slice(ht * 8, ht * 8 + 8)
            a = a_ref[tile, rows, :]
            q = q_ref[tile, rows, :] * att
            q_ref[tile, rows, :] = q
            for s in range(samples):
                h = jnp.maximum(a + base_ref[tile, s * LANES + ht * 8 : s * LANES + ht * 8 + 8, :], 0.0)
                h_ref[ht * samples + s] = h
                sums[s] = sums[s] + h * q
        along = jnp.concatenate([jnp.sum(v, axis=0, keepdims=True) for v in sums], axis=0)
        weight = weight_ref[tile]
        carried = along * weight
        through = running_sum(carried)
        later = through[samples - 1 : samples, :] - through
        grad_thick = row_ref[tile] + along * pass_ref[tile] - later
        grad_density = (grad_thick * slope_ref[tile]).astype(BF16).astype(F32)
        scale = [jnp.broadcast_to(weight[s : s + 1, :], (8, LANES)) for s in range(samples)]
        slant = [jnp.broadcast_to(grad_density[s : s + 1, :], (8, LANES)) for s in range(samples)]
        lanes = pl.ds(pl.multiple_of(tile * LANES, LANES), LANES)
        for pair in range(8):
            at = [slice((2 * pair + u) * 8, (2 * pair + u) * 8 + 8) for u in range(2)]
            q = [q_ref[tile, rows, :] for rows in at]
            wd = [base_ref[tile, samples * LANES + rows.start : samples * LANES + rows.stop, :] for rows in at]
            g1 = [jnp.zeros((8, LANES), F32)] * 2
            hd = [jnp.zeros((8, LANES), F32)] * 2
            for s in range(samples):
                both = []
                for u in range(2):
                    h = h_ref[(2 * pair + u) * samples + s]
                    gp = jnp.where(h > 0.0, scale[s] * q[u] + slant[s] * wd[u], 0.0)
                    g1[u] = g1[u] + gp
                    hd[u] = hd[u] + slant[s] * h
                    both.append(gp)
                gp_ref[s, 16 * pair : 16 * pair + 16, lanes] = jnp.concatenate(both, axis=0).astype(BF16)
            for u in range(2):
                g1_ref[tile, at[u], :] = g1[u]
            hd_ref[16 * pair : 16 * pair + 16, lanes] = jnp.concatenate(hd, axis=0).astype(BF16)
        return carry

    lax.fori_loop(0, 2 * segs, step, 0)
    codes = codes_ref[...]
    tail_ref[...] = jnp.zeros(tail_ref.shape, F32)
    for s in range(samples):
        tail_ref[:, s, :] = dot(hot, gp_ref[s], 1, 1)
    tail_ref[:, samples, :] = dot(hot, hd_ref[...], 1, 1)
    for r in range(regions):
        out, to = block_of(mine_ref, other_ref, half, r)
        held = spread(g1_ref, wanted, r).astype(BF16)
        out[to, 0:WF_AT] = dot(held, codes).astype(BF16)
        out[to, G2_AT:PART_ROWS] = tail_ref[r].astype(BF16)


def finish_kernel(part_ref, samp_ref, wh_ref, hid_ref, feat_ref, dens_ref, code_ref):
    total = part_ref[0].astype(F32)
    for i in range(1, part_ref.shape[0]):
        total = total + part_ref[i].astype(F32)
    g2 = total[G2_AT:DG_AT]
    high, low = split(g2)
    samples = samp_ref[0]
    wh = wh_ref[0]
    hid_ref[0] = total[0:WF_AT].T + dot(samples, high, 0, 0) + dot(samples, low, 0, 0)
    feat_ref[0] = total[WF_AT:G2_AT].T
    dens_ref[...] = total[DG_AT : DG_AT + 1]
    code_ref[0] = dot(high, wh, 1, 1) + dot(low, wh, 1, 1)


def local(ray_code, seg_region, seg_count, pixel_of_ray, sample_code, w_hidden, w_feat, w_density, decoder, target):
    regions = lax.axis_size("region")
    half = regions // 2
    rays, segs = seg_region.shape
    code_width = ray_code.shape[1]
    hid_width = w_hidden.shape[2]
    feat_width = w_feat.shape[2]
    samples = sample_code.shape[1]
    group = rays // regions
    room = max(16, 2 * group)
    pack_rows = RAYS_AT + room
    tiles = 2 * segs
    lanes = segs * rays
    core = lax.axis_index("region") & 1
    same_core = [list(range(c, regions, 2)) for c in range(2)]
    inner = [(i, i ^ 1) for i in range(regions)]
    cross = [(i, i + 1) for i in range(1, regions - 1, 2)] + [(i + 1, i) for i in range(1, regions - 1, 2)]

    packed = pl.pallas_call(
        functools.partial(pack_kernel, half, group, room),
        out_shape=jax.ShapeDtypeStruct((half, pack_rows, LANES), BF16),
        scratch_shapes=[pltpu.VMEM((16, rays), F32)],
        compiler_params=PARAMS,
        name="pack",
    )(
        pixel_of_ray.reshape(1, rays), seg_region.T, seg_count.T,
        ray_code, sample_code, w_hidden, w_feat, w_density,
    )
    block_a = lax.all_to_all(packed, "region", 0, 0, axis_index_groups=same_core, tiled=True)
    block_b = lax.ppermute(block_a, "region", inner)

    target_t = target.T
    first, last = target_t[:, :IW], target_t[:, rays - IW :]
    target_in = lax.ppermute(jnp.where(core == 0, last, first), "region", inner)
    target_cr = lax.ppermute(jnp.where(core == 0, first, last), "region", cross)

    image, a, table, att_hw, weight, passing, slope, att, rel, codes = pl.pallas_call(
        functools.partial(forward_kernel, half, group, room),
        out_shape=(
            jax.ShapeDtypeStruct((feat_width, rays), BF16),
            jax.ShapeDtypeStruct((tiles, hid_width, LANES), F32),
            jax.ShapeDtypeStruct((samples + 1, 2 * regions, hid_width), BF16),
            jax.ShapeDtypeStruct((tiles, hid_width, LANES), F32),
            jax.ShapeDtypeStruct((tiles, samples, LANES), F32),
            jax.ShapeDtypeStruct((tiles, samples, LANES), F32),
            jax.ShapeDtypeStruct((tiles, samples, LANES), F32),
            jax.ShapeDtypeStruct((tiles, 1, LANES), F32),
            jax.ShapeDtypeStruct((segs, rays), jnp.int32),
            jax.ShapeDtypeStruct((rays, code_width), BF16),
        ),
        scratch_shapes=[
            pltpu.VMEM((16, regions * room), F32),
            pltpu.VMEM((samples + 1, regions, hid_width), F32),
            pltpu.VMEM((regions, hid_width, rays), F32),
            pltpu.VMEM((tiles, (samples + 1) * hid_width, LANES), F32),
            pltpu.VMEM((16 * samples, 8, LANES), F32),
            pltpu.VMEM((tiles, 1, LANES), F32),
            pltpu.VMEM((2, 1, LANES), F32),
        ],
        compiler_params=PARAMS,
        name="forward",
    )(block_a, block_b)

    image_in = lax.ppermute(image, "region", inner)
    image_cr = lax.ppermute(image, "region", cross)

    def whole(x):
        return pl.BlockSpec(x.shape, lambda i: (0,) * len(x.shape))

    wf_spec = pl.BlockSpec((half, feat_width, LANES), lambda i: (0, WF_AT // feat_width, 0))
    operands = (
        image, image_in, image_cr, target_t, target_in, target_cr, decoder, decoder.T,
        block_a, block_b, a, table, att_hw, weight, passing, slope, att, rel, codes,
    )
    part = jax.ShapeDtypeStruct((half, PART_ROWS, LANES), BF16)
    mine, other = pl.pallas_call(
        functools.partial(backward_kernel, half),
        out_shape=(part, part),
        grid=(1,),
        out_specs=(whole(part), whole(part)),
        in_specs=[wf_spec if i in (8, 9) else whole(x) for i, x in enumerate(operands)],
        scratch_shapes=[
            pltpu.VMEM((decoder.shape[0], 4 * IW), BF16),
            pltpu.VMEM((regions, hid_width, rays), F32),
            pltpu.VMEM((tiles, hid_width, LANES), F32),
            pltpu.VMEM((tiles, (samples + 1) * hid_width, LANES), F32),
            pltpu.VMEM((16 * samples, 8, LANES), F32),
            pltpu.VMEM((samples, hid_width, lanes), BF16),
            pltpu.VMEM((tiles, hid_width, LANES), F32),
            pltpu.VMEM((hid_width, lanes), BF16),
            pltpu.VMEM((regions, PART_ROWS - G2_AT, hid_width), F32),
            pltpu.VMEM((tiles, 1, LANES), F32),
        ],
        compiler_params=PARAMS,
        name="backward",
    )(*operands)

    theirs = lax.ppermute(other, "region", inner)
    chip = (mine.astype(F32) + theirs.astype(F32)).astype(BF16)
    parts = lax.all_to_all(chip, "region", 0, 0, axis_index_groups=same_core, tiled=True)
    return pl.pallas_call(
        finish_kernel,
        out_shape=(
            jax.ShapeDtypeStruct((1, code_width, hid_width), F32),
            jax.ShapeDtypeStruct((1, hid_width, feat_width), F32),
            jax.ShapeDtypeStruct((1, hid_width), F32),
            jax.ShapeDtypeStruct((1, samples, code_width), F32),
        ),
        compiler_params=PARAMS,
        name="finish",
    )(parts, sample_code, w_hidden)


def solution(mesh):
    in_specs = (
        P(("groups", "region"), None),
        P(("groups", "region"), None),
        P(("groups", "region"), None),
        P(("groups", "region")),
        P("region", None, None),
        P("region", None, None),
        P("region", None, None),
        P("region", None),
        P(),
        P(("groups", "region"), None),
    )
    out_specs = (
        P("region", "groups", None),
        P("region", "groups", None),
        P("region", "groups"),
        P("region", "groups", None),
    )
    return jax.shard_map(local, mesh=mesh, in_specs=in_specs, out_specs=out_specs, check_vma=False)
```

profile of v0, /device:TPU:0, one launch (start us, length us, event | category | flops | bytes accessed | tf_op | source)
XLA Modules:
  0.0 76.4 jit_solution(16132326498776419752)
XLA Ops:
  0.6 0.0 copy-start.4
  0.6 0.0 copy-start.7
  0.7 0.0 copy-start.8
  0.7 0.8 %copy.14.wf_ref = bf16[1,128,64]{2,1,0:T(8,128)(2,1)S(1)} copy(bf16[1,128,64]{1,2,0:T(8,128)(2,1)} %param.16) | data formatting | bytes 32768 | tf_op args[6]
  1.5 0.0 copy-start.6
  1.5 0.0 copy-start.9
  1.5 0.0 copy-start.10
  1.5 0.0 copy-done.4
  1.6 0.0 copy-done.7
  1.6 0.0 copy-done.8
  1.6 0.6 copy-done.6
  2.2 0.0 copy-done.9
  2.2 0.0 copy-done.10
  2.2 0.0 copy-start.5
  2.2 0.8 %copy-done.5 = bf16[256,128]{1,0:T(8,128)(2,1)S(1)} copy-done((bf16[256,128]{1,0:T(8,128)(2,1)S(1)}, bf16[256,128]{1,0:T(8,128)(2,1)}, u32[]{:S(2)}) %copy-start.5) | copy-done | bytes 65560
  3.1 0.4 pack.1
  3.5 0.0 copy-start.12
  3.5 21.7 %all_to_all.10.a_ref.wa_ref = bf16[8,256,128]{2,1,0:T(8,128)(2,1)S(1)} all-to-all(bf16[8,256,128]{2,1,0:T(8,128)(2,1)S(1)} %pack.1), channel_id=1, replica_groups={{0,2,4,6,8,10,12,14},{1,3,5,7,9,11,13,15},{16,18,20,22,24,26,28,30},{17..., dimensions={0} | all-to-all | bytes 1048576 | tf_op jit(solution)/shard_map/all_to_all | solution.py:418
  25.2 0.0 copy-start
  25.2 0.0 collective-permute-start
  25.2 0.0 copy-done.12
  25.2 0.1 copy.15
  25.4 0.7 collective-permute-start.4
  26.1 0.0 copy-start.1
  26.1 2.9 %collective-permute-start.3 = (bf16[384,128]{1,0:T(8,128)(2,1)S(1)}, bf16[384,128]{1,0:T(8,128)(2,1)S(1)}, u32[]{:S(2)}, u32[]{:S(2)}) collective-permute-start(bf16[384,128]{1,0:T(8,128)(2,1)S(1)} %get-tuple-element.33), channel_id=1, source_target_pairs={{0,1},{1,0},{2,3},{3,2},{4,5},{5,4},{6,7},{7,6},{8,9},{9,8},{10,11... | collective-permute-start | bytes 294920 | tf_op jit(solution)/shard_map/ppermute | solution.py:423
  29.0 0.0 collective-permute-done.b_ref.wb_ref
  29.0 0.0 copy-start.11
  29.0 0.8 %copy-done.11 = bf16[8,256,128]{2,1,0:T(8,128)(2,1)} copy-done((bf16[8,256,128]{2,1,0:T(8,128)(2,1)}, bf16[8,256,128]{2,1,0:T(8,128)(2,1)S(1)}, u32[]{:S(2)}) %copy-start.11) | copy-done | bytes 524312
  29.8 7.6 %forward.1 = (bf16[64,256]{1,0:T(8,128)(2,1)S(1)}, f32[8,128,128]{2,1,0:T(8,128)S(1)}, bf16[17,32,128]{2,1,0:T(8,128)(2,1)S(1)}, f32[8,128,128]{2,1,0:T(8,128)S(...) custom-call(bf16[8,256,128]{2,1,0:T(8,128)(2,1)S(1)} %all_to_all.10., ...), custom_call_target="tpu_custom_call" | custom-call | tf_op jit(solution)/shard_map/forward/pallas_call | solution.py:426
  37.4 0.0 copy-done
  37.4 0.0 copy-start.2
  37.4 0.8 %copy-done.2 = f32[8,128,128]{2,1,0:T(8,128)} copy-done((f32[8,128,128]{2,1,0:T(8,128)}, f32[8,128,128]{2,1,0:T(8,128)S(1)}, u32[]{:S(2)}) %copy-start.2) | copy-done | bytes 524312
  38.2 0.0 copy-start.3
  38.2 0.8 %copy-done.3 = f32[8,128,128]{2,1,0:T(8,128)} copy-done((f32[8,128,128]{2,1,0:T(8,128)}, f32[8,128,128]{2,1,0:T(8,128)S(1)}, u32[]{:S(2)}) %copy-start.3) | copy-done | bytes 524312
  39.0 0.7 collective-permute-start.2
  39.6 2.5 %collective-permute-start.1 = (bf16[64,256]{1,0:T(8,128)(2,1)S(1)}, bf16[64,256]{1,0:T(8,128)(2,1)S(1)}, u32[]{:S(2)}, u32[]{:S(2)}) collective-permute-start(bf16[64,256]{1,0:T(8,128)(2,1)S(1)} %get-tuple-element.16.own_ref), channel_id=1, source_target_pairs={{0,1},{1,0},{2,3},{3,2},{4,5},{5,4},{6,7},{7,6},{8,9},{9,8},{10,11... | collective-permute-start | bytes 98312 | tf_op jit(solution)/shard_map/ppermute | solution.py:453
  42.2 0.0 copy-done.1
  42.2 1.0 %copy.16 = bf16[576,384]{0,1:T(8,128)(2,1)} copy(bf16[576,384]{1,0:T(8,128)(2,1)S(1)} %copy-done.1) | data formatting | bytes 884736 | tf_op args[8]
  43.2 0.0 collective-permute-done.4.tcr_ref
  43.2 0.0 collective-permute-done.3.tin_ref
  43.2 0.0 collective-permute-done.2.cross_ref
  43.2 0.0 collective-permute-done.1.inner_ref
  43.2 11.5 %backward.1 = (bf16[8,224,128]{2,1,0:T(8,128)(2,1)S(1)}, bf16[8,224,128]{2,1,0:T(8,128)(2,1)}) custom-call(bf16[64,256]{1,0:T(8,128)(2,1)S(1)} %get-tuple-element.16.own_ref, bf16[64,256]{1,0:T(8,128)(2,1)S(1)} %collective-permute-done.1.inner_ref, bf16[64,256]{1,0:T(8,128)(2,1)S(1)} %collective-permute-done.2.cross_ref, bf16[384,256]{1,0:T(8,128)(2,1)S(1)} %bitcast.6, ...), custom_call_target="tpu_custom_call" | custom-call | tf_op jit(solution)/shard_map/backward/pallas_call | solution.py:465
  54.7 1.0 %collective-permute-start.5 = (bf16[8,224,128]{2,1,0:T(8,128)(2,1)}, bf16[8,224,128]{2,1,0:T(8,128)(2,1)S(1)}, u32[]{:S(2)}, u32[]{:S(2)}) collective-permute-start(bf16[8,224,128]{2,1,0:T(8,128)(2,1)} %get-tuple-element.27), channel_id=1, source_target_pairs={{0,1},{1,0},{2,3},{3,2},{4,5},{5,4},{6,7},{7,6},{8,9},{9,8},{10,11... | collective-permute-start | bytes 1376264 | tf_op jit(solution)/shard_map/ppermute | solution.py:487
  55.7 1.7 %collective-permute-done.5 = bf16[8,224,128]{2,1,0:T(8,128)(2,1)S(1)} collective-permute-done((bf16[8,224,128]{2,1,0:T(8,128)(2,1)}, bf16[8,224,128]{2,1,0:T(8,128)(2,1)S(1)}, u32[]{:S(2)}, u32[]{:S(2)}) %collective-permute-start.5) | collective-permute-done | bytes 458784 | tf_op jit(solution)/shard_map/ppermute | solution.py:487
  57.4 0.1 add_convert_fusion
  57.5 17.4 %all_to_all.11.part_ref = bf16[8,224,128]{2,1,0:T(8,128)(2,1)S(1)} all-to-all(bf16[8,224,128]{2,1,0:T(8,128)(2,1)S(1)} %add_convert_fusion), channel_id=1, replica_groups={{0,2,4,6,8,10,12,14},{1,3,5,7,9,11,13,15},{16,18,20,22,24,26,28,30},{17..., dimensions={0} | all-to-all | bytes 917504 | tf_op jit(solution)/shard_map/all_to_all | solution.py:489
  74.9 0.8 %finish.1 = (f32[1,128,128]{2,1,0:T(8,128)}, f32[1,128,64]{2,1,0:T(8,128)S(1)}, f32[1,128]{1,0:T(1,128)}, f32[1,16,128]{2,1,0:T(8,128)}) custom-call(bf16[8,224,128]{2,1,0:T(8,128)(2,1)S(1)} %all_to_all.11.part_ref, bf16[1,16,128]{2,1,0:T(8,128)(2,1)S(1)} %copy-done.6, bf16[1,128,128]{2,1,0:T(8,128)(2,1)S(1)} %copy-done.4), custom_call_target="tpu_custom_call" | custom-call | tf_op jit(solution)/shard_map/finish/pallas_call | solution.py:490
  75.7 0.7 copy.17
  (1 shorter events, 0.0 us)
Async XLA Ops:
  0.6 0.9 %copy-start.4 = (bf16[1,128,128]{2,1,0:T(8,128)(2,1)S(1)}, bf16[1,128,128]{2,1,0:T(8,128)(2,1)}, u32[]{:S(2)}) copy-start(bf16[1,128,128]{2,1,0:T(8,128)(2,1)} %wh_ref.3) | copy-start | bytes 98308
  0.6 0.9 %copy-start.7 = (s32[256,4]{0,1:T(4,128)S(1)}, s32[256,4]{0,1:T(4,128)}, u32[]{:S(2)}) copy-start(s32[256,4]{0,1:T(4,128)} %param.11) | copy-start | bytes 12292
  0.7 0.9 %copy-start.8 = (s32[256,4]{0,1:T(4,128)S(1)}, s32[256,4]{0,1:T(4,128)}, u32[]{:S(2)}) copy-start(s32[256,4]{0,1:T(4,128)} %param.12) | copy-start | bytes 12292
  1.5 0.7 copy-start.6
  1.5 0.7 copy-start.9
  1.5 0.7 copy-start.10
  2.2 0.8 %copy-start.5 = (bf16[256,128]{1,0:T(8,128)(2,1)S(1)}, bf16[256,128]{1,0:T(8,128)(2,1)}, u32[]{:S(2)}) copy-start(bf16[256,128]{1,0:T(8,128)(2,1)} %code_ref.1) | copy-start | bytes 196612
  3.5 21.7 %copy-start.12 = (bf16[256,384]{1,0:T(8,128)(2,1)S(1)}, bf16[256,384]{1,0:T(8,128)(2,1)}, u32[]{:S(2)}) copy-start(bf16[256,384]{1,0:T(8,128)(2,1)} %param.19) | copy-start | bytes 589828
  25.2 12.2 %copy-start = (bf16[8,256,128]{2,1,0:T(8,128)(2,1)}, bf16[8,256,128]{2,1,0:T(8,128)(2,1)S(1)}, u32[]{:S(2)}) copy-start(bf16[8,256,128]{2,1,0:T(8,128)(2,1)S(1)} %all_to_all.10.a_ref.wa_ref) | copy-start | bytes 1572868
  25.2 3.8 %collective-permute-start = (bf16[8,256,128]{2,1,0:T(8,128)(2,1)S(1)}, bf16[8,256,128]{2,1,0:T(8,128)(2,1)S(1)}, u32[]{:S(2)}, u32[]{:S(2)}) collective-permute-start(bf16[8,256,128]{2,1,0:T(8,128)(2,1)S(1)} %all_to_all.10.a_ref.wa_ref), channel_id=1, source_target_pairs={{0,1},{1,0},{2,3},{3,2},{4,5},{5,4},{6,7},{7,6},{8,9},{9,8},{10,11... | collective-permute-start | bytes 1572872 | tf_op jit(solution)/shard_map/ppermute | solution.py:419
  25.4 17.8 %collective-permute-start.4 = (bf16[384,128]{1,0:T(8,128)(2,1)S(1)}, bf16[384,128]{1,0:T(8,128)(2,1)S(1)}, u32[]{:S(2)}, u32[]{:S(2)}) collective-permute-start(bf16[384,128]{1,0:T(8,128)(2,1)S(1)} %get-tuple-element.32), channel_id=1, source_target_pairs={{1,2},{3,4},{5,6},{7,8},{9,10},{11,12},{13,14},{2,1},{4,3},{6,5},{... | collective-permute-start | bytes 294920 | tf_op jit(solution)/shard_map/ppermute | solution.py:424
  26.1 16.1 %copy-start.1 = (bf16[576,384]{1,0:T(8,128)(2,1)S(1)}, bf16[576,384]{1,0:T(8,128)(2,1)}, u32[]{:S(2)}) copy-start(bf16[576,384]{1,0:T(8,128)(2,1)} %dec_ref.1) | copy-start | bytes 1327108
  26.1 17.1 %collective-permute-start.3 = (bf16[384,128]{1,0:T(8,128)(2,1)S(1)}, bf16[384,128]{1,0:T(8,128)(2,1)S(1)}, u32[]{:S(2)}, u32[]{:S(2)}) collective-permute-start(bf16[384,128]{1,0:T(8,128)(2,1)S(1)} %get-tuple-element.33), channel_id=1, source_target_pairs={{0,1},{1,0},{2,3},{3,2},{4,5},{5,4},{6,7},{7,6},{8,9},{9,8},{10,11... | collective-permute-start | bytes 294920 | tf_op jit(solution)/shard_map/ppermute | solution.py:423
  29.0 0.8 %copy-start.11 = (bf16[8,256,128]{2,1,0:T(8,128)(2,1)}, bf16[8,256,128]{2,1,0:T(8,128)(2,1)S(1)}, u32[]{:S(2)}) copy-start(bf16[8,256,128]{2,1,0:T(8,128)(2,1)S(1)} %collective-permute-done.b_ref.wb_ref) | copy-start | bytes 1572868
  37.4 0.8 %copy-start.2 = (f32[8,128,128]{2,1,0:T(8,128)}, f32[8,128,128]{2,1,0:T(8,128)S(1)}, u32[]{:S(2)}) copy-start(f32[8,128,128]{2,1,0:T(8,128)S(1)} %get-tuple-element.17.a_ref) | copy-start | bytes 1572868
  38.2 0.8 %copy-start.3 = (f32[8,128,128]{2,1,0:T(8,128)}, f32[8,128,128]{2,1,0:T(8,128)S(1)}, u32[]{:S(2)}) copy-start(f32[8,128,128]{2,1,0:T(8,128)S(1)} %get-tuple-element.19.att_hw_ref) | copy-start | bytes 1572868
  39.0 4.2 %collective-permute-start.2 = (bf16[64,256]{1,0:T(8,128)(2,1)S(1)}, bf16[64,256]{1,0:T(8,128)(2,1)S(1)}, u32[]{:S(2)}, u32[]{:S(2)}) collective-permute-start(bf16[64,256]{1,0:T(8,128)(2,1)S(1)} %get-tuple-element.16.own_ref), channel_id=1, source_target_pairs={{1,2},{3,4},{5,6},{7,8},{9,10},{11,12},{13,14},{2,1},{4,3},{6,5},{... | collective-permute-start | bytes 98312 | tf_op jit(solution)/shard_map/ppermute | solution.py:454
  39.6 3.6 %collective-permute-start.1 = (bf16[64,256]{1,0:T(8,128)(2,1)S(1)}, bf16[64,256]{1,0:T(8,128)(2,1)S(1)}, u32[]{:S(2)}, u32[]{:S(2)}) collective-permute-start(bf16[64,256]{1,0:T(8,128)(2,1)S(1)} %get-tuple-element.16.own_ref), channel_id=1, source_target_pairs={{0,1},{1,0},{2,3},{3,2},{4,5},{5,4},{6,7},{7,6},{8,9},{9,8},{10,11... | collective-permute-start | bytes 98312 | tf_op jit(solution)/shard_map/ppermute | solution.py:453
  54.7 2.7 %collective-permute-start.5 = (bf16[8,224,128]{2,1,0:T(8,128)(2,1)}, bf16[8,224,128]{2,1,0:T(8,128)(2,1)S(1)}, u32[]{:S(2)}, u32[]{:S(2)}) collective-permute-start(bf16[8,224,128]{2,1,0:T(8,128)(2,1)} %get-tuple-element.27), channel_id=1, source_target_pairs={{0,1},{1,0},{2,3},{3,2},{4,5},{5,4},{6,7},{7,6},{8,9},{9,8},{10,11... | collective-permute-start | bytes 1376264 | tf_op jit(solution)/shard_map/ppermute | solution.py:487
where the time goes:
time: 76.9 us; the launch traced here: 76.4 us
  blocking collectives  39.1 us (51%)
  Pallas kernels  20.3 us (26%)
  starting transfers between devices  7.75 us (10%)
  local copies, waits for them, and re-layouts  6.62 us (9%)
  waiting for transfers between devices  1.67 us (2%)
  between operations  0.81 us (1%)
    all_to_all x1, blocking collectives, local(): lax.all_to_all(packed, 'region', 0, 0, axis_index_groups=same_core, tiled...  21.7 us
    all_to_all x1, blocking collectives, local(): lax.all_to_all(chip, 'region', 0, 0, axis_index_groups=same_core, tiled=T...  17.4 us
    pallas_call x1, Pallas kernels, local(): pl.pallas_call(functools.partial(backward_kernel, half), out_shape=(part,...  11.5 us
    pallas_call x1, Pallas kernels, local(): pl.pallas_call(functools.partial(forward_kernel, half, group, room), out_...  7.57 us
    unnamed x29, local copies, waits for them, and re-layouts  5.92 us
    ppermute x1, starting transfers between devices, local(): target_in = lax.ppermute(jnp.where(core == 0, last, first), 'region', inner)  2.89 us
    ppermute x1, starting transfers between devices, local(): image_in = lax.ppermute(image, 'region', inner)  2.54 us
    ppermute x1, waiting for transfers between devices, local(): theirs = lax.ppermute(other, 'region', inner)  1.65 us
  transfers between devices with their start and end apart: 6, of which 1 were waited for; matrix products, arithmetic and copies ran while one was open for 2% of the time, Pallas kernels for 10%

commit v1 on v0

v1 whole, which is shorter than its diff:
```python
import functools

import jax
import jax.numpy as jnp
from jax import lax
from jax.experimental import pallas as pl
from jax.experimental.pallas import tpu as pltpu
from jax.sharding import PartitionSpec as P

IW = 128
STEP = 0.08
F32 = jnp.float32
BF16 = jnp.bfloat16
LANES = 128

WF_AT = 128
SAMPLE_AT = 192
META_AT = 208
RAYS_AT = 224
G2_AT = 192
DG_AT = 208
PART_ROWS = 216

PARAMS = pltpu.CompilerParams(vmem_limit_bytes=40 << 20)


def iota(shape, dim):
    return lax.broadcasted_iota(jnp.int32, shape, dim)


def dot(lhs, rhs, left=1, right=0):
    return lax.dot_general(lhs, rhs, (((left,), (right,)), ((), ())), preferred_element_type=F32)


def split(values):
    high = values.astype(BF16)
    return high, (values - high.astype(F32)).astype(BF16)


def running_sum(values):
    rows = values.shape[0]
    row = iota(values.shape, 0)
    step = 1
    while step < rows:
        values = values + jnp.where(row >= step, pltpu.roll(values, step, 0), 0.0)
        step *= 2
    return values


def pack_kernel(half, group, room, *refs):
    hbm, blocks, halos, held, sems = refs[:9], refs[9 : 9 + half], refs[9 + half : 11 + half], refs[11 + half : 19 + half], refs[19 + half]
    meta_ref, codes_ref = refs[20 + half :]
    me = lax.axis_index("region")
    core = me & 1
    mine = lax.shift_right_logical(me, 1)
    copies = [pltpu.make_async_copy(hbm[i], held[i], sems.at[i]) for i in range(8)]
    target, width = hbm[8], halos[0].shape[0]
    inward = pl.multiple_of((1 - core) * width, width)
    outward = pl.multiple_of(core * width, width)
    copies.append(pltpu.make_async_copy(target.at[pl.ds(inward, width)], halos[0], sems.at[8]))
    copies.append(pltpu.make_async_copy(target.at[pl.ds(outward, width)], halos[1], sems.at[9]))
    for copy in copies:
        copy.start()
    for copy in copies[:8]:
        copy.wait()
    pix_ref, reg_ref, cnt_ref, code_ref, samp_ref, wh_ref, wf_ref, wd_ref = held
    rays = code_ref.shape[0]
    regions = 2 * half
    shift = rays.bit_length() - 1
    pix = pix_ref[...]
    tile = lax.shift_right_logical(pix, shift)
    spot = pix & (rays - 1)
    same = jnp.where(iota((regions, rays), 0) == tile, 1.0, 0.0)
    earlier = jnp.where(iota((rays, rays), 0) < iota((rays, rays), 1), 1.0, 0.0).astype(BF16)
    counts = dot(same.astype(BF16), earlier)
    rank = jnp.sum(counts * same, axis=0, keepdims=True).astype(jnp.int32)
    row_place = lax.shift_right_logical(tile, 1) * room + (tile & 1) * group + rank
    lane_place = tile * group + rank
    meta_ref[...] = jnp.zeros(meta_ref.shape, F32)
    meta_ref[1:2, :] = spot.astype(F32)
    meta_ref[2:6, :] = reg_ref[...].astype(F32)
    meta_ref[6:10, :] = cnt_ref[...].astype(F32)
    row_hot = jnp.where(iota((half * room, rays), 0) == row_place, 1.0, 0.0).astype(BF16)
    codes_ref[...] = dot(row_hot, code_ref[...]).astype(BF16)
    lane_hot = jnp.where(iota((rays, rays), 0) == lane_place, 1.0, 0.0).astype(BF16)
    meta = dot(meta_ref[...].astype(BF16), lane_hot, 1, 1)
    wh_t = wh_ref[0].astype(F32).T.astype(BF16)
    density = wd_ref[...].astype(F32)
    first = iota((16, LANES), 0) == 0
    for k, out_ref in enumerate(blocks):
        chip = jnp.bitwise_xor(mine, k)
        out_ref[0:WF_AT] = wh_t
        out_ref[WF_AT:SAMPLE_AT] = wf_ref[0]
        out_ref[SAMPLE_AT:META_AT] = samp_ref[0]
        here = pltpu.roll(meta, (rays - chip * 2 * group) & (rays - 1), 1)[:, :LANES]
        out_ref[META_AT:RAYS_AT] = jnp.where(first, density, here).astype(BF16)
        out_ref[RAYS_AT : RAYS_AT + room] = codes_ref[pl.ds(pl.multiple_of(chip * room, 16), room), :]
    for copy in copies[8:]:
        copy.wait()


def bits_of(row, regions):
    count = regions.bit_length() - 1
    row = jnp.broadcast_to(row, (8, LANES))
    return [(lax.shift_right_logical(row, b) & 1) == 1 for b in range(count)]


def choose(values, bits):
    for bit in bits:
        values = [jnp.where(bit, values[i + 1], values[i]) for i in range(0, len(values), 2)]
    return values[0]


def seg_hot(wanted, regions):
    return jnp.concatenate(
        [jnp.where(iota((regions, row.shape[1]), 0) == row, 1.0, 0.0) for row in wanted], axis=1
    )


def forward_kernel(half, group, room, *refs):
    regions = 2 * half
    blocks = refs[:regions]
    (
        image_ref, h_ref, wd_ref, att_hw_ref, wide_hw_ref, weight_ref, pass_ref, slope_ref, att_ref, rel_ref, codes_ref, wf_out,
        meta_ref, plain_ref, table_ref, proj_ref, a_ref, picked_ref, row_ref, ahead_ref,
    ) = refs[regions:]
    rays = codes_ref.shape[1]
    segs = rel_ref.shape[0]
    samples = weight_ref.shape[1]
    feats = image_ref.shape[0]
    me = lax.axis_index("region")
    core = me & 1
    chip = lax.shift_right_logical(me, 1)
    per_tile = LANES // room
    lane = iota((16, LANES), 1)
    chunk = lax.div(lane, room)
    inside = lane - chunk * room
    mine = (inside < 2 * group) & (lax.div(inside, group) == core)
    for tile in range(regions // per_tile):
        total = jnp.zeros((16, LANES), F32)
        for spot in range(per_tile):
            block = blocks[tile * per_tile + spot][META_AT:RAYS_AT].astype(F32)
            total = jnp.where(chunk == spot, pltpu.roll(block, spot * room, 1), total)
        meta_ref[:, tile * LANES : (tile + 1) * LANES] = jnp.where(mine, total, -1.0)
    meta_src = meta_ref[...]
    places = regions * room
    to_pixel = jnp.where(
        iota((rays, places), 0).astype(F32) == meta_src[1:2, :], 1.0, 0.0
    ).astype(BF16)
    sources = jnp.concatenate([block[RAYS_AT : RAYS_AT + room] for block in blocks], axis=0)
    codes_t = dot(to_pixel, sources).T.astype(BF16)
    codes_ref[...] = codes_t
    meta = dot(meta_src.astype(BF16), to_pixel, 1, 1)
    region = meta[2 : 2 + segs].astype(jnp.int32)
    rel = jnp.bitwise_xor(region & 1, core) * half + jnp.bitwise_xor(lax.shift_right_logical(region, 1), chip)
    rel_ref[...] = rel
    for k in range(segs):
        for part in range(2):
            row_ref[2 * k + part] = meta[6 + k : 7 + k, part * LANES : (part + 1) * LANES]
    wanted = [rel_ref[k : k + 1, :] for k in range(segs)]
    for r, block in enumerate(blocks):
        w_t = block[0:WF_AT]
        proj_ref[r] = dot(w_t, codes_t)
        plain_ref[0:samples, r, :] = dot(block[SAMPLE_AT:META_AT], w_t, 1, 1)
        plain_ref[samples, r : r + 1, :] = block[META_AT:RAYS_AT].astype(F32)[0:1, :]
        wf_out[r * feats : (r + 1) * feats] = block[WF_AT:SAMPLE_AT]
    for s in range(samples + 1):
        high, low = split(plain_ref[s])
        table_ref[s] = jnp.concatenate([high.astype(F32), low.astype(F32)], axis=0).T.astype(BF16)
    for part in range(2):
        lanes = slice(part * LANES, (part + 1) * LANES)

        def pick_rows(index, carry):
            rows = pl.ds(pl.multiple_of(index * 8, 8), 8)
            bits = [bits_of(row[:, lanes], regions) for row in wanted]
            values = [proj_ref[r, rows, lanes] for r in range(regions)]
            for k in range(segs):
                a_ref[2 * k + part, rows, :] = choose(values, bits[k])
            return carry

        lax.fori_loop(0, 16, pick_rows, 0)
    hot = seg_hot(wanted, regions).astype(BF16)
    hot2 = jnp.concatenate([hot, hot], axis=0)
    for tile in range(2 * segs):
        picked_ref[tile] = hot2[:, tile * LANES : (tile + 1) * LANES]
    ahead_ref[...] = jnp.zeros(ahead_ref.shape, F32)
    order = iota((samples, LANES), 0).astype(F32)

    def step(tile, carry):
        here = picked_ref[tile]
        wd = dot(table_ref[samples], here)
        wd_ref[tile] = wd
        sums = []
        for s in range(samples):
            h = jnp.maximum(a_ref[tile] + dot(table_ref[s], here), 0.0)
            h_ref[tile, s] = h
            sums.append(jnp.sum(h * wd_ref[tile], axis=0, keepdims=True))
        density = jnp.concatenate(sums, axis=0)
        part = tile & 1
        live = order < row_ref[tile]
        soft = jnp.maximum(density, 0.0) + jnp.log1p(jnp.exp(-jnp.abs(density)))
        thick = jnp.where(live, STEP * soft, 0.0)
        through = running_sum(thick)
        passing = jnp.exp(-(through - thick))
        keeping = jnp.exp(-thick)
        weight = passing * (1.0 - keeping)
        weight_ref[tile] = weight
        pass_ref[tile] = passing * keeping
        slope_ref[tile] = jnp.where(live, STEP / (1.0 + jnp.exp(-density)), 0.0)
        before = ahead_ref[part]
        att = jnp.exp(-before)
        ahead_ref[part] = before + through[samples - 1 : samples, :]
        att_ref[tile] = att
        scale = [jnp.broadcast_to(weight[s : s + 1, :] * att, (8, LANES)) for s in range(samples)]
        lanes = pl.ds(pl.multiple_of(tile * LANES, LANES), LANES)
        for pair in range(8):
            both = []
            for ht in (2 * pair, 2 * pair + 1):
                rows = slice(ht * 8, ht * 8 + 8)
                total = scale[0] * h_ref[tile, 0, rows, :]
                for s in range(1, samples):
                    total = total + scale[s] * h_ref[tile, s, rows, :]
                att_hw_ref[tile, rows, :] = total
                both.append(total)
            wide_hw_ref[pair * 16 : pair * 16 + 16, lanes] = jnp.concatenate(both, axis=0).astype(BF16)
        return carry

    lax.fori_loop(0, 2 * segs, step, 0)
    wf_twice = jnp.concatenate([wf_out[...], wf_out[...]], axis=1)
    for part in range(2):
        feat = [jnp.zeros((8, LANES), F32)] * (feats // 8)
        for k in range(segs):
            tile = 2 * k + part
            high, low = split(att_hw_ref[tile])
            proj_ref[0 : regions * feats // LANES, :, 0:LANES] = dot(wf_twice, jnp.concatenate([high, low], axis=0)).reshape(
                regions * feats // LANES, LANES, LANES
            )
            bits = bits_of(wanted[k][:, part * LANES : (part + 1) * LANES], regions)
            for ft in range(feats // 8):
                values = []
                for r in range(regions):
                    at = r * feats + ft * 8
                    values.append(proj_ref[at // LANES, at % LANES : at % LANES + 8, 0:LANES])
                feat[ft] = feat[ft] + choose(values, bits)
        image_ref[:, part * LANES : (part + 1) * LANES] = jnp.concatenate(feat, axis=0).astype(BF16)


def shifted(values, by):
    lane = iota(values.shape, 1)
    if by == 0:
        return values
    if by > 0:
        return jnp.where(lane == 0, 0.0, pltpu.roll(values, 1, 1))
    return jnp.where(lane == LANES - 1, 0.0, pltpu.roll(values, LANES - 1, 1))


def backward_kernel(
    half, own_ref, inner_ref, cross_ref, tgt_ref, tin_ref, tcr_ref, dec_ref, dect_ref,
    h_in, wd_ref, att_hw_ref, wide_hw_ref, weight_ref, pass_ref, slope_ref, att_ref, rel_ref, codes_ref, wf_ref,
    mine_ref, other_ref,
    patch_ref, masked_ref, q_ref, gp_ref, g1_ref, hd_ref, tail_ref, row_ref,
):
    regions = 2 * half
    feats, rays = own_ref.shape
    segs = rel_ref.shape[0]
    samples = weight_ref.shape[1]
    me = lax.axis_index("region")
    core = me & 1
    own = own_ref[...].astype(F32)
    inner = inner_ref[...].astype(F32)
    cross = cross_ref[...].astype(F32)
    top = jnp.where(core == 0, cross, inner)
    bottom = jnp.where(core == 0, inner, cross)
    rows = [v[:, i * IW : (i + 1) * IW] for v in (top, own, bottom) for i in range(2)]
    for at, row in enumerate(rows):
        for dx in range(3):
            piece = shifted(row, 1 - dx).astype(BF16)
            for dy in range(3):
                if 0 <= at - dy < 4:
                    patch_ref[(3 * dy + dx) * feats : (3 * dy + dx + 1) * feats, (at - dy) * IW : (at - dy + 1) * IW] = piece
    tin = tin_ref[...].astype(F32)
    tcr = tcr_ref[...].astype(F32)
    t_top = jnp.where(core == 0, tcr, tin)
    t_bottom = jnp.where(core == 0, tin, tcr)
    decoded = dot(dect_ref[...], patch_ref[...])
    tgt = tgt_ref[...].astype(F32)
    g_top = jnp.where(me > 0, decoded[:, 0:IW] - t_top, 0.0)
    g_own = decoded[:, IW : 3 * IW] - tgt
    g_bottom = jnp.where(me < regions - 1, decoded[:, 3 * IW :] - t_bottom, 0.0)
    grad_dec = jnp.concatenate([g_top, g_own, g_bottom], axis=1).astype(BF16)
    grad_patch = dot(dec_ref[...], grad_dec)
    image_rows = []
    for i in range(2):
        total = jnp.zeros((feats, IW), F32)
        for dx in range(3):
            term = jnp.zeros((feats, IW), F32)
            for dy in range(3):
                at = (3 * dy + dx) * feats
                term = term + grad_patch[at : at + feats, (i - dy + 2) * IW : (i - dy + 3) * IW]
            total = total + shifted(term, dx - 1)
        image_rows.append(total)
    grad_ray = jnp.concatenate(image_rows, axis=1)
    wanted = [rel_ref[k : k + 1, :] for k in range(segs)]
    for r in range(regions):
        for k in range(segs):
            masked = jnp.where(wanted[k] == r, grad_ray, 0.0).astype(BF16)
            masked_ref[r * feats : (r + 1) * feats, k * rays : (k + 1) * rays] = masked
    raw = dot(wf_ref[...], masked_ref[...], 0, 0)
    for tile in range(2 * segs):
        q_ref[tile] = raw[:, tile * LANES : (tile + 1) * LANES]
    feat_grad = dot(masked_ref[...], wide_hw_ref[...], 1, 1).astype(BF16)
    for r in range(regions):
        out, to = (mine_ref, r) if r < half else (other_ref, r - half)
        out[to, WF_AT:G2_AT] = feat_grad[r * feats : (r + 1) * feats]
    hot = seg_hot(wanted, regions).astype(BF16)
    for part in range(2):
        later = jnp.zeros((1, LANES), F32)
        for k in reversed(range(segs)):
            row_ref[2 * k + part] = -later
            pulled = jnp.sum(att_hw_ref[2 * k + part] * q_ref[2 * k + part], axis=0, keepdims=True)
            later = later + pulled

    def step(tile, carry):
        att = jnp.broadcast_to(att_ref[tile], (8, LANES))
        sums = [jnp.zeros((8, LANES), F32)] * samples
        for ht in range(16):
            rows = slice(ht * 8, ht * 8 + 8)
            q = q_ref[tile, rows, :] * att
            q_ref[tile, rows, :] = q
            for s in range(samples):
                sums[s] = sums[s] + h_in[tile, s, rows, :] * q
        along = jnp.concatenate([jnp.sum(v, axis=0, keepdims=True) for v in sums], axis=0)
        weight = weight_ref[tile]
        through = running_sum(along * weight)
        later = through[samples - 1 : samples, :] - through
        grad_thick = row_ref[tile] + along * pass_ref[tile] - later
        grad_density = (grad_thick * slope_ref[tile]).astype(BF16).astype(F32)
        scale = [jnp.broadcast_to(weight[s : s + 1, :], (8, LANES)) for s in range(samples)]
        slant = [jnp.broadcast_to(grad_density[s : s + 1, :], (8, LANES)) for s in range(samples)]
        lanes = pl.ds(pl.multiple_of(tile * LANES, LANES), LANES)
        for pair in range(8):
            at = [slice((2 * pair + u) * 8, (2 * pair + u) * 8 + 8) for u in range(2)]
            q = [q_ref[tile, rows, :] for rows in at]
            wd = [wd_ref[tile, rows, :] for rows in at]
            g1 = [jnp.zeros((8, LANES), F32)] * 2
            hd = [jnp.zeros((8, LANES), F32)] * 2
            for s in range(samples):
                both = []
                for u in range(2):
                    h = h_in[tile, s, at[u], :]
                    gp = jnp.where(h > 0.0, scale[s] * q[u] + slant[s] * wd[u], 0.0)
                    g1[u] = g1[u] + gp
                    hd[u] = hd[u] + slant[s] * h
                    both.append(gp)
                gp_ref[s, 16 * pair : 16 * pair + 16, lanes] = jnp.concatenate(both, axis=0).astype(BF16)
            g1_ref[16 * pair : 16 * pair + 16, lanes] = jnp.concatenate(g1, axis=0).astype(BF16)
            hd_ref[16 * pair : 16 * pair + 16, lanes] = jnp.concatenate(hd, axis=0).astype(BF16)
        return carry

    lax.fori_loop(0, 2 * segs, step, 0)
    codes = codes_ref[...].astype(F32)
    tail_ref[...] = jnp.zeros(tail_ref.shape, F32)
    for s in range(samples):
        tail_ref[:, s, :] = dot(hot, gp_ref[s], 1, 1)
    tail_ref[:, samples, :] = dot(hot, hd_ref[...], 1, 1)
    g1 = g1_ref[...]
    for r in range(regions):
        out, to = (mine_ref, r) if r < half else (other_ref, r - half)
        held = jnp.concatenate([jnp.where(row == r, codes, 0.0).astype(BF16) for row in wanted], axis=1)
        out[to, 0:WF_AT] = dot(held, g1, 1, 1).astype(BF16)
        out[to, G2_AT:PART_ROWS] = tail_ref[r].astype(BF16)


def merge_kernel(mine_ref, theirs_ref, *outs):
    for k, out in enumerate(outs):
        out[...] = (mine_ref[k].astype(F32) + theirs_ref[k].astype(F32)).astype(BF16)


def finish_kernel(*refs):
    parts, (samp_ref, wh_ref, hid_ref, feat_ref, dens_ref, code_ref) = refs[:-6], refs[-6:]
    total = parts[0][...].astype(F32)
    for part in parts[1:]:
        total = total + part[...].astype(F32)
    high, low = split(total[G2_AT:DG_AT])
    samples = samp_ref[0]
    wh = wh_ref[0]
    hid_ref[0] = total[0:WF_AT] + dot(samples, high, 0, 0) + dot(samples, low, 0, 0)
    feat_ref[0] = total[WF_AT:G2_AT]
    dens_ref[...] = total[DG_AT : DG_AT + 1]
    code_ref[0] = dot(high, wh, 1, 1) + dot(low, wh, 1, 1)


def local(ray_code, seg_region, seg_count, pixel_of_ray, sample_code, w_hidden, w_feat, w_density, decoder, target):
    regions = lax.axis_size("region")
    half = regions // 2
    rays, segs = seg_region.shape
    code_width = ray_code.shape[1]
    hid_width = w_hidden.shape[2]
    feat_width = w_feat.shape[2]
    dino_width = target.shape[1]
    samples = sample_code.shape[1]
    group = rays // regions
    room = max(16, 2 * group)
    tiles = 2 * segs
    lanes = segs * rays
    inner = [(i, i ^ 1) for i in range(regions)]
    cross = [(i, i + 1) for i in range(1, regions - 1, 2)] + [(i + 1, i) for i in range(1, regions - 1, 2)]

    def shape(*dims, kind=F32):
        return jax.ShapeDtypeStruct(dims, kind)

    def to_chips(blocks):
        return [blocks[0]] + [
            lax.ppermute(blocks[k], "region", [(i, i ^ (2 * k)) for i in range(regions)]) for k in range(1, half)
        ]

    pack_args = (
        pixel_of_ray.reshape(1, rays), seg_region.T, seg_count.T,
        ray_code, sample_code, w_hidden, w_feat.swapaxes(1, 2), w_density, target,
    )
    outs = pl.pallas_call(
        functools.partial(pack_kernel, half, group, room),
        out_shape=[shape(RAYS_AT + room, LANES, kind=BF16)] * half + [shape(IW, dino_width, kind=BF16)] * 2,
        in_specs=[pl.BlockSpec(memory_space=pltpu.HBM)] * 9,
        scratch_shapes=[pltpu.VMEM(x.shape, x.dtype) for x in pack_args[:8]]
        + [
            pltpu.SemaphoreType.DMA((10,)),
            pltpu.VMEM((16, rays), F32),
            pltpu.VMEM((half * room, LANES), BF16),
        ],
        compiler_params=PARAMS,
        name="pack",
    )(*pack_args)
    blocks = to_chips(outs[:half])
    blocks = blocks + [lax.ppermute(block, "region", inner) for block in blocks]
    target_in = lax.ppermute(outs[half], "region", inner)
    target_cr = lax.ppermute(outs[half + 1], "region", cross)

    image, *kept = pl.pallas_call(
        functools.partial(forward_kernel, half, group, room),
        out_shape=(
            shape(feat_width, rays, kind=BF16),
            shape(tiles, samples, hid_width, LANES),
            shape(tiles, hid_width, LANES),
            shape(tiles, hid_width, LANES),
            shape(hid_width, lanes, kind=BF16),
            shape(tiles, samples, LANES),
            shape(tiles, samples, LANES),
            shape(tiles, samples, LANES),
            shape(tiles, 1, LANES),
            shape(segs, rays, kind=jnp.int32),
            shape(code_width, rays, kind=BF16),
            shape(regions * feat_width, hid_width, kind=BF16),
        ),
        scratch_shapes=[
            pltpu.VMEM((16, regions * room), F32),
            pltpu.VMEM((samples + 1, regions, hid_width), F32),
            pltpu.VMEM((samples + 1, hid_width, 2 * regions), BF16),
            pltpu.VMEM((regions, hid_width, rays), F32),
            pltpu.VMEM((tiles, hid_width, LANES), F32),
            pltpu.VMEM((tiles, 2 * regions, LANES), BF16),
            pltpu.VMEM((tiles, 1, LANES), F32),
            pltpu.VMEM((2, 1, LANES), F32),
        ],
        compiler_params=PARAMS,
        name="forward",
    )(*blocks)

    image_in = lax.ppermute(image, "region", inner)
    image_cr = lax.ppermute(image, "region", cross)

    part = shape(half, PART_ROWS, LANES, kind=BF16)
    mine, other = pl.pallas_call(
        functools.partial(backward_kernel, half),
        out_shape=(part, part),
        scratch_shapes=[
            pltpu.VMEM((decoder.shape[0], 4 * IW), BF16),
            pltpu.VMEM((regions * feat_width, lanes), BF16),
            pltpu.VMEM((tiles, hid_width, LANES), F32),
            pltpu.VMEM((samples, hid_width, lanes), BF16),
            pltpu.VMEM((hid_width, lanes), BF16),
            pltpu.VMEM((hid_width, lanes), BF16),
            pltpu.VMEM((regions, PART_ROWS - G2_AT, hid_width), F32),
            pltpu.VMEM((tiles, 1, LANES), F32),
        ],
        compiler_params=PARAMS,
        name="backward",
    )(image, image_in, image_cr, target.T, target_in.T, target_cr.T, decoder, decoder.T, *kept)

    theirs = lax.ppermute(other, "region", inner)
    chip = pl.pallas_call(
        merge_kernel,
        out_shape=[shape(PART_ROWS, LANES, kind=BF16)] * half,
        compiler_params=PARAMS,
        name="merge",
    )(mine, theirs)
    hid_grad, feat_grad, dens_grad, code_grad = pl.pallas_call(
        finish_kernel,
        out_shape=(
            shape(1, code_width, hid_width),
            shape(1, feat_width, hid_width),
            shape(1, hid_width),
            shape(1, samples, code_width),
        ),
        compiler_params=PARAMS,
        name="finish",
    )(*to_chips(chip), sample_code, w_hidden)
    return hid_grad, feat_grad.swapaxes(1, 2), dens_grad, code_grad


def solution(mesh):
    in_specs = (
        P(("groups", "region"), None),
        P(("groups", "region"), None),
        P(("groups", "region"), None),
        P(("groups", "region")),
        P("region", None, None),
        P("region", None, None),
        P("region", None, None),
        P("region", None),
        P(),
        P(("groups", "region"), None),
    )
    out_specs = (
        P("region", "groups", None),
        P("region", "groups", None),
        P("region", "groups"),
        P("region", "groups", None),
    )
    return jax.shard_map(local, mesh=mesh, in_specs=in_specs, out_specs=out_specs, check_vma=False)
```

time: 76.9 us -> 80.4 us (1.046)
  blocking collectives: 39.1 us -> 0 us
  starting transfers between devices: 7.75 us -> 34.8 us
  local copies, waits for them, and re-layouts: 6.62 us -> 16.9 us
  waiting for transfers between devices: 1.67 us -> 9.81 us
  Pallas kernels: 20.3 us -> 17.5 us
    all_to_all x2 -> x0, blocking collectives: 39.1 us -> none  [the longest x1 21.7 us: local(): lax.all_to_all(packed, 'region', 0, 0, axis_index_groups=same_core, tiled...]
    ppermute x3 -> x24, starting transfers between devices: 3.55 us -> 27.9 us  [the longest x14 25.3 us: to_chips(): lax.ppermute(blocks[k], 'region', [(i, i ^ 2 * k) for i in range(regions)])]
    unnamed x29 -> x30, local copies, waits for them, and re-layouts: 5.92 us -> 16.6 us
    ppermute x3 -> x24, waiting for transfers between devices: 0.01 us -> 8.39 us  [the longest x14 7.91 us: to_chips(): lax.ppermute(blocks[k], 'region', [(i, i ^ 2 * k) for i in range(regions)])]
    ppermute x1, starting transfers between devices: 1.01 us -> 3.98 us  [local(): theirs = lax.ppermute(other, 'region', inner)]
    pallas_call x1, Pallas kernels: 11.5 us -> 8.82 us  [local(): pl.pallas_call(functools.partial(backward_kernel, half), out_shape=(part,...]
    pallas_call x1, Pallas kernels: 7.57 us -> 6.76 us  [local(): pl.pallas_call(functools.partial(forward_kernel, half, group, room), out_...]
  transfers between devices with their start and end apart: 6 -> 27, of which waited for: 1 -> 9; matrix products, arithmetic and copies ran while one was open for 2% -> 3% of each run, Pallas kernels for 10% -> 8%
where the time goes in v1:
time: 80.4 us; the launch traced here: 79.8 us
  starting transfers between devices  34.8 us (43%)
  Pallas kernels  17.5 us (22%)
  local copies, waits for them, and re-layouts  16.9 us (21%)
  waiting for transfers between devices  9.81 us (12%)
  between operations  0.81 us (1%)
    ppermute x14, starting transfers between devices, to_chips(): lax.ppermute(blocks[k], 'region', [(i, i ^ 2 * k) for i in range(regions)])  25.3 us
    unnamed x30, local copies, waits for them, and re-layouts  16.6 us
    pallas_call x1, Pallas kernels, local(): pl.pallas_call(functools.partial(backward_kernel, half), out_shape=(part,...  8.82 us
    ppermute x14, waiting for transfers between devices, to_chips(): lax.ppermute(blocks[k], 'region', [(i, i ^ 2 * k) for i in range(regions)])  7.91 us
    pallas_call x1, Pallas kernels, local(): pl.pallas_call(functools.partial(forward_kernel, half, group, room), out_...  6.76 us
    ppermute x1, starting transfers between devices, local(): theirs = lax.ppermute(other, 'region', inner)  3.98 us
    ppermute x1, starting transfers between devices, local(): image_in = lax.ppermute(image, 'region', inner)  2.29 us
  transfers between devices with their start and end apart: 27, of which 9 were waited for; matrix products, arithmetic and copies ran while one was open for 3% of the time, Pallas kernels for 8%

profile of v1, /device:TPU:0, one launch (start us, length us, event | category | flops | bytes accessed | tf_op | source)
XLA Modules:
  0.0 79.8 jit_solution(15926322256306514943)
XLA Ops:
  0.6 0.0 copy-start.3
  0.7 0.9 %copy-done.3 = bf16[256,384]{1,0:T(8,128)(2,1)S(1)} copy-done((bf16[256,384]{1,0:T(8,128)(2,1)S(1)}, bf16[256,384]{1,0:T(8,128)(2,1)}, u32[]{:S(2)}) %copy-start.3) | copy-done | bytes 196632
  1.6 0.8 copy-done.4
  2.3 0.8 %copy-done.6 = bf16[256,128]{1,0:T(8,128)(2,1)S(1)} copy-done((bf16[256,128]{1,0:T(8,128)(2,1)S(1)}, bf16[256,128]{1,0:T(8,128)(2,1)}, u32[]{:S(2)}) %copy-start.6) | copy-done | bytes 65560
  3.2 0.7 copy-done.7
  3.9 0.7 copy-done.9
  4.6 0.7 copy-done.10
  5.3 0.7 copy-done.11
  6.0 0.7 copy-done.12
  6.6 0.7 copy-done.13
  7.3 1.0 %pack.1 = (bf16[256,128]{1,0:T(8,128)(2,1)S(1)}, bf16[256,128]{1,0:T(8,128)(2,1)S(1)}, bf16[256,128]{1,0:T(8,128)(2,1)S(1)}, bf16[256,128]{1,0:T(8,128)(2,1)S(1)...) custom-call(s32[1,256]{1,0:T(1,128)S(1)} %bitcast.16, ...), custom_call_target="tpu_custom_call" | custom-call | tf_op jit(solution)/shard_map/pack/pallas_call | solution.py:421
  8.3 4.0 %collective-permute-start.2 = (bf16[256,128]{1,0:T(8,128)(2,1)S(1)}, bf16[256,128]{1,0:T(8,128)(2,1)S(1)}, u32[]{:S(2)}, u32[]{:S(2)}) collective-permute-start(bf16[256,128]{1,0:T(8,128)(2,1)S(1)} %get-tuple-element.43), channel_id=1, source_target_pairs={{0,6},{1,7},{2,4},{3,5},{4,2},{5,3},{6,0},{7,1},{8,14},{9,15},{10,... | collective-permute-start | bytes 196616 | tf_op jit(solution)/shard_map/ppermute | solution.py:414
  12.3 2.6 %collective-permute-start.3 = (bf16[256,128]{1,0:T(8,128)(2,1)S(1)}, bf16[256,128]{1,0:T(8,128)(2,1)S(1)}, u32[]{:S(2)}, u32[]{:S(2)}) collective-permute-start(bf16[256,128]{1,0:T(8,128)(2,1)S(1)} %get-tuple-element.44), channel_id=1, source_target_pairs={{0,8},{1,9},{2,10},{3,11},{4,12},{5,13},{6,14},{7,15},{8,0},{9,1},... | collective-permute-start | bytes 196616 | tf_op jit(solution)/shard_map/ppermute | solution.py:414
  14.9 0.3 collective-permute-start.4
  15.2 2.5 %collective-permute-start.5 = (bf16[256,128]{1,0:T(8,128)(2,1)S(1)}, bf16[256,128]{1,0:T(8,128)(2,1)S(1)}, u32[]{:S(2)}, u32[]{:S(2)}) collective-permute-start(bf16[256,128]{1,0:T(8,128)(2,1)S(1)} %get-tuple-element.46), channel_id=1, source_target_pairs={{0,12},{1,13},{2,14},{3,15},{4,8},{5,9},{6,10},{7,11},{8,4},{9,5},... | collective-permute-start | bytes 196616 | tf_op jit(solution)/shard_map/ppermute | solution.py:414
  17.7 2.3 %collective-permute-start.6 = (bf16[256,128]{1,0:T(8,128)(2,1)S(1)}, bf16[256,128]{1,0:T(8,128)(2,1)S(1)}, u32[]{:S(2)}, u32[]{:S(2)}) collective-permute-start(bf16[256,128]{1,0:T(8,128)(2,1)S(1)} %get-tuple-element.47), channel_id=1, source_target_pairs={{0,14},{1,15},{2,12},{3,13},{4,10},{5,11},{6,8},{7,9},{8,6},{9,7},... | collective-permute-start | bytes 196616 | tf_op jit(solution)/shard_map/ppermute | solution.py:414
  20.0 0.0 collective-permute-done.2.refs_3_
  20.0 0.5 collective-permute-start
  20.5 1.9 %collective-permute-start.1 = (bf16[256,128]{1,0:T(8,128)(2,1)S(1)}, bf16[256,128]{1,0:T(8,128)(2,1)S(1)}, u32[]{:S(2)}, u32[]{:S(2)}) collective-permute-start(bf16[256,128]{1,0:T(8,128)(2,1)S(1)} %get-tuple-element.42), channel_id=1, source_target_pairs={{0,4},{1,5},{2,6},{3,7},{4,0},{5,1},{6,2},{7,3},{8,12},{9,13},{10,... | collective-permute-start | bytes 196616 | tf_op jit(solution)/shard_map/ppermute | solution.py:414
  22.4 1.4 %collective-permute-done.4.refs_5_ = bf16[256,128]{1,0:T(8,128)(2,1)S(1)} collective-permute-done((bf16[256,128]{1,0:T(8,128)(2,1)S(1)}, bf16[256,128]{1,0:T(8,128)(2,1)S(1)}, u32[]{:S(2)}, u32[]{:S(2)}) %collective-permute-start.4) | collective-permute-done | bytes 65568 | tf_op jit(solution)/shard_map/ppermute | solution.py:414
  23.8 0.5 collective-permute-start.10
  24.3 0.5 collective-permute-done.6.refs_7_
  24.8 0.0 collective-permute-start.11
  24.8 0.2 collective-permute-done.refs_1_
  25.1 0.3 collective-permute-start.12
  25.3 0.1 collective-permute-done.1.refs_2_
  25.5 0.1 collective-permute-start.13
  25.6 0.1 copy.15
  25.7 0.1 copy.16
  25.8 0.0 collective-permute-done.7.refs_8_
  25.8 0.5 collective-permute-start.17
  26.3 0.0 collective-permute-done.10.refs_11_
  26.3 0.1 collective-permute-start.14
  26.4 0.0 collective-permute-done.11.refs_12_
  26.4 0.4 collective-permute-start.8
  26.8 0.0 collective-permute-done.12.refs_13_
  26.8 0.1 collective-permute-start.9
  26.9 0.7 collective-permute-start.18
  27.6 0.1 collective-permute-done.8.refs_9_
  27.7 0.4 collective-permute-done.9.refs_10_
  28.1 6.8 %forward.1 = (bf16[64,256]{1,0:T(8,128)(2,1)S(1)}, f32[8,16,128,128]{3,2,1,0:T(8,128)S(1)}, f32[8,128,128]{2,1,0:T(8,128)S(1)}, f32[8,128,128]{2,1,0:T(8,128)S(1...) custom-call(bf16[256,128]{1,0:T(8,128)(2,1)S(1)} %get-tuple-element., ...), custom_call_target="tpu_custom_call" | custom-call | tf_op jit(solution)/shard_map/forward/pallas_call | solution.py:439
  34.9 3.3 %copy-done = f32[8,16,128,128]{3,2,1,0:T(8,128)} copy-done((f32[8,16,128,128]{3,2,1,0:T(8,128)}, f32[8,16,128,128]{3,2,1,0:T(8,128)S(1)}, u32[]{:S(2)}) %copy-start) | copy-done | bytes 8388632
  38.1 2.3 %collective-permute-start.15 = (bf16[64,256]{1,0:T(8,128)(2,1)S(1)}, bf16[64,256]{1,0:T(8,128)(2,1)S(1)}, u32[]{:S(2)}, u32[]{:S(2)}) collective-permute-start(bf16[64,256]{1,0:T(8,128)(2,1)S(1)} %get-tuple-element.48.own_ref), channel_id=1, source_target_pairs={{0,1},{1,0},{2,3},{3,2},{4,5},{5,4},{6,7},{7,6},{8,9},{9,8},{10,11... | collective-permute-start | bytes 98312 | tf_op jit(solution)/shard_map/ppermute | solution.py:469
  40.4 0.7 collective-permute-start.16
  41.1 1.1 %copy.14 = bf16[256,384]{0,1:T(8,128)(2,1)S(1)} copy(bf16[256,384]{1,0:T(8,128)(2,1)} %refs_8_.2) | data formatting | bytes 393216 | tf_op args[9]
  42.1 1.3 %copy.17 = bf16[576,384]{0,1:T(8,128)(2,1)S(1)} copy(bf16[576,384]{1,0:T(8,128)(2,1)} %dec_ref.1) | data formatting | bytes 884736 | tf_op args[8]
  43.4 0.0 collective-permute-done.17
  43.4 0.0 collective-permute-done.15.inner_ref
  43.5 3.4 %copy-done.1 = f32[8,16,128,128]{3,2,1,0:T(8,128)S(1)} copy-done((f32[8,16,128,128]{3,2,1,0:T(8,128)S(1)}, f32[8,16,128,128]{3,2,1,0:T(8,128)}, u32[]{:S(2)}) %copy-start.1) | copy-done | bytes 8388632
  46.8 1.0 %copy-done.2 = bf16[576,384]{1,0:T(8,128)(2,1)S(1)} copy-done((bf16[576,384]{1,0:T(8,128)(2,1)S(1)}, bf16[576,384]{1,0:T(8,128)(2,1)}, u32[]{:S(2)}) %copy-start.2) | copy-done | bytes 442392
  47.8 8.8 %backward.1 = (bf16[8,216,128]{2,1,0:T(8,128)(2,1)S(1)}, bf16[8,216,128]{2,1,0:T(8,128)(2,1)S(1)}) custom-call(bf16[64,256]{1,0:T(8,128)(2,1)S(1)} %get-tuple-element.48.own_ref, bf16[64,256]{1,0:T(8,128)(2,1)S(1)} %collective-permute-done.15.inner_ref, bf16[64,256]{1,0:T(8,128)(2,1)S(1)} %collective-permute-done.16.cross_ref, ...), custom_call_target="tpu_custom_call" | custom-call | tf_op jit(solution)/shard_map/backward/pallas_call | solution.py:473
  56.7 4.0 %collective-permute-start.19 = (bf16[8,216,128]{2,1,0:T(8,128)(2,1)S(1)}, bf16[8,216,128]{2,1,0:T(8,128)(2,1)S(1)}, u32[]{:S(2)}, u32[]{:S(2)}) collective-permute-start(bf16[8,216,128]{2,1,0:T(8,128)(2,1)S(1)} %get-tuple-element.63), channel_id=1, source_target_pairs={{0,1},{1,0},{2,3},{3,2},{4,5},{5,4},{6,7},{7,6},{8,9},{9,8},{10,11... | collective-permute-start | bytes 1327112 | tf_op jit(solution)/shard_map/ppermute | solution.py:490
  60.6 1.4 %collective-permute-done.19.theirs_ref = bf16[8,216,128]{2,1,0:T(8,128)(2,1)S(1)} collective-permute-done((bf16[8,216,128]{2,1,0:T(8,128)(2,1)S(1)}, bf16[8,216,128]{2,1,0:T(8,128)(2,1)S(1)}, u32[]{:S(2)}, u32[]{:S(2)}) %collective-permute-start.19) | collective-permute-done | bytes 442400 | tf_op jit(solution)/shard_map/ppermute | solution.py:490
  62.1 0.1 merge.1
  62.2 1.8 %collective-permute-start.20 = (bf16[216,128]{1,0:T(8,128)(2,1)S(1)}, bf16[216,128]{1,0:T(8,128)(2,1)S(1)}, u32[]{:S(2)}, u32[]{:S(2)}) collective-permute-start(bf16[216,128]{1,0:T(8,128)(2,1)S(1)} %get-tuple-element.65), channel_id=1, source_target_pairs={{0,2},{1,3},{2,0},{3,1},{4,6},{5,7},{6,4},{7,5},{8,10},{9,11},{10,... | collective-permute-start | bytes 165896 | tf_op jit(solution)/shard_map/ppermute | solution.py:414
  64.0 1.5 %collective-permute-start.21 = (bf16[216,128]{1,0:T(8,128)(2,1)S(1)}, bf16[216,128]{1,0:T(8,128)(2,1)S(1)}, u32[]{:S(2)}, u32[]{:S(2)}) collective-permute-start(bf16[216,128]{1,0:T(8,128)(2,1)S(1)} %get-tuple-element.66), channel_id=1, source_target_pairs={{0,4},{1,5},{2,6},{3,7},{4,0},{5,1},{6,2},{7,3},{8,12},{9,13},{10,... | collective-permute-start | bytes 165896 | tf_op jit(solution)/shard_map/ppermute | solution.py:414
  65.5 0.2 collective-permute-start.22
  65.7 2.9 %collective-permute-start.23 = (bf16[216,128]{1,0:T(8,128)(2,1)S(1)}, bf16[216,128]{1,0:T(8,128)(2,1)S(1)}, u32[]{:S(2)}, u32[]{:S(2)}) collective-permute-start(bf16[216,128]{1,0:T(8,128)(2,1)S(1)} %get-tuple-element.68), channel_id=1, source_target_pairs={{0,8},{1,9},{2,10},{3,11},{4,12},{5,13},{6,14},{7,15},{8,0},{9,1},... | collective-permute-start | bytes 165896 | tf_op jit(solution)/shard_map/ppermute | solution.py:414
  68.6 1.2 %collective-permute-start.24 = (bf16[216,128]{1,0:T(8,128)(2,1)S(1)}, bf16[216,128]{1,0:T(8,128)(2,1)S(1)}, u32[]{:S(2)}, u32[]{:S(2)}) collective-permute-start(bf16[216,128]{1,0:T(8,128)(2,1)S(1)} %get-tuple-element.69), channel_id=1, source_target_pairs={{0,10},{1,11},{2,8},{3,9},{4,14},{5,15},{6,12},{7,13},{8,2},{9,3},... | collective-permute-start | bytes 165896 | tf_op jit(solution)/shard_map/ppermute | solution.py:414
  69.8 2.2 %collective-permute-start.25 = (bf16[216,128]{1,0:T(8,128)(2,1)S(1)}, bf16[216,128]{1,0:T(8,128)(2,1)S(1)}, u32[]{:S(2)}, u32[]{:S(2)}) collective-permute-start(bf16[216,128]{1,0:T(8,128)(2,1)S(1)} %get-tuple-element.70), channel_id=1, source_target_pairs={{0,12},{1,13},{2,14},{3,15},{4,8},{5,9},{6,10},{7,11},{8,4},{9,5},... | collective-permute-start | bytes 165896 | tf_op jit(solution)/shard_map/ppermute | solution.py:414
  72.0 1.4 %collective-permute-start.26 = (bf16[216,128]{1,0:T(8,128)(2,1)S(1)}, bf16[216,128]{1,0:T(8,128)(2,1)S(1)}, u32[]{:S(2)}, u32[]{:S(2)}) collective-permute-start(bf16[216,128]{1,0:T(8,128)(2,1)S(1)} %get-tuple-element.71), channel_id=1, source_target_pairs={{0,14},{1,15},{2,12},{3,13},{4,10},{5,11},{6,8},{7,9},{8,6},{9,7},... | collective-permute-start | bytes 165896 | tf_op jit(solution)/shard_map/ppermute | solution.py:414
  73.4 4.0 %collective-permute-done.24.refs_5_ = bf16[216,128]{1,0:T(8,128)(2,1)S(1)} collective-permute-done((bf16[216,128]{1,0:T(8,128)(2,1)S(1)}, bf16[216,128]{1,0:T(8,128)(2,1)S(1)}, u32[]{:S(2)}, u32[]{:S(2)}) %collective-permute-start.24) | collective-permute-done | bytes 55328 | tf_op jit(solution)/shard_map/ppermute | solution.py:414
  77.4 1.6 %collective-permute-done.26.refs_7_ = bf16[216,128]{1,0:T(8,128)(2,1)S(1)} collective-permute-done((bf16[216,128]{1,0:T(8,128)(2,1)S(1)}, bf16[216,128]{1,0:T(8,128)(2,1)S(1)}, u32[]{:S(2)}, u32[]{:S(2)}) %collective-permute-start.26) | collective-permute-done | bytes 55328 | tf_op jit(solution)/shard_map/ppermute | solution.py:414
  79.0 0.8 %finish.1 = (f32[1,128,128]{2,1,0:T(8,128)}, f32[1,64,128]{2,1,0:T(8,128)}, f32[1,128]{1,0:T(1,128)}, f32[1,16,128]{2,1,0:T(8,128)}) custom-call(bf16[216,128]{1,0:T(8,128)(2,1)S(1)} %get-tuple-element.64.refs_0_, bf16[216,128]{1,0:T(8,128)(2,1)S(1)} %collective-permute-done.20.refs_1_, bf16[216,128]{1,0:T(8,128)(2,1)S(1)} %collective-permute-done.21.refs_2_, ...), custom_call_target="tpu_custom_call" | custom-call | tf_op jit(solution)/shard_map/finish/pallas_call | solution.py:497
  (27 shorter events, 0.1 us)
Async XLA Ops:
  0.6 78.4 %copy-start.8 = (bf16[1,16,128]{2,1,0:T(8,128)(2,1)S(1)}, bf16[1,16,128]{2,1,0:T(8,128)(2,1)}, u32[]{:S(2)}) copy-start(bf16[1,16,128]{2,1,0:T(8,128)(2,1)} %refs_8_.3) | copy-start | bytes 12292
  0.6 0.9 %copy-start.3 = (bf16[256,384]{1,0:T(8,128)(2,1)S(1)}, bf16[256,384]{1,0:T(8,128)(2,1)}, u32[]{:S(2)}) copy-start(bf16[256,384]{1,0:T(8,128)(2,1)} %refs_8_.2) | copy-start | bytes 589828
  1.6 0.8 copy-start.4
  2.3 0.8 %copy-start.6 = (bf16[256,128]{1,0:T(8,128)(2,1)S(1)}, bf16[256,128]{1,0:T(8,128)(2,1)}, u32[]{:S(2)}) copy-start(bf16[256,128]{1,0:T(8,128)(2,1)} %refs_3_.1) | copy-start | bytes 196612
  3.2 0.7 copy-start.7
  3.9 0.7 copy-start.9
  4.6 0.7 copy-start.10
  5.3 0.7 copy-start.11
  6.0 0.7 copy-start.12
  6.6 0.7 copy-start.13
  7.3 71.7 %copy-start.5 = (bf16[1,128,128]{2,1,0:T(8,128)(2,1)S(1)}, bf16[1,128,128]{2,1,0:T(8,128)(2,1)}, u32[]{:S(2)}) copy-start(bf16[1,128,128]{2,1,0:T(8,128)(2,1)} %refs_9_.1) | copy-start | bytes 98308
  8.3 11.7 %collective-permute-start.2 = (bf16[256,128]{1,0:T(8,128)(2,1)S(1)}, bf16[256,128]{1,0:T(8,128)(2,1)S(1)}, u32[]{:S(2)}, u32[]{:S(2)}) collective-permute-start(bf16[256,128]{1,0:T(8,128)(2,1)S(1)} %get-tuple-element.43), channel_id=1, source_target_pairs={{0,6},{1,7},{2,4},{3,5},{4,2},{5,3},{6,0},{7,1},{8,14},{9,15},{10,... | collective-permute-start | bytes 196616 | tf_op jit(solution)/shard_map/ppermute | solution.py:414
  12.3 8.2 %collective-permute-start.3 = (bf16[256,128]{1,0:T(8,128)(2,1)S(1)}, bf16[256,128]{1,0:T(8,128)(2,1)S(1)}, u32[]{:S(2)}, u32[]{:S(2)}) collective-permute-start(bf16[256,128]{1,0:T(8,128)(2,1)S(1)} %get-tuple-element.44), channel_id=1, source_target_pairs={{0,8},{1,9},{2,10},{3,11},{4,12},{5,13},{6,14},{7,15},{8,0},{9,1},... | collective-permute-start | bytes 196616 | tf_op jit(solution)/shard_map/ppermute | solution.py:414
  14.9 8.9 %collective-permute-start.4 = (bf16[256,128]{1,0:T(8,128)(2,1)S(1)}, bf16[256,128]{1,0:T(8,128)(2,1)S(1)}, u32[]{:S(2)}, u32[]{:S(2)}) collective-permute-start(bf16[256,128]{1,0:T(8,128)(2,1)S(1)} %get-tuple-element.45), channel_id=1, source_target_pairs={{0,10},{1,11},{2,8},{3,9},{4,14},{5,15},{6,12},{7,13},{8,2},{9,3},... | collective-permute-start | bytes 196616 | tf_op jit(solution)/shard_map/ppermute | solution.py:414
  15.2 8.6 %collective-permute-start.5 = (bf16[256,128]{1,0:T(8,128)(2,1)S(1)}, bf16[256,128]{1,0:T(8,128)(2,1)S(1)}, u32[]{:S(2)}, u32[]{:S(2)}) collective-permute-start(bf16[256,128]{1,0:T(8,128)(2,1)S(1)} %get-tuple-element.46), channel_id=1, source_target_pairs={{0,12},{1,13},{2,14},{3,15},{4,8},{5,9},{6,10},{7,11},{8,4},{9,5},... | collective-permute-start | bytes 196616 | tf_op jit(solution)/shard_map/ppermute | solution.py:414
  17.7 7.1 %collective-permute-start.6 = (bf16[256,128]{1,0:T(8,128)(2,1)S(1)}, bf16[256,128]{1,0:T(8,128)(2,1)S(1)}, u32[]{:S(2)}, u32[]{:S(2)}) collective-permute-start(bf16[256,128]{1,0:T(8,128)(2,1)S(1)} %get-tuple-element.47), channel_id=1, source_target_pairs={{0,14},{1,15},{2,12},{3,13},{4,10},{5,11},{6,8},{7,9},{8,6},{9,7},... | collective-permute-start | bytes 196616 | tf_op jit(solution)/shard_map/ppermute | solution.py:414
  20.0 5.1 %collective-permute-start = (bf16[256,128]{1,0:T(8,128)(2,1)S(1)}, bf16[256,128]{1,0:T(8,128)(2,1)S(1)}, u32[]{:S(2)}, u32[]{:S(2)}) collective-permute-start(bf16[256,128]{1,0:T(8,128)(2,1)S(1)} %get-tuple-element.41), channel_id=1, source_target_pairs={{0,2},{1,3},{2,0},{3,1},{4,6},{5,7},{6,4},{7,5},{8,10},{9,11},{10,... | collective-permute-start | bytes 196616 | tf_op jit(solution)/shard_map/ppermute | solution.py:414
  20.5 5.0 %collective-permute-start.1 = (bf16[256,128]{1,0:T(8,128)(2,1)S(1)}, bf16[256,128]{1,0:T(8,128)(2,1)S(1)}, u32[]{:S(2)}, u32[]{:S(2)}) collective-permute-start(bf16[256,128]{1,0:T(8,128)(2,1)S(1)} %get-tuple-element.42), channel_id=1, source_target_pairs={{0,4},{1,5},{2,6},{3,7},{4,0},{5,1},{6,2},{7,3},{8,12},{9,13},{10,... | collective-permute-start | bytes 196616 | tf_op jit(solution)/shard_map/ppermute | solution.py:414
  23.8 2.0 %collective-permute-start.7 = (bf16[256,128]{1,0:T(8,128)(2,1)S(1)}, bf16[256,128]{1,0:T(8,128)(2,1)S(1)}, u32[]{:S(2)}, u32[]{:S(2)}) collective-permute-start(bf16[256,128]{1,0:T(8,128)(2,1)S(1)} %get-tuple-element.40.refs_0_), channel_id=1, source_target_pairs={{0,1},{1,0},{2,3},{3,2},{4,5},{5,4},{6,7},{7,6},{8,9},{9,8},{10,11... | collective-permute-start | bytes 196616 | tf_op jit(solution)/shard_map/ppermute | solution.py:435
  23.8 2.5 %collective-permute-start.10 = (bf16[256,128]{1,0:T(8,128)(2,1)S(1)}, bf16[256,128]{1,0:T(8,128)(2,1)S(1)}, u32[]{:S(2)}, u32[]{:S(2)}) collective-permute-start(bf16[256,128]{1,0:T(8,128)(2,1)S(1)} %collective-permute-done.2.refs_3_), channel_id=1, source_target_pairs={{0,1},{1,0},{2,3},{3,2},{4,5},{5,4},{6,7},{7,6},{8,9},{9,8},{10,11... | collective-permute-start | bytes 196616 | tf_op jit(solution)/shard_map/ppermute | solution.py:435
  24.8 1.6 %collective-permute-start.11 = (bf16[256,128]{1,0:T(8,128)(2,1)S(1)}, bf16[256,128]{1,0:T(8,128)(2,1)S(1)}, u32[]{:S(2)}, u32[]{:S(2)}) collective-permute-start(bf16[256,128]{1,0:T(8,128)(2,1)S(1)} %collective-permute-done.3.refs_4_), channel_id=1, source_target_pairs={{0,1},{1,0},{2,3},{3,2},{4,5},{5,4},{6,7},{7,6},{8,9},{9,8},{10,11... | collective-permute-start | bytes 196616 | tf_op jit(solution)/shard_map/ppermute | solution.py:435
  25.1 1.8 %collective-permute-start.12 = (bf16[256,128]{1,0:T(8,128)(2,1)S(1)}, bf16[256,128]{1,0:T(8,128)(2,1)S(1)}, u32[]{:S(2)}, u32[]{:S(2)}) collective-permute-start(bf16[256,128]{1,0:T(8,128)(2,1)S(1)} %collective-permute-done.4.refs_5_), channel_id=1, source_target_pairs={{0,1},{1,0},{2,3},{3,2},{4,5},{5,4},{6,7},{7,6},{8,9},{9,8},{10,11... | collective-permute-start | bytes 196616 | tf_op jit(solution)/shard_map/ppermute | solution.py:435
  25.5 1.5 %collective-permute-start.13 = (bf16[256,128]{1,0:T(8,128)(2,1)S(1)}, bf16[256,128]{1,0:T(8,128)(2,1)S(1)}, u32[]{:S(2)}, u32[]{:S(2)}) collective-permute-start(bf16[256,128]{1,0:T(8,128)(2,1)S(1)} %collective-permute-done.5.refs_6_), channel_id=1, source_target_pairs={{0,1},{1,0},{2,3},{3,2},{4,5},{5,4},{6,7},{7,6},{8,9},{9,8},{10,11... | collective-permute-start | bytes 196616 | tf_op jit(solution)/shard_map/ppermute | solution.py:435
  25.8 17.6 %collective-permute-start.17 = (bf16[128,384]{0,1:T(8,128)(2,1)S(1)}, bf16[128,384]{0,1:T(8,128)(2,1)S(1)}, u32[]{:S(2)}, u32[]{:S(2)}) collective-permute-start(bf16[128,384]{0,1:T(8,128)(2,1)S(1)} %copy.15), channel_id=1, source_target_pairs={{0,1},{1,0},{2,3},{3,2},{4,5},{5,4},{6,7},{7,6},{8,9},{9,8},{10,11... | collective-permute-start | bytes 294920 | tf_op jit(solution)/shard_map/ppermute | solution.py:436
  26.3 1.3 %collective-permute-start.14 = (bf16[256,128]{1,0:T(8,128)(2,1)S(1)}, bf16[256,128]{1,0:T(8,128)(2,1)S(1)}, u32[]{:S(2)}, u32[]{:S(2)}) collective-permute-start(bf16[256,128]{1,0:T(8,128)(2,1)S(1)} %collective-permute-done.6.refs_7_), channel_id=1, source_target_pairs={{0,1},{1,0},{2,3},{3,2},{4,5},{5,4},{6,7},{7,6},{8,9},{9,8},{10,11... | collective-permute-start | bytes 196616 | tf_op jit(solution)/shard_map/ppermute | solution.py:435
  26.4 1.3 %collective-permute-start.8 = (bf16[256,128]{1,0:T(8,128)(2,1)S(1)}, bf16[256,128]{1,0:T(8,128)(2,1)S(1)}, u32[]{:S(2)}, u32[]{:S(2)}) collective-permute-start(bf16[256,128]{1,0:T(8,128)(2,1)S(1)} %collective-permute-done.refs_1_), channel_id=1, source_target_pairs={{0,1},{1,0},{2,3},{3,2},{4,5},{5,4},{6,7},{7,6},{8,9},{9,8},{10,11... | collective-permute-start | bytes 196616 | tf_op jit(solution)/shard_map/ppermute | solution.py:435
  26.8 1.3 %collective-permute-start.9 = (bf16[256,128]{1,0:T(8,128)(2,1)S(1)}, bf16[256,128]{1,0:T(8,128)(2,1)S(1)}, u32[]{:S(2)}, u32[]{:S(2)}) collective-permute-start(bf16[256,128]{1,0:T(8,128)(2,1)S(1)} %collective-permute-done.1.refs_2_), channel_id=1, source_target_pairs={{0,1},{1,0},{2,3},{3,2},{4,5},{5,4},{6,7},{7,6},{8,9},{9,8},{10,11... | collective-permute-start | bytes 196616 | tf_op jit(solution)/shard_map/ppermute | solution.py:435
  26.9 16.5 %collective-permute-start.18 = (bf16[128,384]{0,1:T(8,128)(2,1)S(1)}, bf16[128,384]{0,1:T(8,128)(2,1)S(1)}, u32[]{:S(2)}, u32[]{:S(2)}) collective-permute-start(bf16[128,384]{0,1:T(8,128)(2,1)S(1)} %copy.16), channel_id=1, source_target_pairs={{1,2},{3,4},{5,6},{7,8},{9,10},{11,12},{13,14},{2,1},{4,3},{6,5},{... | collective-permute-start | bytes 294920 | tf_op jit(solution)/shard_map/ppermute | solution.py:437
  34.8 3.3 %copy-start = (f32[8,16,128,128]{3,2,1,0:T(8,128)}, f32[8,16,128,128]{3,2,1,0:T(8,128)S(1)}, u32[]{:S(2)}) copy-start(f32[8,16,128,128]{3,2,1,0:T(8,128)S(1)} %get-tuple-element.51.h_in) | copy-start | bytes 25165828
  38.1 5.3 %collective-permute-start.15 = (bf16[64,256]{1,0:T(8,128)(2,1)S(1)}, bf16[64,256]{1,0:T(8,128)(2,1)S(1)}, u32[]{:S(2)}, u32[]{:S(2)}) collective-permute-start(bf16[64,256]{1,0:T(8,128)(2,1)S(1)} %get-tuple-element.48.own_ref), channel_id=1, source_target_pairs={{0,1},{1,0},{2,3},{3,2},{4,5},{5,4},{6,7},{7,6},{8,9},{9,8},{10,11... | collective-permute-start | bytes 98312 | tf_op jit(solution)/shard_map/ppermute | solution.py:469
  40.4 3.0 %collective-permute-start.16 = (bf16[64,256]{1,0:T(8,128)(2,1)S(1)}, bf16[64,256]{1,0:T(8,128)(2,1)S(1)}, u32[]{:S(2)}, u32[]{:S(2)}) collective-permute-start(bf16[64,256]{1,0:T(8,128)(2,1)S(1)} %get-tuple-element.48.own_ref), channel_id=1, source_target_pairs={{1,2},{3,4},{5,6},{7,8},{9,10},{11,12},{13,14},{2,1},{4,3},{6,5},{... | collective-permute-start | bytes 98312 | tf_op jit(solution)/shard_map/ppermute | solution.py:470
  43.4 3.4 %copy-start.1 = (f32[8,16,128,128]{3,2,1,0:T(8,128)S(1)}, f32[8,16,128,128]{3,2,1,0:T(8,128)}, u32[]{:S(2)}) copy-start(f32[8,16,128,128]{3,2,1,0:T(8,128)} %copy-done) | copy-start | bytes 25165828
  46.8 1.0 %copy-start.2 = (bf16[576,384]{1,0:T(8,128)(2,1)S(1)}, bf16[576,384]{1,0:T(8,128)(2,1)}, u32[]{:S(2)}) copy-start(bf16[576,384]{1,0:T(8,128)(2,1)} %dec_ref.1) | copy-start | bytes 1327108
  56.7 5.4 %collective-permute-start.19 = (bf16[8,216,128]{2,1,0:T(8,128)(2,1)S(1)}, bf16[8,216,128]{2,1,0:T(8,128)(2,1)S(1)}, u32[]{:S(2)}, u32[]{:S(2)}) collective-permute-start(bf16[8,216,128]{2,1,0:T(8,128)(2,1)S(1)} %get-tuple-element.63), channel_id=1, source_target_pairs={{0,1},{1,0},{2,3},{3,2},{4,5},{5,4},{6,7},{7,6},{8,9},{9,8},{10,11... | collective-permute-start | bytes 1327112 | tf_op jit(solution)/shard_map/ppermute | solution.py:490
  62.2 7.7 %collective-permute-start.20 = (bf16[216,128]{1,0:T(8,128)(2,1)S(1)}, bf16[216,128]{1,0:T(8,128)(2,1)S(1)}, u32[]{:S(2)}, u32[]{:S(2)}) collective-permute-start(bf16[216,128]{1,0:T(8,128)(2,1)S(1)} %get-tuple-element.65), channel_id=1, source_target_pairs={{0,2},{1,3},{2,0},{3,1},{4,6},{5,7},{6,4},{7,5},{8,10},{9,11},{10,... | collective-permute-start | bytes 165896 | tf_op jit(solution)/shard_map/ppermute | solution.py:414
  64.0 8.1 %collective-permute-start.21 = (bf16[216,128]{1,0:T(8,128)(2,1)S(1)}, bf16[216,128]{1,0:T(8,128)(2,1)S(1)}, u32[]{:S(2)}, u32[]{:S(2)}) collective-permute-start(bf16[216,128]{1,0:T(8,128)(2,1)S(1)} %get-tuple-element.66), channel_id=1, source_target_pairs={{0,4},{1,5},{2,6},{3,7},{4,0},{5,1},{6,2},{7,3},{8,12},{9,13},{10,... | collective-permute-start | bytes 165896 | tf_op jit(solution)/shard_map/ppermute | solution.py:414
  65.5 7.9 %collective-permute-start.22 = (bf16[216,128]{1,0:T(8,128)(2,1)S(1)}, bf16[216,128]{1,0:T(8,128)(2,1)S(1)}, u32[]{:S(2)}, u32[]{:S(2)}) collective-permute-start(bf16[216,128]{1,0:T(8,128)(2,1)S(1)} %get-tuple-element.67), channel_id=1, source_target_pairs={{0,6},{1,7},{2,4},{3,5},{4,2},{5,3},{6,0},{7,1},{8,14},{9,15},{10,... | collective-permute-start | bytes 165896 | tf_op jit(solution)/shard_map/ppermute | solution.py:414
  65.7 7.7 %collective-permute-start.23 = (bf16[216,128]{1,0:T(8,128)(2,1)S(1)}, bf16[216,128]{1,0:T(8,128)(2,1)S(1)}, u32[]{:S(2)}, u32[]{:S(2)}) collective-permute-start(bf16[216,128]{1,0:T(8,128)(2,1)S(1)} %get-tuple-element.68), channel_id=1, source_target_pairs={{0,8},{1,9},{2,10},{3,11},{4,12},{5,13},{6,14},{7,15},{8,0},{9,1},... | collective-permute-start | bytes 165896 | tf_op jit(solution)/shard_map/ppermute | solution.py:414
  68.6 8.8 %collective-permute-start.24 = (bf16[216,128]{1,0:T(8,128)(2,1)S(1)}, bf16[216,128]{1,0:T(8,128)(2,1)S(1)}, u32[]{:S(2)}, u32[]{:S(2)}) collective-permute-start(bf16[216,128]{1,0:T(8,128)(2,1)S(1)} %get-tuple-element.69), channel_id=1, source_target_pairs={{0,10},{1,11},{2,8},{3,9},{4,14},{5,15},{6,12},{7,13},{8,2},{9,3},... | collective-permute-start | bytes 165896 | tf_op jit(solution)/shard_map/ppermute | solution.py:414
  69.8 7.5 %collective-permute-start.25 = (bf16[216,128]{1,0:T(8,128)(2,1)S(1)}, bf16[216,128]{1,0:T(8,128)(2,1)S(1)}, u32[]{:S(2)}, u32[]{:S(2)}) collective-permute-start(bf16[216,128]{1,0:T(8,128)(2,1)S(1)} %get-tuple-element.70), channel_id=1, source_target_pairs={{0,12},{1,13},{2,14},{3,15},{4,8},{5,9},{6,10},{7,11},{8,4},{9,5},... | collective-permute-start | bytes 165896 | tf_op jit(solution)/shard_map/ppermute | solution.py:414
  72.0 7.0 %collective-permute-start.26 = (bf16[216,128]{1,0:T(8,128)(2,1)S(1)}, bf16[216,128]{1,0:T(8,128)(2,1)S(1)}, u32[]{:S(2)}, u32[]{:S(2)}) collective-permute-start(bf16[216,128]{1,0:T(8,128)(2,1)S(1)} %get-tuple-element.71), channel_id=1, source_target_pairs={{0,14},{1,15},{2,12},{3,13},{4,10},{5,11},{6,8},{7,9},{8,6},{9,7},... | collective-permute-start | bytes 165896 | tf_op jit(solution)/shard_map/ppermute | solution.py:414

commit v2 on v1

--- a/solution.py
+++ b/solution.py
@@ -21,7 +21,9 @@
 DG_AT = 208
 PART_ROWS = 216
 
-PARAMS = pltpu.CompilerParams(vmem_limit_bytes=40 << 20)
+
+def grant(mib):
+    return pltpu.CompilerParams(vmem_limit_bytes=int(mib * (1 << 20)))
 
 
 def iota(shape, dim):
@@ -48,20 +50,14 @@
 
 
 def pack_kernel(half, group, room, *refs):
-    hbm, blocks, halos, held, sems = refs[:9], refs[9 : 9 + half], refs[9 + half : 11 + half], refs[11 + half : 19 + half], refs[19 + half]
-    meta_ref, codes_ref = refs[20 + half :]
+    hbm, blocks, held, sems = refs[:8], refs[8 : 8 + half], refs[8 + half : 16 + half], refs[16 + half]
+    meta_ref, codes_ref = refs[17 + half :]
     me = lax.axis_index("region")
-    core = me & 1
     mine = lax.shift_right_logical(me, 1)
     copies = [pltpu.make_async_copy(hbm[i], held[i], sems.at[i]) for i in range(8)]
-    target, width = hbm[8], halos[0].shape[0]
-    inward = pl.multiple_of((1 - core) * width, width)
-    outward = pl.multiple_of(core * width, width)
-    copies.append(pltpu.make_async_copy(target.at[pl.ds(inward, width)], halos[0], sems.at[8]))
-    copies.append(pltpu.make_async_copy(target.at[pl.ds(outward, width)], halos[1], sems.at[9]))
     for copy in copies:
         copy.start()
-    for copy in copies[:8]:
+    for copy in copies:
         copy.wait()
     pix_ref, reg_ref, cnt_ref, code_ref, samp_ref, wh_ref, wf_ref, wd_ref = held
     rays = code_ref.shape[0]
@@ -95,8 +91,6 @@
         here = pltpu.roll(meta, (rays - chip * 2 * group) & (rays - 1), 1)[:, :LANES]
         out_ref[META_AT:RAYS_AT] = jnp.where(first, density, here).astype(BF16)
         out_ref[RAYS_AT : RAYS_AT + room] = codes_ref[pl.ds(pl.multiple_of(chip * room, 16), room), :]
-    for copy in copies[8:]:
-        copy.wait()
 
 
 def bits_of(row, regions):
@@ -119,11 +113,11 @@
 
 def forward_kernel(half, group, room, *refs):
     regions = 2 * half
-    blocks = refs[:regions]
+    blocks, target_ref = refs[:regions], refs[regions]
     (
-        image_ref, h_ref, wd_ref, att_hw_ref, wide_hw_ref, weight_ref, pass_ref, slope_ref, att_ref, rel_ref, codes_ref, wf_out,
+        image_ref, halo_in_ref, halo_cr_ref, h_ref, wd_ref, att_hw_ref, wide_hw_ref, weight_ref, pass_ref, slope_ref, att_ref, rel_ref, codes_ref, wf_out,
         meta_ref, plain_ref, table_ref, proj_ref, a_ref, picked_ref, row_ref, ahead_ref,
-    ) = refs[regions:]
+    ) = refs[regions + 1 :]
     rays = codes_ref.shape[1]
     segs = rel_ref.shape[0]
     samples = weight_ref.shape[1]
@@ -243,6 +237,12 @@
                     values.append(proj_ref[at // LANES, at % LANES : at % LANES + 8, 0:LANES])
                 feat[ft] = feat[ft] + choose(values, bits)
         image_ref[:, part * LANES : (part + 1) * LANES] = jnp.concatenate(feat, axis=0).astype(BF16)
+    near, far = target_ref[:, :IW].astype(F32), target_ref[:, rays - IW :].astype(F32)
+    for out_ref, row in ((halo_in_ref, jnp.where(core == 0, far, near)), (halo_cr_ref, jnp.where(core == 0, near, far))):
+        out_ref[0:feats] = image_ref[...]
+        depth = target_ref.shape[0] // 2
+        out_ref[feats:, 0:IW] = row[:depth].astype(BF16)
+        out_ref[feats:, rays - IW :] = row[depth:].astype(BF16)
 
 
 def shifted(values, by):
@@ -255,7 +255,7 @@
 
 
 def backward_kernel(
-    half, own_ref, inner_ref, cross_ref, tgt_ref, tin_ref, tcr_ref, dec_ref, dect_ref,
+    half, own_ref, inner_ref, cross_ref, tgt_ref, dec_ref, dect_ref,
     h_in, wd_ref, att_hw_ref, wide_hw_ref, weight_ref, pass_ref, slope_ref, att_ref, rel_ref, codes_ref, wf_ref,
     mine_ref, other_ref,
     patch_ref, masked_ref, q_ref, gp_ref, g1_ref, hd_ref, tail_ref, row_ref,
@@ -267,8 +267,10 @@
     me = lax.axis_index("region")
     core = me & 1
     own = own_ref[...].astype(F32)
-    inner = inner_ref[...].astype(F32)
-    cross = cross_ref[...].astype(F32)
+    halo_in = inner_ref[...].astype(F32)
+    halo_cr = cross_ref[...].astype(F32)
+    inner, tin = halo_in[:feats], jnp.concatenate([halo_in[feats:, :IW], halo_in[feats:, rays - IW :]], axis=0)
+    cross, tcr = halo_cr[:feats], jnp.concatenate([halo_cr[feats:, :IW], halo_cr[feats:, rays - IW :]], axis=0)
     top = jnp.where(core == 0, cross, inner)
     bottom = jnp.where(core == 0, inner, cross)
     rows = [v[:, i * IW : (i + 1) * IW] for v in (top, own, bottom) for i in range(2)]
@@ -278,8 +280,6 @@
             for dy in range(3):
                 if 0 <= at - dy < 4:
                     patch_ref[(3 * dy + dx) * feats : (3 * dy + dx + 1) * feats, (at - dy) * IW : (at - dy + 1) * IW] = piece
-    tin = tin_ref[...].astype(F32)
-    tcr = tcr_ref[...].astype(F32)
     t_top = jnp.where(core == 0, tcr, tin)
     t_bottom = jnp.where(core == 0, tin, tcr)
     decoded = dot(dect_ref[...], patch_ref[...])
@@ -371,6 +371,13 @@
         out[to, G2_AT:PART_ROWS] = tail_ref[r].astype(BF16)
 
 
+def flip_kernel(target_ref, decoder_ref, block_ref, target_out, decoder_out, same_out, block_out):
+    block_out[...] = block_ref[...]
+    same_out[...] = decoder_ref[...]
+    target_out[...] = target_ref[...].astype(F32).T.astype(BF16)
+    decoder_out[...] = decoder_ref[...].astype(F32).T.astype(BF16)
+
+
 def merge_kernel(mine_ref, theirs_ref, *outs):
     for k, out in enumerate(outs):
         out[...] = (mine_ref[k].astype(F32) + theirs_ref[k].astype(F32)).astype(BF16)
@@ -416,30 +423,43 @@
 
     pack_args = (
         pixel_of_ray.reshape(1, rays), seg_region.T, seg_count.T,
-        ray_code, sample_code, w_hidden, w_feat.swapaxes(1, 2), w_density, target,
+        ray_code, sample_code, w_hidden, w_feat.swapaxes(1, 2), w_density,
     )
     outs = pl.pallas_call(
         functools.partial(pack_kernel, half, group, room),
-        out_shape=[shape(RAYS_AT + room, LANES, kind=BF16)] * half + [shape(IW, dino_width, kind=BF16)] * 2,
-        in_specs=[pl.BlockSpec(memory_space=pltpu.HBM)] * 9,
-        scratch_shapes=[pltpu.VMEM(x.shape, x.dtype) for x in pack_args[:8]]
+        out_shape=[shape(RAYS_AT + room, LANES, kind=BF16)] * half,
+        in_specs=[pl.BlockSpec(memory_space=pltpu.HBM)] * 8,
+        scratch_shapes=[pltpu.VMEM(x.shape, x.dtype) for x in pack_args]
         + [
-            pltpu.SemaphoreType.DMA((10,)),
+            pltpu.SemaphoreType.DMA((8,)),
             pltpu.VMEM((16, rays), F32),
             pltpu.VMEM((half * room, LANES), BF16),
         ],
-        compiler_params=PARAMS,
+        compiler_params=grant(60),
         name="pack",
     )(*pack_args)
-    blocks = to_chips(outs[:half])
+    target, decoder, own_block = lax.optimization_barrier((target, decoder, outs[0]))
+    target_t, decoder_t, decoder, own_block = pl.pallas_call(
+        flip_kernel,
+        out_shape=(
+            shape(dino_width, rays, kind=BF16),
+            shape(*decoder.shape[::-1], kind=BF16),
+            shape(*decoder.shape, kind=BF16),
+            shape(*own_block.shape, kind=BF16),
+        ),
+        compiler_params=grant(8),
+        name="flip",
+    )(target, decoder, own_block)
+    blocks = to_chips([own_block] + list(outs[1:]))
+    blocks[1], (blocks[0], target_t) = lax.optimization_barrier((blocks[1], (blocks[0], target_t)))
     blocks = blocks + [lax.ppermute(block, "region", inner) for block in blocks]
-    target_in = lax.ppermute(outs[half], "region", inner)
-    target_cr = lax.ppermute(outs[half + 1], "region", cross)
-
-    image, *kept = pl.pallas_call(
+
+    image, halo_in, halo_cr, *kept = pl.pallas_call(
         functools.partial(forward_kernel, half, group, room),
         out_shape=(
             shape(feat_width, rays, kind=BF16),
+            shape(feat_width + dino_width // 2, rays, kind=BF16),
+            shape(feat_width + dino_width // 2, rays, kind=BF16),
             shape(tiles, samples, hid_width, LANES),
             shape(tiles, hid_width, LANES),
             shape(tiles, hid_width, LANES),
@@ -462,12 +482,12 @@
             pltpu.VMEM((tiles, 1, LANES), F32),
             pltpu.VMEM((2, 1, LANES), F32),
         ],
-        compiler_params=PARAMS,
+        compiler_params=grant(10 + regions / 4),
         name="forward",
-    )(*blocks)
-
-    image_in = lax.ppermute(image, "region", inner)
-    image_cr = lax.ppermute(image, "region", cross)
+    )(*blocks, target_t)
+
+    halo_in = lax.ppermute(halo_in, "region", inner)
+    halo_cr = lax.ppermute(halo_cr, "region", cross)
 
     part = shape(half, PART_ROWS, LANES, kind=BF16)
     mine, other = pl.pallas_call(
@@ -483,15 +503,15 @@
             pltpu.VMEM((regions, PART_ROWS - G2_AT, hid_width), F32),
             pltpu.VMEM((tiles, 1, LANES), F32),
         ],
-        compiler_params=PARAMS,
+        compiler_params=grant(16 + regions / 4),
         name="backward",
-    )(image, image_in, image_cr, target.T, target_in.T, target_cr.T, decoder, decoder.T, *kept)
+    )(image, halo_in, halo_cr, target_t, decoder, decoder_t, *kept)
 
     theirs = lax.ppermute(other, "region", inner)
     chip = pl.pallas_call(
         merge_kernel,
         out_shape=[shape(PART_ROWS, LANES, kind=BF16)] * half,
-        compiler_params=PARAMS,
+        compiler_params=grant(8 + regions / 8),
         name="merge",
     )(mine, theirs)
     hid_grad, feat_grad, dens_grad, code_grad = pl.pallas_call(
@@ -502,7 +522,7 @@
             shape(1, hid_width),
             shape(1, samples, code_width),
         ),
-        compiler_params=PARAMS,
+        compiler_params=grant(8 + regions / 8),
         name="finish",
     )(*to_chips(chip), sample_code, w_hidden)
     return hid_grad, feat_grad.swapaxes(1, 2), dens_grad, code_grad

time: 80.4 us -> 69.3 us (0.86)
  local copies, waits for them, and re-layouts: 16.9 us -> 2.79 us
  waiting for transfers between devices: 9.81 us -> 13.1 us
  Pallas kernels: 17.5 us -> 19.1 us
  starting transfers between devices: 34.8 us -> 33.2 us
    unnamed x30 -> x10, local copies, waits for them, and re-layouts: 16.6 us -> 2.79 us
    ppermute x4 -> x2, starting transfers between devices: 4.05 us -> 1.07 us  [the longest x1 0.66 us: local(): halo_cr = lax.ppermute(halo_cr, 'region', cross)]
    ppermute x14, waiting for transfers between devices: 7.91 us -> 10.5 us  [to_chips(): lax.ppermute(blocks[k], 'region', [(i, i ^ 2 * k) for i in range(regions)])]
    ppermute x1, starting transfers between devices: 3.98 us -> 5.49 us  [local(): theirs = lax.ppermute(other, 'region', inner)]
    pallas_call x1, Pallas kernels: 0.99 us -> 2.2 us  [local(): pl.pallas_call(functools.partial(pack_kernel, half, group, room), out_sha...]
  transfers between devices with their start and end apart: 27 -> 25, of which waited for: 9 -> 9; matrix products, arithmetic and copies ran while one was open for 3% -> 0% of each run, Pallas kernels for 8% -> 0%
where the time goes in v2:
time: 69.3 us; the launch traced here: 69 us
  starting transfers between devices  33.2 us (48%)
  Pallas kernels  19.1 us (28%)
  waiting for transfers between devices  13.1 us (19%)
  local copies, waits for them, and re-layouts  2.79 us (4%)
  between operations  0.73 us (1%)
    ppermute x14, starting transfers between devices, to_chips(): lax.ppermute(blocks[k], 'region', [(i, i ^ 2 * k) for i in range(regions)])  24.6 us
    ppermute x14, waiting for transfers between devices, to_chips(): lax.ppermute(blocks[k], 'region', [(i, i ^ 2 * k) for i in range(regions)])  10.5 us
    pallas_call x1, Pallas kernels, local(): pl.pallas_call(functools.partial(backward_kernel, half), out_shape=(part,...  8.85 us
    pallas_call x1, Pallas kernels, local(): pl.pallas_call(functools.partial(forward_kernel, half, group, room), out_...  6.83 us
    ppermute x1, starting transfers between devices, local(): theirs = lax.ppermute(other, 'region', inner)  5.49 us
    unnamed x10, local copies, waits for them, and re-layouts  2.79 us
    pallas_call x1, Pallas kernels, local(): pl.pallas_call(functools.partial(pack_kernel, half, group, room), out_sha...  2.2 us
    ppermute x8, starting transfers between devices, local(): blocks = blocks + [lax.ppermute(block, 'region', inner) for block in blocks]  2.12 us
  transfers between devices with their start and end apart: 25, of which 9 were waited for; matrix products, arithmetic and copies ran while one was open for 0% of the time, Pallas kernels for 0%

profile of v2, /device:TPU:0, one launch (start us, length us, event | category | flops | bytes accessed | tf_op | source)
XLA Modules:
  0.0 69.0 jit_solution(17359759898834462707)
XLA Ops:
  0.6 0.0 copy-start.2
  0.6 0.0 copy-start.4
  0.7 2.2 %pack.1 = (bf16[256,128]{1,0:T(8,128)(2,1)}, bf16[256,128]{1,0:T(8,128)(2,1)}, bf16[256,128]{1,0:T(8,128)(2,1)}, bf16[256,128]{1,0:T(8,128)(2,1)}, bf16[256,128]...) custom-call(s32[1,256]{1,0:T(1,128)} %bitcast.8, ...), custom_call_target="tpu_custom_call" | custom-call | tf_op jit(solution)/shard_map/pack/pallas_call | solution.py:428
  2.9 3.0 %collective-permute-start = (bf16[256,128]{1,0:T(8,128)(2,1)}, bf16[256,128]{1,0:T(8,128)(2,1)S(1)}, u32[]{:S(2)}, u32[]{:S(2)}) collective-permute-start(bf16[256,128]{1,0:T(8,128)(2,1)} %get-tuple-element.50), channel_id=1, source_target_pairs={{0,2},{1,3},{2,0},{3,1},{4,6},{5,7},{6,4},{7,5},{8,10},{9,11},{10,... | collective-permute-start | bytes 196616 | tf_op jit(solution)/shard_map/ppermute | solution.py:421
  5.9 1.6 %collective-permute-start.1 = (bf16[256,128]{1,0:T(8,128)(2,1)}, bf16[256,128]{1,0:T(8,128)(2,1)S(1)}, u32[]{:S(2)}, u32[]{:S(2)}) collective-permute-start(bf16[256,128]{1,0:T(8,128)(2,1)} %get-tuple-element.59), channel_id=1, source_target_pairs={{0,4},{1,5},{2,6},{3,7},{4,0},{5,1},{6,2},{7,3},{8,12},{9,13},{10,... | collective-permute-start | bytes 196616 | tf_op jit(solution)/shard_map/ppermute | solution.py:421
  7.4 0.0 collective-permute-start.2
  7.5 3.0 %collective-permute-start.3 = (bf16[256,128]{1,0:T(8,128)(2,1)}, bf16[256,128]{1,0:T(8,128)(2,1)S(1)}, u32[]{:S(2)}, u32[]{:S(2)}) collective-permute-start(bf16[256,128]{1,0:T(8,128)(2,1)} %get-tuple-element.61), channel_id=1, source_target_pairs={{0,8},{1,9},{2,10},{3,11},{4,12},{5,13},{6,14},{7,15},{8,0},{9,1},... | collective-permute-start | bytes 196616 | tf_op jit(solution)/shard_map/ppermute | solution.py:421
  10.5 1.3 %collective-permute-start.4 = (bf16[256,128]{1,0:T(8,128)(2,1)}, bf16[256,128]{1,0:T(8,128)(2,1)S(1)}, u32[]{:S(2)}, u32[]{:S(2)}) collective-permute-start(bf16[256,128]{1,0:T(8,128)(2,1)} %get-tuple-element.62), channel_id=1, source_target_pairs={{0,10},{1,11},{2,8},{3,9},{4,14},{5,15},{6,12},{7,13},{8,2},{9,3},... | collective-permute-start | bytes 196616 | tf_op jit(solution)/shard_map/ppermute | solution.py:421
  11.7 0.0 collective-permute-done.refs_1_
  11.7 3.6 %collective-permute-start.5 = (bf16[256,128]{1,0:T(8,128)(2,1)}, bf16[256,128]{1,0:T(8,128)(2,1)S(1)}, u32[]{:S(2)}, u32[]{:S(2)}) collective-permute-start(bf16[256,128]{1,0:T(8,128)(2,1)} %get-tuple-element.63), channel_id=1, source_target_pairs={{0,12},{1,13},{2,14},{3,15},{4,8},{5,9},{6,10},{7,11},{8,4},{9,5},... | collective-permute-start | bytes 196616 | tf_op jit(solution)/shard_map/ppermute | solution.py:421
  15.3 0.0 collective-permute-done.1.refs_2_
  15.3 0.0 collective-permute-start.6
  15.4 0.0 collective-permute-done.2.refs_3_
  15.4 0.0 collective-permute-start.9
  15.4 0.0 collective-permute-done.3.refs_4_
  15.4 0.5 collective-permute-start.10
  15.9 4.9 %collective-permute-done.4.refs_5_ = bf16[256,128]{1,0:T(8,128)(2,1)S(1)} collective-permute-done((bf16[256,128]{1,0:T(8,128)(2,1)}, bf16[256,128]{1,0:T(8,128)(2,1)S(1)}, u32[]{:S(2)}, u32[]{:S(2)}) %collective-permute-start.4) | collective-permute-done | bytes 65568 | tf_op jit(solution)/shard_map/ppermute | solution.py:421
  20.9 0.0 collective-permute-start.11
  20.9 0.0 copy-start
  20.9 1.0 %copy-done = bf16[576,384]{1,0:T(8,128)(2,1)S(1)} copy-done((bf16[576,384]{1,0:T(8,128)(2,1)S(1)}, bf16[576,384]{1,0:T(8,128)(2,1)}, u32[]{:S(2)}) %copy-start) | copy-done | bytes 442392
  21.9 0.9 %copy-done.1 = bf16[256,384]{1,0:T(8,128)(2,1)S(1)} copy-done((bf16[256,384]{1,0:T(8,128)(2,1)S(1)}, bf16[256,384]{1,0:T(8,128)(2,1)}, u32[]{:S(2)}) %copy-start.1) | copy-done | bytes 196632
  22.8 0.8 %copy-done.3 = bf16[256,128]{1,0:T(8,128)(2,1)S(1)} copy-done((bf16[256,128]{1,0:T(8,128)(2,1)S(1)}, bf16[256,128]{1,0:T(8,128)(2,1)}, u32[]{:S(2)}) %copy-start.3) | copy-done | bytes 65560
  23.6 0.3 flip.1
  23.9 0.0 collective-permute-done.5.refs_6_
  23.9 0.6 collective-permute-start.7
  24.5 0.0 collective-permute-done.6.refs_7_
  24.5 0.1 collective-permute-start.12
  24.6 0.0 collective-permute-done.9.refs_10_
  24.6 0.4 collective-permute-start.13
  25.0 0.0 collective-permute-done.10.refs_11_
  25.0 0.1 collective-permute-start.14
  25.1 0.0 collective-permute-done.11.refs_12_
  25.1 0.4 collective-permute-start.8
  25.5 0.2 collective-permute-done.12.refs_13_
  25.8 0.2 collective-permute-done.13.refs_14_
  25.9 0.4 collective-permute-done.14.refs_15_
  26.3 0.0 collective-permute-done.7.refs_8_
  26.3 0.2 collective-permute-done.8.refs_9_
  26.4 6.8 %forward.1 = (bf16[64,256]{1,0:T(8,128)(2,1)S(1)}, bf16[256,256]{1,0:T(8,128)(2,1)S(1)}, bf16[256,256]{1,0:T(8,128)(2,1)S(1)}, f32[8,16,128,128]{3,2,1,0:T(8,128...) custom-call(bf16[256,128]{1,0:T(8,128)(2,1)S(1)} %get-tuple-element., ...), custom_call_target="tpu_custom_call" | custom-call | tf_op jit(solution)/shard_map/forward/pallas_call | solution.py:457
  33.3 0.4 collective-permute-start.15
  33.7 0.7 collective-permute-start.16
  34.4 0.3 collective-permute-done.15.inner_ref
  34.7 0.0 collective-permute-done.16.cross_ref
  34.7 8.9 %backward.1 = (bf16[8,216,128]{2,1,0:T(8,128)(2,1)S(1)}, bf16[8,216,128]{2,1,0:T(8,128)(2,1)S(1)}) custom-call(bf16[64,256]{1,0:T(8,128)(2,1)S(1)} %get-tuple-element.66.own_ref, bf16[256,256]{1,0:T(8,128)(2,1)S(1)} %collective-permute-done.15.inner_ref, bf16[256,256]{1,0:T(8,128)(2,1)S(1)} %collective-permute-done.16.cross_ref, ...), custom_call_target="tpu_custom_call" | custom-call | tf_op jit(solution)/shard_map/backward/pallas_call | solution.py:493
  43.6 5.5 %collective-permute-start.17 = (bf16[8,216,128]{2,1,0:T(8,128)(2,1)S(1)}, bf16[8,216,128]{2,1,0:T(8,128)(2,1)S(1)}, u32[]{:S(2)}, u32[]{:S(2)}) collective-permute-start(bf16[8,216,128]{2,1,0:T(8,128)(2,1)S(1)} %get-tuple-element.83), channel_id=1, source_target_pairs={{0,1},{1,0},{2,3},{3,2},{4,5},{5,4},{6,7},{7,6},{8,9},{9,8},{10,11... | collective-permute-start | bytes 1327112 | tf_op jit(solution)/shard_map/ppermute | solution.py:510
  49.0 1.4 %collective-permute-done.17.theirs_ref = bf16[8,216,128]{2,1,0:T(8,128)(2,1)S(1)} collective-permute-done((bf16[8,216,128]{2,1,0:T(8,128)(2,1)S(1)}, bf16[8,216,128]{2,1,0:T(8,128)(2,1)S(1)}, u32[]{:S(2)}, u32[]{:S(2)}) %collective-permute-start.17) | collective-permute-done | bytes 442400 | tf_op jit(solution)/shard_map/ppermute | solution.py:510
  50.5 0.1 merge.1
  50.6 2.4 %collective-permute-start.18 = (bf16[216,128]{1,0:T(8,128)(2,1)S(1)}, bf16[216,128]{1,0:T(8,128)(2,1)S(1)}, u32[]{:S(2)}, u32[]{:S(2)}) collective-permute-start(bf16[216,128]{1,0:T(8,128)(2,1)S(1)} %get-tuple-element.85), channel_id=1, source_target_pairs={{0,2},{1,3},{2,0},{3,1},{4,6},{5,7},{6,4},{7,5},{8,10},{9,11},{10,... | collective-permute-start | bytes 165896 | tf_op jit(solution)/shard_map/ppermute | solution.py:421
  53.0 0.3 collective-permute-start.19
  53.3 1.2 %collective-permute-start.20 = (bf16[216,128]{1,0:T(8,128)(2,1)S(1)}, bf16[216,128]{1,0:T(8,128)(2,1)S(1)}, u32[]{:S(2)}, u32[]{:S(2)}) collective-permute-start(bf16[216,128]{1,0:T(8,128)(2,1)S(1)} %get-tuple-element.87), channel_id=1, source_target_pairs={{0,6},{1,7},{2,4},{3,5},{4,2},{5,3},{6,0},{7,1},{8,14},{9,15},{10,... | collective-permute-start | bytes 165896 | tf_op jit(solution)/shard_map/ppermute | solution.py:421
  54.5 2.7 %collective-permute-start.21 = (bf16[216,128]{1,0:T(8,128)(2,1)S(1)}, bf16[216,128]{1,0:T(8,128)(2,1)S(1)}, u32[]{:S(2)}, u32[]{:S(2)}) collective-permute-start(bf16[216,128]{1,0:T(8,128)(2,1)S(1)} %get-tuple-element.88), channel_id=1, source_target_pairs={{0,8},{1,9},{2,10},{3,11},{4,12},{5,13},{6,14},{7,15},{8,0},{9,1},... | collective-permute-start | bytes 165896 | tf_op jit(solution)/shard_map/ppermute | solution.py:421
  57.3 1.6 %collective-permute-start.22 = (bf16[216,128]{1,0:T(8,128)(2,1)S(1)}, bf16[216,128]{1,0:T(8,128)(2,1)S(1)}, u32[]{:S(2)}, u32[]{:S(2)}) collective-permute-start(bf16[216,128]{1,0:T(8,128)(2,1)S(1)} %get-tuple-element.89), channel_id=1, source_target_pairs={{0,10},{1,11},{2,8},{3,9},{4,14},{5,15},{6,12},{7,13},{8,2},{9,3},... | collective-permute-start | bytes 165896 | tf_op jit(solution)/shard_map/ppermute | solution.py:421
  58.8 0.0 collective-permute-done.18.refs_1_
  58.8 2.4 %collective-permute-start.23 = (bf16[216,128]{1,0:T(8,128)(2,1)S(1)}, bf16[216,128]{1,0:T(8,128)(2,1)S(1)}, u32[]{:S(2)}, u32[]{:S(2)}) collective-permute-start(bf16[216,128]{1,0:T(8,128)(2,1)S(1)} %get-tuple-element.90), channel_id=1, source_target_pairs={{0,12},{1,13},{2,14},{3,15},{4,8},{5,9},{6,10},{7,11},{8,4},{9,5},... | collective-permute-start | bytes 165896 | tf_op jit(solution)/shard_map/ppermute | solution.py:421
  61.2 0.0 collective-permute-done.19.refs_2_
  61.2 1.4 %collective-permute-start.24 = (bf16[216,128]{1,0:T(8,128)(2,1)S(1)}, bf16[216,128]{1,0:T(8,128)(2,1)S(1)}, u32[]{:S(2)}, u32[]{:S(2)}) collective-permute-start(bf16[216,128]{1,0:T(8,128)(2,1)S(1)} %get-tuple-element.91), channel_id=1, source_target_pairs={{0,14},{1,15},{2,12},{3,13},{4,10},{5,11},{6,8},{7,9},{8,6},{9,7},... | collective-permute-start | bytes 165896 | tf_op jit(solution)/shard_map/ppermute | solution.py:421
  62.6 0.0 collective-permute-done.20.refs_3_
  62.6 0.0 collective-permute-done.21.refs_4_
  62.6 4.0 %collective-permute-done.22.refs_5_ = bf16[216,128]{1,0:T(8,128)(2,1)S(1)} collective-permute-done((bf16[216,128]{1,0:T(8,128)(2,1)S(1)}, bf16[216,128]{1,0:T(8,128)(2,1)S(1)}, u32[]{:S(2)}, u32[]{:S(2)}) %collective-permute-start.22) | collective-permute-done | bytes 55328 | tf_op jit(solution)/shard_map/ppermute | solution.py:421
  66.7 0.0 collective-permute-done.23.refs_6_
  66.7 1.5 %collective-permute-done.24.refs_7_ = bf16[216,128]{1,0:T(8,128)(2,1)S(1)} collective-permute-done((bf16[216,128]{1,0:T(8,128)(2,1)S(1)}, bf16[216,128]{1,0:T(8,128)(2,1)S(1)}, u32[]{:S(2)}, u32[]{:S(2)}) %collective-permute-start.24) | collective-permute-done | bytes 55328 | tf_op jit(solution)/shard_map/ppermute | solution.py:421
  68.2 0.0 copy-done.2
  68.2 0.0 copy-done.4
  68.2 0.8 %finish.1 = (f32[1,128,128]{2,1,0:T(8,128)}, f32[1,64,128]{2,1,0:T(8,128)}, f32[1,128]{1,0:T(1,128)}, f32[1,16,128]{2,1,0:T(8,128)}) custom-call(bf16[216,128]{1,0:T(8,128)(2,1)S(1)} %get-tuple-element.84.refs_0_, bf16[216,128]{1,0:T(8,128)(2,1)S(1)} %collective-permute-done.18.refs_1_, bf16[216,128]{1,0:T(8,128)(2,1)S(1)} %collective-permute-done.19.refs_2_, ...), custom_call_target="tpu_custom_call" | custom-call | tf_op jit(solution)/shard_map/finish/pallas_call | solution.py:517
  (2 shorter events, 0.0 us)
Async XLA Ops:
  0.6 67.5 %copy-start.2 = (bf16[1,128,128]{2,1,0:T(8,128)(2,1)S(1)}, bf16[1,128,128]{2,1,0:T(8,128)(2,1)}, u32[]{:S(2)}) copy-start(bf16[1,128,128]{2,1,0:T(8,128)(2,1)} %refs_9_.1) | copy-start | bytes 98308
  0.6 67.5 %copy-start.4 = (bf16[1,16,128]{2,1,0:T(8,128)(2,1)S(1)}, bf16[1,16,128]{2,1,0:T(8,128)(2,1)}, u32[]{:S(2)}) copy-start(bf16[1,16,128]{2,1,0:T(8,128)(2,1)} %refs_8_.1) | copy-start | bytes 12292
  2.9 8.9 %collective-permute-start = (bf16[256,128]{1,0:T(8,128)(2,1)}, bf16[256,128]{1,0:T(8,128)(2,1)S(1)}, u32[]{:S(2)}, u32[]{:S(2)}) collective-permute-start(bf16[256,128]{1,0:T(8,128)(2,1)} %get-tuple-element.50), channel_id=1, source_target_pairs={{0,2},{1,3},{2,0},{3,1},{4,6},{5,7},{6,4},{7,5},{8,10},{9,11},{10,... | collective-permute-start | bytes 196616 | tf_op jit(solution)/shard_map/ppermute | solution.py:421
  5.9 9.5 %collective-permute-start.1 = (bf16[256,128]{1,0:T(8,128)(2,1)}, bf16[256,128]{1,0:T(8,128)(2,1)S(1)}, u32[]{:S(2)}, u32[]{:S(2)}) collective-permute-start(bf16[256,128]{1,0:T(8,128)(2,1)} %get-tuple-element.59), channel_id=1, source_target_pairs={{0,4},{1,5},{2,6},{3,7},{4,0},{5,1},{6,2},{7,3},{8,12},{9,13},{10,... | collective-permute-start | bytes 196616 | tf_op jit(solution)/shard_map/ppermute | solution.py:421
  7.4 7.9 %collective-permute-start.2 = (bf16[256,128]{1,0:T(8,128)(2,1)}, bf16[256,128]{1,0:T(8,128)(2,1)S(1)}, u32[]{:S(2)}, u32[]{:S(2)}) collective-permute-start(bf16[256,128]{1,0:T(8,128)(2,1)} %get-tuple-element.60), channel_id=1, source_target_pairs={{0,6},{1,7},{2,4},{3,5},{4,2},{5,3},{6,0},{7,1},{8,14},{9,15},{10,... | collective-permute-start | bytes 196616 | tf_op jit(solution)/shard_map/ppermute | solution.py:421
  7.5 8.0 %collective-permute-start.3 = (bf16[256,128]{1,0:T(8,128)(2,1)}, bf16[256,128]{1,0:T(8,128)(2,1)S(1)}, u32[]{:S(2)}, u32[]{:S(2)}) collective-permute-start(bf16[256,128]{1,0:T(8,128)(2,1)} %get-tuple-element.61), channel_id=1, source_target_pairs={{0,8},{1,9},{2,10},{3,11},{4,12},{5,13},{6,14},{7,15},{8,0},{9,1},... | collective-permute-start | bytes 196616 | tf_op jit(solution)/shard_map/ppermute | solution.py:421
  10.5 10.4 %collective-permute-start.4 = (bf16[256,128]{1,0:T(8,128)(2,1)}, bf16[256,128]{1,0:T(8,128)(2,1)S(1)}, u32[]{:S(2)}, u32[]{:S(2)}) collective-permute-start(bf16[256,128]{1,0:T(8,128)(2,1)} %get-tuple-element.62), channel_id=1, source_target_pairs={{0,10},{1,11},{2,8},{3,9},{4,14},{5,15},{6,12},{7,13},{8,2},{9,3},... | collective-permute-start | bytes 196616 | tf_op jit(solution)/shard_map/ppermute | solution.py:421
  11.7 12.2 %collective-permute-start.5 = (bf16[256,128]{1,0:T(8,128)(2,1)}, bf16[256,128]{1,0:T(8,128)(2,1)S(1)}, u32[]{:S(2)}, u32[]{:S(2)}) collective-permute-start(bf16[256,128]{1,0:T(8,128)(2,1)} %get-tuple-element.63), channel_id=1, source_target_pairs={{0,12},{1,13},{2,14},{3,15},{4,8},{5,9},{6,10},{7,11},{8,4},{9,5},... | collective-permute-start | bytes 196616 | tf_op jit(solution)/shard_map/ppermute | solution.py:421
  15.3 9.2 %collective-permute-start.6 = (bf16[256,128]{1,0:T(8,128)(2,1)}, bf16[256,128]{1,0:T(8,128)(2,1)S(1)}, u32[]{:S(2)}, u32[]{:S(2)}) collective-permute-start(bf16[256,128]{1,0:T(8,128)(2,1)} %get-tuple-element.64), channel_id=1, source_target_pairs={{0,14},{1,15},{2,12},{3,13},{4,10},{5,11},{6,8},{7,9},{8,6},{9,7},... | collective-permute-start | bytes 196616 | tf_op jit(solution)/shard_map/ppermute | solution.py:421
  15.4 9.2 %collective-permute-start.9 = (bf16[256,128]{1,0:T(8,128)(2,1)S(1)}, bf16[256,128]{1,0:T(8,128)(2,1)S(1)}, u32[]{:S(2)}, u32[]{:S(2)}) collective-permute-start(bf16[256,128]{1,0:T(8,128)(2,1)S(1)} %collective-permute-done.1.refs_2_), channel_id=1, source_target_pairs={{0,1},{1,0},{2,3},{3,2},{4,5},{5,4},{6,7},{7,6},{8,9},{9,8},{10,11... | collective-permute-start | bytes 196616 | tf_op jit(solution)/shard_map/ppermute | solution.py:455
  15.4 9.6 %collective-permute-start.10 = (bf16[256,128]{1,0:T(8,128)(2,1)S(1)}, bf16[256,128]{1,0:T(8,128)(2,1)S(1)}, u32[]{:S(2)}, u32[]{:S(2)}) collective-permute-start(bf16[256,128]{1,0:T(8,128)(2,1)S(1)} %collective-permute-done.2.refs_3_), channel_id=1, source_target_pairs={{0,1},{1,0},{2,3},{3,2},{4,5},{5,4},{6,7},{7,6},{8,9},{9,8},{10,11... | collective-permute-start | bytes 196616 | tf_op jit(solution)/shard_map/ppermute | solution.py:455
  20.9 4.3 %collective-permute-start.11 = (bf16[256,128]{1,0:T(8,128)(2,1)S(1)}, bf16[256,128]{1,0:T(8,128)(2,1)S(1)}, u32[]{:S(2)}, u32[]{:S(2)}) collective-permute-start(bf16[256,128]{1,0:T(8,128)(2,1)S(1)} %collective-permute-done.3.refs_4_), channel_id=1, source_target_pairs={{0,1},{1,0},{2,3},{3,2},{4,5},{5,4},{6,7},{7,6},{8,9},{9,8},{10,11... | collective-permute-start | bytes 196616 | tf_op jit(solution)/shard_map/ppermute | solution.py:455
  20.9 1.0 %copy-start = (bf16[576,384]{1,0:T(8,128)(2,1)S(1)}, bf16[576,384]{1,0:T(8,128)(2,1)}, u32[]{:S(2)}) copy-start(bf16[576,384]{1,0:T(8,128)(2,1)} %decoder_ref) | copy-start | bytes 1327108
  21.9 0.9 %copy-start.1 = (bf16[256,384]{1,0:T(8,128)(2,1)S(1)}, bf16[256,384]{1,0:T(8,128)(2,1)}, u32[]{:S(2)}) copy-start(bf16[256,384]{1,0:T(8,128)(2,1)} %target_ref) | copy-start | bytes 589828
  22.8 0.8 %copy-start.3 = (bf16[256,128]{1,0:T(8,128)(2,1)S(1)}, bf16[256,128]{1,0:T(8,128)(2,1)}, u32[]{:S(2)}) copy-start(bf16[256,128]{1,0:T(8,128)(2,1)} %get-tuple-element.54.block_ref) | copy-start | bytes 196612
  23.9 2.4 %collective-permute-start.7 = (bf16[256,128]{1,0:T(8,128)(2,1)S(1)}, bf16[256,128]{1,0:T(8,128)(2,1)S(1)}, u32[]{:S(2)}, u32[]{:S(2)}) collective-permute-start(bf16[256,128]{1,0:T(8,128)(2,1)S(1)} %get-tuple-element.57.refs_0_), channel_id=1, source_target_pairs={{0,1},{1,0},{2,3},{3,2},{4,5},{5,4},{6,7},{7,6},{8,9},{9,8},{10,11... | collective-permute-start | bytes 196616 | tf_op jit(solution)/shard_map/ppermute | solution.py:455
  24.5 1.3 %collective-permute-start.12 = (bf16[256,128]{1,0:T(8,128)(2,1)S(1)}, bf16[256,128]{1,0:T(8,128)(2,1)S(1)}, u32[]{:S(2)}, u32[]{:S(2)}) collective-permute-start(bf16[256,128]{1,0:T(8,128)(2,1)S(1)} %collective-permute-done.4.refs_5_), channel_id=1, source_target_pairs={{0,1},{1,0},{2,3},{3,2},{4,5},{5,4},{6,7},{7,6},{8,9},{9,8},{10,11... | collective-permute-start | bytes 196616 | tf_op jit(solution)/shard_map/ppermute | solution.py:455
  24.6 1.3 %collective-permute-start.13 = (bf16[256,128]{1,0:T(8,128)(2,1)S(1)}, bf16[256,128]{1,0:T(8,128)(2,1)S(1)}, u32[]{:S(2)}, u32[]{:S(2)}) collective-permute-start(bf16[256,128]{1,0:T(8,128)(2,1)S(1)} %collective-permute-done.5.refs_6_), channel_id=1, source_target_pairs={{0,1},{1,0},{2,3},{3,2},{4,5},{5,4},{6,7},{7,6},{8,9},{9,8},{10,11... | collective-permute-start | bytes 196616 | tf_op jit(solution)/shard_map/ppermute | solution.py:455
  25.0 1.3 %collective-permute-start.14 = (bf16[256,128]{1,0:T(8,128)(2,1)S(1)}, bf16[256,128]{1,0:T(8,128)(2,1)S(1)}, u32[]{:S(2)}, u32[]{:S(2)}) collective-permute-start(bf16[256,128]{1,0:T(8,128)(2,1)S(1)} %collective-permute-done.6.refs_7_), channel_id=1, source_target_pairs={{0,1},{1,0},{2,3},{3,2},{4,5},{5,4},{6,7},{7,6},{8,9},{9,8},{10,11... | collective-permute-start | bytes 196616 | tf_op jit(solution)/shard_map/ppermute | solution.py:455
  25.1 1.3 %collective-permute-start.8 = (bf16[256,128]{1,0:T(8,128)(2,1)S(1)}, bf16[256,128]{1,0:T(8,128)(2,1)S(1)}, u32[]{:S(2)}, u32[]{:S(2)}) collective-permute-start(bf16[256,128]{1,0:T(8,128)(2,1)S(1)} %collective-permute-done.refs_1_), channel_id=1, source_target_pairs={{0,1},{1,0},{2,3},{3,2},{4,5},{5,4},{6,7},{7,6},{8,9},{9,8},{10,11... | collective-permute-start | bytes 196616 | tf_op jit(solution)/shard_map/ppermute | solution.py:455
  33.3 1.4 %collective-permute-start.15 = (bf16[256,256]{1,0:T(8,128)(2,1)S(1)}, bf16[256,256]{1,0:T(8,128)(2,1)S(1)}, u32[]{:S(2)}, u32[]{:S(2)}) collective-permute-start(bf16[256,256]{1,0:T(8,128)(2,1)S(1)} %get-tuple-element.67), channel_id=1, source_target_pairs={{0,1},{1,0},{2,3},{3,2},{4,5},{5,4},{6,7},{7,6},{8,9},{9,8},{10,11... | collective-permute-start | bytes 393224 | tf_op jit(solution)/shard_map/ppermute | solution.py:489
  33.7 1.0 %collective-permute-start.16 = (bf16[256,256]{1,0:T(8,128)(2,1)S(1)}, bf16[256,256]{1,0:T(8,128)(2,1)S(1)}, u32[]{:S(2)}, u32[]{:S(2)}) collective-permute-start(bf16[256,256]{1,0:T(8,128)(2,1)S(1)} %get-tuple-element.68), channel_id=1, source_target_pairs={{1,2},{3,4},{5,6},{7,8},{9,10},{11,12},{13,14},{2,1},{4,3},{6,5},{... | collective-permute-start | bytes 393224 | tf_op jit(solution)/shard_map/ppermute | solution.py:490
  43.6 6.9 %collective-permute-start.17 = (bf16[8,216,128]{2,1,0:T(8,128)(2,1)S(1)}, bf16[8,216,128]{2,1,0:T(8,128)(2,1)S(1)}, u32[]{:S(2)}, u32[]{:S(2)}) collective-permute-start(bf16[8,216,128]{2,1,0:T(8,128)(2,1)S(1)} %get-tuple-element.83), channel_id=1, source_target_pairs={{0,1},{1,0},{2,3},{3,2},{4,5},{5,4},{6,7},{7,6},{8,9},{9,8},{10,11... | collective-permute-start | bytes 1327112 | tf_op jit(solution)/shard_map/ppermute | solution.py:510
  50.6 8.3 %collective-permute-start.18 = (bf16[216,128]{1,0:T(8,128)(2,1)S(1)}, bf16[216,128]{1,0:T(8,128)(2,1)S(1)}, u32[]{:S(2)}, u32[]{:S(2)}) collective-permute-start(bf16[216,128]{1,0:T(8,128)(2,1)S(1)} %get-tuple-element.85), channel_id=1, source_target_pairs={{0,2},{1,3},{2,0},{3,1},{4,6},{5,7},{6,4},{7,5},{8,10},{9,11},{10,... | collective-permute-start | bytes 165896 | tf_op jit(solution)/shard_map/ppermute | solution.py:421
  53.0 8.2 %collective-permute-start.19 = (bf16[216,128]{1,0:T(8,128)(2,1)S(1)}, bf16[216,128]{1,0:T(8,128)(2,1)S(1)}, u32[]{:S(2)}, u32[]{:S(2)}) collective-permute-start(bf16[216,128]{1,0:T(8,128)(2,1)S(1)} %get-tuple-element.86), channel_id=1, source_target_pairs={{0,4},{1,5},{2,6},{3,7},{4,0},{5,1},{6,2},{7,3},{8,12},{9,13},{10,... | collective-permute-start | bytes 165896 | tf_op jit(solution)/shard_map/ppermute | solution.py:421
  53.3 9.3 %collective-permute-start.20 = (bf16[216,128]{1,0:T(8,128)(2,1)S(1)}, bf16[216,128]{1,0:T(8,128)(2,1)S(1)}, u32[]{:S(2)}, u32[]{:S(2)}) collective-permute-start(bf16[216,128]{1,0:T(8,128)(2,1)S(1)} %get-tuple-element.87), channel_id=1, source_target_pairs={{0,6},{1,7},{2,4},{3,5},{4,2},{5,3},{6,0},{7,1},{8,14},{9,15},{10,... | collective-permute-start | bytes 165896 | tf_op jit(solution)/shard_map/ppermute | solution.py:421
  54.5 8.1 %collective-permute-start.21 = (bf16[216,128]{1,0:T(8,128)(2,1)S(1)}, bf16[216,128]{1,0:T(8,128)(2,1)S(1)}, u32[]{:S(2)}, u32[]{:S(2)}) collective-permute-start(bf16[216,128]{1,0:T(8,128)(2,1)S(1)} %get-tuple-element.88), channel_id=1, source_target_pairs={{0,8},{1,9},{2,10},{3,11},{4,12},{5,13},{6,14},{7,15},{8,0},{9,1},... | collective-permute-start | bytes 165896 | tf_op jit(solution)/shard_map/ppermute | solution.py:421
  57.3 9.4 %collective-permute-start.22 = (bf16[216,128]{1,0:T(8,128)(2,1)S(1)}, bf16[216,128]{1,0:T(8,128)(2,1)S(1)}, u32[]{:S(2)}, u32[]{:S(2)}) collective-permute-start(bf16[216,128]{1,0:T(8,128)(2,1)S(1)} %get-tuple-element.89), channel_id=1, source_target_pairs={{0,10},{1,11},{2,8},{3,9},{4,14},{5,15},{6,12},{7,13},{8,2},{9,3},... | collective-permute-start | bytes 165896 | tf_op jit(solution)/shard_map/ppermute | solution.py:421
  58.8 7.8 %collective-permute-start.23 = (bf16[216,128]{1,0:T(8,128)(2,1)S(1)}, bf16[216,128]{1,0:T(8,128)(2,1)S(1)}, u32[]{:S(2)}, u32[]{:S(2)}) collective-permute-start(bf16[216,128]{1,0:T(8,128)(2,1)S(1)} %get-tuple-element.90), channel_id=1, source_target_pairs={{0,12},{1,13},{2,14},{3,15},{4,8},{5,9},{6,10},{7,11},{8,4},{9,5},... | collective-permute-start | bytes 165896 | tf_op jit(solution)/shard_map/ppermute | solution.py:421
  61.2 7.0 %collective-permute-start.24 = (bf16[216,128]{1,0:T(8,128)(2,1)S(1)}, bf16[216,128]{1,0:T(8,128)(2,1)S(1)}, u32[]{:S(2)}, u32[]{:S(2)}) collective-permute-start(bf16[216,128]{1,0:T(8,128)(2,1)S(1)} %get-tuple-element.91), channel_id=1, source_target_pairs={{0,14},{1,15},{2,12},{3,13},{4,10},{5,11},{6,8},{7,9},{8,6},{9,7},... | collective-permute-start | bytes 165896 | tf_op jit(solution)/shard_map/ppermute | solution.py:421

commit v3 on v2

--- a/solution.py
+++ b/solution.py
@@ -50,8 +50,8 @@
 
 
 def pack_kernel(half, group, room, *refs):
-    hbm, blocks, held, sems = refs[:8], refs[8 : 8 + half], refs[8 + half : 16 + half], refs[16 + half]
-    meta_ref, codes_ref = refs[17 + half :]
+    hbm, (near_ref, far_ref), held, sems = refs[:8], refs[8:10], refs[10:18], refs[18]
+    meta_ref, codes_ref = refs[19:]
     me = lax.axis_index("region")
     mine = lax.shift_right_logical(me, 1)
     copies = [pltpu.make_async_copy(hbm[i], held[i], sems.at[i]) for i in range(8)]
@@ -83,14 +83,29 @@
     wh_t = wh_ref[0].astype(F32).T.astype(BF16)
     density = wd_ref[...].astype(F32)
     first = iota((16, LANES), 0) == 0
-    for k, out_ref in enumerate(blocks):
+
+    def rays_for(k):
         chip = jnp.bitwise_xor(mine, k)
-        out_ref[0:WF_AT] = wh_t
-        out_ref[WF_AT:SAMPLE_AT] = wf_ref[0]
-        out_ref[SAMPLE_AT:META_AT] = samp_ref[0]
         here = pltpu.roll(meta, (rays - chip * 2 * group) & (rays - 1), 1)[:, :LANES]
-        out_ref[META_AT:RAYS_AT] = jnp.where(first, density, here).astype(BF16)
-        out_ref[RAYS_AT : RAYS_AT + room] = codes_ref[pl.ds(pl.multiple_of(chip * room, 16), room), :]
+        codes = codes_ref[pl.ds(pl.multiple_of(chip * room, 16), room), :]
+        return jnp.where(first, density, here).astype(BF16), codes
+
+    for ref in [near_ref.at[k] for k in range(half // 2)] + [far_ref]:
+        ref[0:WF_AT] = wh_t
+        ref[WF_AT:SAMPLE_AT] = wf_ref[0]
+        ref[SAMPLE_AT:META_AT] = samp_ref[0]
+    for k in range(half // 2):
+        near_ref[k, META_AT:RAYS_AT], near_ref[k, RAYS_AT:] = rays_for(k)
+        at = META_AT + k * (16 + room)
+        far_ref[at : at + 16], far_ref[at + 16 : at + 16 + room] = rays_for(k + half // 2)
+
+
+def relay_kernel(near_ref, far_ref, *outs):
+    for k, out in enumerate(outs):
+        out[0] = near_ref[k]
+        out[1, 0:META_AT] = far_ref[0:META_AT]
+        rows = near_ref.shape[1] - META_AT
+        out[1, META_AT:] = far_ref[META_AT + k * rows : META_AT + (k + 1) * rows]
 
 
 def bits_of(row, regions):
@@ -113,11 +128,13 @@
 
 def forward_kernel(half, group, room, *refs):
     regions = 2 * half
-    blocks, target_ref = refs[:regions], refs[regions]
+    quarter = half // 2
+    received, target_ref = refs[:half], refs[half]
+    blocks = [received[c * quarter + k].at[side] for c in range(2) for side in range(2) for k in range(quarter)]
     (
         image_ref, halo_in_ref, halo_cr_ref, h_ref, wd_ref, att_hw_ref, wide_hw_ref, weight_ref, pass_ref, slope_ref, att_ref, rel_ref, codes_ref, wf_out,
         meta_ref, plain_ref, table_ref, proj_ref, a_ref, picked_ref, row_ref, ahead_ref,
-    ) = refs[regions + 1 :]
+    ) = refs[half + 1 :]
     rays = codes_ref.shape[1]
     segs = rel_ref.shape[0]
     samples = weight_ref.shape[1]
@@ -371,8 +388,7 @@
         out[to, G2_AT:PART_ROWS] = tail_ref[r].astype(BF16)
 
 
-def flip_kernel(target_ref, decoder_ref, block_ref, target_out, decoder_out, same_out, block_out):
-    block_out[...] = block_ref[...]
+def flip_kernel(target_ref, decoder_ref, target_out, decoder_out, same_out):
     same_out[...] = decoder_ref[...]
     target_out[...] = target_ref[...].astype(F32).T.astype(BF16)
     decoder_out[...] = decoder_ref[...].astype(F32).T.astype(BF16)
@@ -380,14 +396,22 @@
 
 def merge_kernel(mine_ref, theirs_ref, *outs):
     for k, out in enumerate(outs):
-        out[...] = (mine_ref[k].astype(F32) + theirs_ref[k].astype(F32)).astype(BF16)
-
-
-def finish_kernel(*refs):
-    parts, (samp_ref, wh_ref, hid_ref, feat_ref, dens_ref, code_ref) = refs[:-6], refs[-6:]
-    total = parts[0][...].astype(F32)
-    for part in parts[1:]:
-        total = total + part[...].astype(F32)
+        for side in range(2):
+            at = side * len(outs) + k
+            out[side] = (mine_ref[at].astype(F32) + theirs_ref[at].astype(F32)).astype(BF16)
+
+
+def reduce_kernel(*refs):
+    parts, (keep_ref, send_ref) = refs[:-2], refs[-2:]
+    for side, out in enumerate((keep_ref, send_ref)):
+        total = parts[0][side].astype(F32)
+        for part in parts[1:]:
+            total = total + part[side].astype(F32)
+        out[...] = total.astype(out.dtype)
+
+
+def finish_kernel(keep_ref, part_ref, samp_ref, wh_ref, hid_ref, feat_ref, dens_ref, code_ref):
+    total = keep_ref[...] + part_ref[...].astype(F32)
     high, low = split(total[G2_AT:DG_AT])
     samples = samp_ref[0]
     wh = wh_ref[0]
@@ -416,18 +440,25 @@
     def shape(*dims, kind=F32):
         return jax.ShapeDtypeStruct(dims, kind)
 
-    def to_chips(blocks):
-        return [blocks[0]] + [
-            lax.ppermute(blocks[k], "region", [(i, i ^ (2 * k)) for i in range(regions)]) for k in range(1, half)
-        ]
+    quarter = half // 2
+    pack_rows = RAYS_AT + room
+
+    def to_chip(block, k):
+        return lax.ppermute(block, "region", [(i, i ^ (2 * k)) for i in range(regions)])
+
+    def to_half(blocks):
+        return [blocks[0]] + [to_chip(blocks[k], k) for k in range(1, quarter)]
 
     pack_args = (
         pixel_of_ray.reshape(1, rays), seg_region.T, seg_count.T,
         ray_code, sample_code, w_hidden, w_feat.swapaxes(1, 2), w_density,
     )
-    outs = pl.pallas_call(
+    near, far = pl.pallas_call(
         functools.partial(pack_kernel, half, group, room),
-        out_shape=[shape(RAYS_AT + room, LANES, kind=BF16)] * half,
+        out_shape=(
+            shape(quarter, pack_rows, LANES, kind=BF16),
+            shape(META_AT + quarter * (16 + room), LANES, kind=BF16),
+        ),
         in_specs=[pl.BlockSpec(memory_space=pltpu.HBM)] * 8,
         scratch_shapes=[pltpu.VMEM(x.shape, x.dtype) for x in pack_args]
         + [
@@ -438,20 +469,26 @@
         compiler_params=grant(60),
         name="pack",
     )(*pack_args)
-    target, decoder, own_block = lax.optimization_barrier((target, decoder, outs[0]))
-    target_t, decoder_t, decoder, own_block = pl.pallas_call(
+    far = to_chip(far, quarter)
+    flipped = pl.pallas_call(
         flip_kernel,
         out_shape=(
             shape(dino_width, rays, kind=BF16),
             shape(*decoder.shape[::-1], kind=BF16),
             shape(*decoder.shape, kind=BF16),
-            shape(*own_block.shape, kind=BF16),
         ),
         compiler_params=grant(8),
         name="flip",
-    )(target, decoder, own_block)
-    blocks = to_chips([own_block] + list(outs[1:]))
-    blocks[1], (blocks[0], target_t) = lax.optimization_barrier((blocks[1], (blocks[0], target_t)))
+    )(target, decoder)
+    far, (target_t, decoder_t, decoder) = lax.optimization_barrier((far, flipped))
+    blocks = to_half(
+        pl.pallas_call(
+            relay_kernel,
+            out_shape=[shape(2, pack_rows, LANES, kind=BF16)] * quarter,
+            compiler_params=grant(8 + regions / 8),
+            name="relay",
+        )(near, far)
+    )
     blocks = blocks + [lax.ppermute(block, "region", inner) for block in blocks]
 
     image, halo_in, halo_cr, *kept = pl.pallas_call(
@@ -508,12 +545,18 @@
     )(image, halo_in, halo_cr, target_t, decoder, decoder_t, *kept)
 
     theirs = lax.ppermute(other, "region", inner)
-    chip = pl.pallas_call(
+    parts = pl.pallas_call(
         merge_kernel,
-        out_shape=[shape(PART_ROWS, LANES, kind=BF16)] * half,
+        out_shape=[shape(2, PART_ROWS, LANES, kind=BF16)] * quarter,
         compiler_params=grant(8 + regions / 8),
         name="merge",
     )(mine, theirs)
+    keep, send = pl.pallas_call(
+        reduce_kernel,
+        out_shape=(shape(PART_ROWS, LANES), shape(PART_ROWS, LANES, kind=BF16)),
+        compiler_params=grant(8 + regions / 8),
+        name="reduce",
+    )(*to_half(parts))
     hid_grad, feat_grad, dens_grad, code_grad = pl.pallas_call(
         finish_kernel,
         out_shape=(
@@ -524,7 +567,7 @@
         ),
         compiler_params=grant(8 + regions / 8),
         name="finish",
-    )(*to_chips(chip), sample_code, w_hidden)
+    )(keep, to_chip(send, quarter), sample_code, w_hidden)
     return hid_grad, feat_grad.swapaxes(1, 2), dens_grad, code_grad
 
 

time: 69.3 us -> 64.6 us (0.932)
  starting transfers between devices: 33.2 us -> 21.3 us
  waiting for transfers between devices: 13.1 us -> 20.2 us
    ppermute x14 -> x8, starting transfers between devices: 24.6 us -> 14.9 us  [to_chip(): lax.ppermute(block, 'region', [(i, i ^ 2 * k) for i in range(regions)])]
    ppermute x14 -> x8, waiting for transfers between devices: 10.5 us -> 16.9 us  [to_chip(): lax.ppermute(block, 'region', [(i, i ^ 2 * k) for i in range(regions)])]
    ppermute x8 -> x4, starting transfers between devices: 2.12 us -> 0.01 us  [local(): blocks = blocks + [lax.ppermute(block, 'region', inner) for block in blocks]]
  transfers between devices with their start and end apart: 25 -> 15, of which waited for: 9 -> 11; matrix products, arithmetic and copies ran while one was open for 0% -> 0% of each run, Pallas kernels for 0% -> 0%
where the time goes in v3:
time: 64.6 us; the launch traced here: 64.3 us
  starting transfers between devices  21.3 us (33%)
  waiting for transfers between devices  20.2 us (31%)
  Pallas kernels  19.2 us (30%)
  local copies, waits for them, and re-layouts  2.9 us (4%)
  between operations  0.72 us (1%)
    ppermute x8, waiting for transfers between devices, to_chip(): lax.ppermute(block, 'region', [(i, i ^ 2 * k) for i in range(regions)])  16.9 us
    ppermute x8, starting transfers between devices, to_chip(): lax.ppermute(block, 'region', [(i, i ^ 2 * k) for i in range(regions)])  14.9 us
    pallas_call x1, Pallas kernels, local(): pl.pallas_call(functools.partial(backward_kernel, half), out_shape=(part,...  8.84 us
    pallas_call x1, Pallas kernels, local(): pl.pallas_call(functools.partial(forward_kernel, half, group, room), out_...  6.83 us
    ppermute x1, starting transfers between devices, local(): theirs = lax.ppermute(other, 'region', inner)  5.5 us
    unnamed x10, local copies, waits for them, and re-layouts  2.9 us
    pallas_call x1, Pallas kernels, local(): pl.pallas_call(functools.partial(pack_kernel, half, group, room), out_sha...  2.16 us
    ppermute x1, waiting for transfers between devices, local(): theirs = lax.ppermute(other, 'region', inner)  1.42 us
  transfers between devices with their start and end apart: 15, of which 11 were waited for; matrix products, arithmetic and copies ran while one was open for 0% of the time, Pallas kernels for 0%

profile of v3, /device:TPU:0, one launch (start us, length us, event | category | flops | bytes accessed | tf_op | source)
XLA Modules:
  0.0 64.3 jit_solution(12716578210895154539)
XLA Ops:
  0.6 0.0 copy-start.3
  0.6 0.0 copy-start.4
  0.7 2.2 %pack.1 = (bf16[4,256,128]{2,1,0:T(8,128)(2,1)}, bf16[400,128]{1,0:T(8,128)(2,1)}) custom-call(s32[1,256]{1,0:T(1,128)} %bitcast.8, s32[4,256]{1,0:T(4,128)} %bitcast.6, s32[4,256]{1,0:T(4,128)} %bitcast.7, bf16[256,128]{1,0:T(8,128)(2,1)} %refs_3_.1, bf16[1,16,128]{2,1,0:T(8,128)(2,1)} %samp_ref.1, bf16[1,128,128]{2,1,0:T(8,128)(2,1)} %wh_ref.1, ...), custom_call_target="tpu_custom_call" | custom-call | tf_op jit(solution)/shard_map/pack/pallas_call | solution.py:456
  2.8 4.1 %collective-permute-start = (bf16[400,128]{1,0:T(8,128)(2,1)}, bf16[400,128]{1,0:T(8,128)(2,1)S(1)}, u32[]{:S(2)}, u32[]{:S(2)}) collective-permute-start(bf16[400,128]{1,0:T(8,128)(2,1)} %get-tuple-element.44), channel_id=1, source_target_pairs={{0,8},{1,9},{2,10},{3,11},{4,12},{5,13},{6,14},{7,15},{8,0},{9,1},... | collective-permute-start | bytes 307208 | tf_op jit(solution)/shard_map/ppermute | solution.py:447
  6.9 0.0 copy-start
  6.9 1.0 %copy-done = bf16[576,384]{1,0:T(8,128)(2,1)S(1)} copy-done((bf16[576,384]{1,0:T(8,128)(2,1)S(1)}, bf16[576,384]{1,0:T(8,128)(2,1)}, u32[]{:S(2)}) %copy-start) | copy-done | bytes 442392
  7.9 0.0 copy-start.2
  7.9 0.9 %copy-done.2 = bf16[256,384]{1,0:T(8,128)(2,1)S(1)} copy-done((bf16[256,384]{1,0:T(8,128)(2,1)S(1)}, bf16[256,384]{1,0:T(8,128)(2,1)}, u32[]{:S(2)}) %copy-start.2) | copy-done | bytes 196632
  8.9 0.3 flip.1
  9.1 3.1 %collective-permute-done.far_ref = bf16[400,128]{1,0:T(8,128)(2,1)S(1)} collective-permute-done((bf16[400,128]{1,0:T(8,128)(2,1)}, bf16[400,128]{1,0:T(8,128)(2,1)S(1)}, u32[]{:S(2)}, u32[]{:S(2)}) %collective-permute-start) | collective-permute-done | bytes 102432 | tf_op jit(solution)/shard_map/ppermute | solution.py:447
  12.2 0.0 copy-start.1
  12.2 0.9 %copy-done.1 = bf16[4,256,128]{2,1,0:T(8,128)(2,1)S(1)} copy-done((bf16[4,256,128]{2,1,0:T(8,128)(2,1)S(1)}, bf16[4,256,128]{2,1,0:T(8,128)(2,1)}, u32[]{:S(2)}) %copy-start.1) | copy-done | bytes 262168
  13.2 1.6 %collective-permute-start.1 = (bf16[2,256,128]{2,1,0:T(8,128)(2,1)S(1)}, bf16[2,256,128]{2,1,0:T(8,128)(2,1)S(1)}, u32[]{:S(2)}, u32[]{:S(2)}) collective-permute-start(bf16[2,256,128]{2,1,0:T(8,128)(2,1)S(1)} %get-tuple-element.50), channel_id=1, source_target_pairs={{0,2},{1,3},{2,0},{3,1},{4,6},{5,7},{6,4},{7,5},{8,10},{9,11},{10,... | collective-permute-start | bytes 393224 | tf_op jit(solution)/shard_map/ppermute | solution.py:447
  14.8 0.8 %collective-permute-start.2 = (bf16[2,256,128]{2,1,0:T(8,128)(2,1)S(1)}, bf16[2,256,128]{2,1,0:T(8,128)(2,1)S(1)}, u32[]{:S(2)}, u32[]{:S(2)}) collective-permute-start(bf16[2,256,128]{2,1,0:T(8,128)(2,1)S(1)} %get-tuple-element.51), channel_id=1, source_target_pairs={{0,4},{1,5},{2,6},{3,7},{4,0},{5,1},{6,2},{7,3},{8,12},{9,13},{10,... | collective-permute-start | bytes 393224 | tf_op jit(solution)/shard_map/ppermute | solution.py:447
  15.6 1.2 %collective-permute-start.3 = (bf16[2,256,128]{2,1,0:T(8,128)(2,1)S(1)}, bf16[2,256,128]{2,1,0:T(8,128)(2,1)S(1)}, u32[]{:S(2)}, u32[]{:S(2)}) collective-permute-start(bf16[2,256,128]{2,1,0:T(8,128)(2,1)S(1)} %get-tuple-element.52), channel_id=1, source_target_pairs={{0,6},{1,7},{2,4},{3,5},{4,2},{5,3},{6,0},{7,1},{8,14},{9,15},{10,... | collective-permute-start | bytes 393224 | tf_op jit(solution)/shard_map/ppermute | solution.py:447
  16.8 0.0 collective-permute-start.4
  16.8 1.8 %collective-permute-done.1.refs_1_ = bf16[2,256,128]{2,1,0:T(8,128)(2,1)S(1)} collective-permute-done((bf16[2,256,128]{2,1,0:T(8,128)(2,1)S(1)}, bf16[2,256,128]{2,1,0:T(8,128)(2,1)S(1)}, u32[]{:S(2)}, u32[]{:S(2)}) %collective-permute-start.1) | collective-permute-done | bytes 131104 | tf_op jit(solution)/shard_map/ppermute | solution.py:447
  18.6 0.0 collective-permute-start.5
  18.6 1.8 %collective-permute-done.2.refs_2_ = bf16[2,256,128]{2,1,0:T(8,128)(2,1)S(1)} collective-permute-done((bf16[2,256,128]{2,1,0:T(8,128)(2,1)S(1)}, bf16[2,256,128]{2,1,0:T(8,128)(2,1)S(1)}, u32[]{:S(2)}, u32[]{:S(2)}) %collective-permute-start.2) | collective-permute-done | bytes 131104 | tf_op jit(solution)/shard_map/ppermute | solution.py:447
  20.4 0.0 collective-permute-start.6
  20.4 2.1 %collective-permute-done.3.refs_3_ = bf16[2,256,128]{2,1,0:T(8,128)(2,1)S(1)} collective-permute-done((bf16[2,256,128]{2,1,0:T(8,128)(2,1)S(1)}, bf16[2,256,128]{2,1,0:T(8,128)(2,1)S(1)}, u32[]{:S(2)}, u32[]{:S(2)}) %collective-permute-start.3) | collective-permute-done | bytes 131104 | tf_op jit(solution)/shard_map/ppermute | solution.py:447
  22.5 0.0 collective-permute-start.7
  22.5 0.0 collective-permute-done.4.refs_4_
  22.5 0.0 collective-permute-done.5.refs_5_
  22.5 0.0 collective-permute-done.6.refs_6_
  22.5 1.3 %collective-permute-done.7.refs_7_ = bf16[2,256,128]{2,1,0:T(8,128)(2,1)S(1)} collective-permute-done((bf16[2,256,128]{2,1,0:T(8,128)(2,1)S(1)}, bf16[2,256,128]{2,1,0:T(8,128)(2,1)S(1)}, u32[]{:S(2)}, u32[]{:S(2)}) %collective-permute-start.7) | collective-permute-done | bytes 131104 | tf_op jit(solution)/shard_map/ppermute | solution.py:492
  23.9 6.8 %forward.1 = (bf16[64,256]{1,0:T(8,128)(2,1)S(1)}, bf16[256,256]{1,0:T(8,128)(2,1)S(1)}, bf16[256,256]{1,0:T(8,128)(2,1)S(1)}, f32[8,16,128,128]{3,2,1,0:T(8,128...) custom-call(bf16[2,256,128]{2,1,0:T(8,128)(2,1)S(1)} %get-tuple-elem, ...), custom_call_target="tpu_custom_call" | custom-call | tf_op jit(solution)/shard_map/forward/pallas_call | solution.py:494
  30.7 0.2 collective-permute-start.8
  30.9 0.7 %collective-permute-start.9 = (bf16[256,256]{1,0:T(8,128)(2,1)S(1)}, bf16[256,256]{1,0:T(8,128)(2,1)S(1)}, u32[]{:S(2)}, u32[]{:S(2)}) collective-permute-start(bf16[256,256]{1,0:T(8,128)(2,1)S(1)} %get-tuple-element.56), channel_id=1, source_target_pairs={{1,2},{3,4},{5,6},{7,8},{9,10},{11,12},{13,14},{2,1},{4,3},{6,5},{... | collective-permute-start | bytes 393224 | tf_op jit(solution)/shard_map/ppermute | solution.py:527
  31.6 0.5 collective-permute-done.8.inner_ref
  32.1 0.0 collective-permute-done.9.cross_ref
  32.1 8.8 %backward.1 = (bf16[8,216,128]{2,1,0:T(8,128)(2,1)S(1)}, bf16[8,216,128]{2,1,0:T(8,128)(2,1)S(1)}) custom-call(bf16[64,256]{1,0:T(8,128)(2,1)S(1)} %get-tuple-element.54.own_ref, bf16[256,256]{1,0:T(8,128)(2,1)S(1)} %collective-permute-done.8.inner_ref, bf16[256,256]{1,0:T(8,128)(2,1)S(1)} %collective-permute-done.9.cross_ref, ...), custom_call_target="tpu_custom_call" | custom-call | tf_op jit(solution)/shard_map/backward/pallas_call | solution.py:530
  41.0 5.5 %collective-permute-start.10 = (bf16[8,216,128]{2,1,0:T(8,128)(2,1)S(1)}, bf16[8,216,128]{2,1,0:T(8,128)(2,1)S(1)}, u32[]{:S(2)}, u32[]{:S(2)}) collective-permute-start(bf16[8,216,128]{2,1,0:T(8,128)(2,1)S(1)} %get-tuple-element.71), channel_id=1, source_target_pairs={{0,1},{1,0},{2,3},{3,2},{4,5},{5,4},{6,7},{7,6},{8,9},{9,8},{10,11... | collective-permute-start | bytes 1327112 | tf_op jit(solution)/shard_map/ppermute | solution.py:547
  46.5 1.4 %collective-permute-done.10.theirs_ref = bf16[8,216,128]{2,1,0:T(8,128)(2,1)S(1)} collective-permute-done((bf16[8,216,128]{2,1,0:T(8,128)(2,1)S(1)}, bf16[8,216,128]{2,1,0:T(8,128)(2,1)S(1)}, u32[]{:S(2)}, u32[]{:S(2)}) %collective-permute-start.10) | collective-permute-done | bytes 442400 | tf_op jit(solution)/shard_map/ppermute | solution.py:547
  47.9 0.1 merge.1
  48.0 1.7 %collective-permute-start.11 = (bf16[2,216,128]{2,1,0:T(8,128)(2,1)S(1)}, bf16[2,216,128]{2,1,0:T(8,128)(2,1)S(1)}, u32[]{:S(2)}, u32[]{:S(2)}) collective-permute-start(bf16[2,216,128]{2,1,0:T(8,128)(2,1)S(1)} %get-tuple-element.73), channel_id=1, source_target_pairs={{0,2},{1,3},{2,0},{3,1},{4,6},{5,7},{6,4},{7,5},{8,10},{9,11},{10,... | collective-permute-start | bytes 331784 | tf_op jit(solution)/shard_map/ppermute | solution.py:447
  49.7 1.7 %collective-permute-start.12 = (bf16[2,216,128]{2,1,0:T(8,128)(2,1)S(1)}, bf16[2,216,128]{2,1,0:T(8,128)(2,1)S(1)}, u32[]{:S(2)}, u32[]{:S(2)}) collective-permute-start(bf16[2,216,128]{2,1,0:T(8,128)(2,1)S(1)} %get-tuple-element.74), channel_id=1, source_target_pairs={{0,4},{1,5},{2,6},{3,7},{4,0},{5,1},{6,2},{7,3},{8,12},{9,13},{10,... | collective-permute-start | bytes 331784 | tf_op jit(solution)/shard_map/ppermute | solution.py:447
  51.5 0.5 collective-permute-start.13
  51.9 1.5 %collective-permute-done.11.refs_1_ = bf16[2,216,128]{2,1,0:T(8,128)(2,1)S(1)} collective-permute-done((bf16[2,216,128]{2,1,0:T(8,128)(2,1)S(1)}, bf16[2,216,128]{2,1,0:T(8,128)(2,1)S(1)}, u32[]{:S(2)}, u32[]{:S(2)}) %collective-permute-start.11) | collective-permute-done | bytes 110624 | tf_op jit(solution)/shard_map/ppermute | solution.py:447
  53.4 1.8 %collective-permute-done.12.refs_2_ = bf16[2,216,128]{2,1,0:T(8,128)(2,1)S(1)} collective-permute-done((bf16[2,216,128]{2,1,0:T(8,128)(2,1)S(1)}, bf16[2,216,128]{2,1,0:T(8,128)(2,1)S(1)}, u32[]{:S(2)}, u32[]{:S(2)}) %collective-permute-start.12) | collective-permute-done | bytes 110624 | tf_op jit(solution)/shard_map/ppermute | solution.py:447
  55.2 2.4 %collective-permute-done.13.refs_3_ = bf16[2,216,128]{2,1,0:T(8,128)(2,1)S(1)} collective-permute-done((bf16[2,216,128]{2,1,0:T(8,128)(2,1)S(1)}, bf16[2,216,128]{2,1,0:T(8,128)(2,1)S(1)}, u32[]{:S(2)}, u32[]{:S(2)}) %collective-permute-start.13) | collective-permute-done | bytes 110624 | tf_op jit(solution)/shard_map/ppermute | solution.py:447
  57.6 0.1 reduce.1
  57.7 3.3 %collective-permute-start.14 = (bf16[216,128]{1,0:T(8,128)(2,1)S(1)}, bf16[216,128]{1,0:T(8,128)(2,1)S(1)}, u32[]{:S(2)}, u32[]{:S(2)}) collective-permute-start(bf16[216,128]{1,0:T(8,128)(2,1)S(1)} %get-tuple-element.77), channel_id=1, source_target_pairs={{0,8},{1,9},{2,10},{3,11},{4,12},{5,13},{6,14},{7,15},{8,0},{9,1},... | collective-permute-start | bytes 165896 | tf_op jit(solution)/shard_map/ppermute | solution.py:447
  61.0 2.4 %collective-permute-done.14.part_ref = bf16[216,128]{1,0:T(8,128)(2,1)S(1)} collective-permute-done((bf16[216,128]{1,0:T(8,128)(2,1)S(1)}, bf16[216,128]{1,0:T(8,128)(2,1)S(1)}, u32[]{:S(2)}, u32[]{:S(2)}) %collective-permute-start.14) | collective-permute-done | bytes 55328 | tf_op jit(solution)/shard_map/ppermute | solution.py:447
  63.5 0.0 copy-done.3
  63.5 0.0 copy-done.4
  63.5 0.8 %finish.1 = (f32[1,128,128]{2,1,0:T(8,128)}, f32[1,64,128]{2,1,0:T(8,128)}, f32[1,128]{1,0:T(1,128)}, f32[1,16,128]{2,1,0:T(8,128)}) custom-call(f32[216,128]{1,0:T(8,128)S(1)} %get-tuple-element.76.keep_ref, bf16[216,128]{1,0:T(8,128)(2,1)S(1)} %collective-permute-done.14.part_ref, bf16[1,16,128]{2,1,0:T(8,128)(2,1)S(1)} %copy-done.4, ...), custom_call_target="tpu_custom_call" | custom-call | tf_op jit(solution)/shard_map/finish/pallas_call | solution.py:560
  (1 shorter events, 0.0 us)
Async XLA Ops:
  0.6 62.8 %copy-start.3 = (bf16[1,128,128]{2,1,0:T(8,128)(2,1)S(1)}, bf16[1,128,128]{2,1,0:T(8,128)(2,1)}, u32[]{:S(2)}) copy-start(bf16[1,128,128]{2,1,0:T(8,128)(2,1)} %wh_ref.1) | copy-start | bytes 98308
  0.6 62.8 %copy-start.4 = (bf16[1,16,128]{2,1,0:T(8,128)(2,1)S(1)}, bf16[1,16,128]{2,1,0:T(8,128)(2,1)}, u32[]{:S(2)}) copy-start(bf16[1,16,128]{2,1,0:T(8,128)(2,1)} %samp_ref.1) | copy-start | bytes 12292
  2.8 9.4 %collective-permute-start = (bf16[400,128]{1,0:T(8,128)(2,1)}, bf16[400,128]{1,0:T(8,128)(2,1)S(1)}, u32[]{:S(2)}, u32[]{:S(2)}) collective-permute-start(bf16[400,128]{1,0:T(8,128)(2,1)} %get-tuple-element.44), channel_id=1, source_target_pairs={{0,8},{1,9},{2,10},{3,11},{4,12},{5,13},{6,14},{7,15},{8,0},{9,1},... | collective-permute-start | bytes 307208 | tf_op jit(solution)/shard_map/ppermute | solution.py:447
  6.9 1.0 %copy-start = (bf16[576,384]{1,0:T(8,128)(2,1)S(1)}, bf16[576,384]{1,0:T(8,128)(2,1)}, u32[]{:S(2)}) copy-start(bf16[576,384]{1,0:T(8,128)(2,1)} %decoder_ref.1) | copy-start | bytes 1327108
  7.9 0.9 %copy-start.2 = (bf16[256,384]{1,0:T(8,128)(2,1)S(1)}, bf16[256,384]{1,0:T(8,128)(2,1)}, u32[]{:S(2)}) copy-start(bf16[256,384]{1,0:T(8,128)(2,1)} %target_ref.1) | copy-start | bytes 589828
  12.2 1.0 %copy-start.1 = (bf16[4,256,128]{2,1,0:T(8,128)(2,1)S(1)}, bf16[4,256,128]{2,1,0:T(8,128)(2,1)}, u32[]{:S(2)}) copy-start(bf16[4,256,128]{2,1,0:T(8,128)(2,1)} %get-tuple-element.43.near_ref) | copy-start | bytes 786436
  13.2 5.4 %collective-permute-start.1 = (bf16[2,256,128]{2,1,0:T(8,128)(2,1)S(1)}, bf16[2,256,128]{2,1,0:T(8,128)(2,1)S(1)}, u32[]{:S(2)}, u32[]{:S(2)}) collective-permute-start(bf16[2,256,128]{2,1,0:T(8,128)(2,1)S(1)} %get-tuple-element.50), channel_id=1, source_target_pairs={{0,2},{1,3},{2,0},{3,1},{4,6},{5,7},{6,4},{7,5},{8,10},{9,11},{10,... | collective-permute-start | bytes 393224 | tf_op jit(solution)/shard_map/ppermute | solution.py:447
  14.8 5.6 %collective-permute-start.2 = (bf16[2,256,128]{2,1,0:T(8,128)(2,1)S(1)}, bf16[2,256,128]{2,1,0:T(8,128)(2,1)S(1)}, u32[]{:S(2)}, u32[]{:S(2)}) collective-permute-start(bf16[2,256,128]{2,1,0:T(8,128)(2,1)S(1)} %get-tuple-element.51), channel_id=1, source_target_pairs={{0,4},{1,5},{2,6},{3,7},{4,0},{5,1},{6,2},{7,3},{8,12},{9,13},{10,... | collective-permute-start | bytes 393224 | tf_op jit(solution)/shard_map/ppermute | solution.py:447
  15.6 6.9 %collective-permute-start.3 = (bf16[2,256,128]{2,1,0:T(8,128)(2,1)S(1)}, bf16[2,256,128]{2,1,0:T(8,128)(2,1)S(1)}, u32[]{:S(2)}, u32[]{:S(2)}) collective-permute-start(bf16[2,256,128]{2,1,0:T(8,128)(2,1)S(1)} %get-tuple-element.52), channel_id=1, source_target_pairs={{0,6},{1,7},{2,4},{3,5},{4,2},{5,3},{6,0},{7,1},{8,14},{9,15},{10,... | collective-permute-start | bytes 393224 | tf_op jit(solution)/shard_map/ppermute | solution.py:447
  16.8 5.8 %collective-permute-start.4 = (bf16[2,256,128]{2,1,0:T(8,128)(2,1)S(1)}, bf16[2,256,128]{2,1,0:T(8,128)(2,1)S(1)}, u32[]{:S(2)}, u32[]{:S(2)}) collective-permute-start(bf16[2,256,128]{2,1,0:T(8,128)(2,1)S(1)} %get-tuple-element.49.refs_0_), channel_id=1, source_target_pairs={{0,1},{1,0},{2,3},{3,2},{4,5},{5,4},{6,7},{7,6},{8,9},{9,8},{10,11... | collective-permute-start | bytes 393224 | tf_op jit(solution)/shard_map/ppermute | solution.py:492
  18.6 3.9 %collective-permute-start.5 = (bf16[2,256,128]{2,1,0:T(8,128)(2,1)S(1)}, bf16[2,256,128]{2,1,0:T(8,128)(2,1)S(1)}, u32[]{:S(2)}, u32[]{:S(2)}) collective-permute-start(bf16[2,256,128]{2,1,0:T(8,128)(2,1)S(1)} %collective-permute-done.1.refs_1_), channel_id=1, source_target_pairs={{0,1},{1,0},{2,3},{3,2},{4,5},{5,4},{6,7},{7,6},{8,9},{9,8},{10,11... | collective-permute-start | bytes 393224 | tf_op jit(solution)/shard_map/ppermute | solution.py:492
  20.4 2.1 %collective-permute-start.6 = (bf16[2,256,128]{2,1,0:T(8,128)(2,1)S(1)}, bf16[2,256,128]{2,1,0:T(8,128)(2,1)S(1)}, u32[]{:S(2)}, u32[]{:S(2)}) collective-permute-start(bf16[2,256,128]{2,1,0:T(8,128)(2,1)S(1)} %collective-permute-done.2.refs_2_), channel_id=1, source_target_pairs={{0,1},{1,0},{2,3},{3,2},{4,5},{5,4},{6,7},{7,6},{8,9},{9,8},{10,11... | collective-permute-start | bytes 393224 | tf_op jit(solution)/shard_map/ppermute | solution.py:492
  22.5 1.3 %collective-permute-start.7 = (bf16[2,256,128]{2,1,0:T(8,128)(2,1)S(1)}, bf16[2,256,128]{2,1,0:T(8,128)(2,1)S(1)}, u32[]{:S(2)}, u32[]{:S(2)}) collective-permute-start(bf16[2,256,128]{2,1,0:T(8,128)(2,1)S(1)} %collective-permute-done.3.refs_3_), channel_id=1, source_target_pairs={{0,1},{1,0},{2,3},{3,2},{4,5},{5,4},{6,7},{7,6},{8,9},{9,8},{10,11... | collective-permute-start | bytes 393224 | tf_op jit(solution)/shard_map/ppermute | solution.py:492
  30.7 1.4 %collective-permute-start.8 = (bf16[256,256]{1,0:T(8,128)(2,1)S(1)}, bf16[256,256]{1,0:T(8,128)(2,1)S(1)}, u32[]{:S(2)}, u32[]{:S(2)}) collective-permute-start(bf16[256,256]{1,0:T(8,128)(2,1)S(1)} %get-tuple-element.55), channel_id=1, source_target_pairs={{0,1},{1,0},{2,3},{3,2},{4,5},{5,4},{6,7},{7,6},{8,9},{9,8},{10,11... | collective-permute-start | bytes 393224 | tf_op jit(solution)/shard_map/ppermute | solution.py:526
  30.9 1.2 %collective-permute-start.9 = (bf16[256,256]{1,0:T(8,128)(2,1)S(1)}, bf16[256,256]{1,0:T(8,128)(2,1)S(1)}, u32[]{:S(2)}, u32[]{:S(2)}) collective-permute-start(bf16[256,256]{1,0:T(8,128)(2,1)S(1)} %get-tuple-element.56), channel_id=1, source_target_pairs={{1,2},{3,4},{5,6},{7,8},{9,10},{11,12},{13,14},{2,1},{4,3},{6,5},{... | collective-permute-start | bytes 393224 | tf_op jit(solution)/shard_map/ppermute | solution.py:527
  41.0 6.9 %collective-permute-start.10 = (bf16[8,216,128]{2,1,0:T(8,128)(2,1)S(1)}, bf16[8,216,128]{2,1,0:T(8,128)(2,1)S(1)}, u32[]{:S(2)}, u32[]{:S(2)}) collective-permute-start(bf16[8,216,128]{2,1,0:T(8,128)(2,1)S(1)} %get-tuple-element.71), channel_id=1, source_target_pairs={{0,1},{1,0},{2,3},{3,2},{4,5},{5,4},{6,7},{7,6},{8,9},{9,8},{10,11... | collective-permute-start | bytes 1327112 | tf_op jit(solution)/shard_map/ppermute | solution.py:547
  48.0 5.4 %collective-permute-start.11 = (bf16[2,216,128]{2,1,0:T(8,128)(2,1)S(1)}, bf16[2,216,128]{2,1,0:T(8,128)(2,1)S(1)}, u32[]{:S(2)}, u32[]{:S(2)}) collective-permute-start(bf16[2,216,128]{2,1,0:T(8,128)(2,1)S(1)} %get-tuple-element.73), channel_id=1, source_target_pairs={{0,2},{1,3},{2,0},{3,1},{4,6},{5,7},{6,4},{7,5},{8,10},{9,11},{10,... | collective-permute-start | bytes 331784 | tf_op jit(solution)/shard_map/ppermute | solution.py:447
  49.7 5.5 %collective-permute-start.12 = (bf16[2,216,128]{2,1,0:T(8,128)(2,1)S(1)}, bf16[2,216,128]{2,1,0:T(8,128)(2,1)S(1)}, u32[]{:S(2)}, u32[]{:S(2)}) collective-permute-start(bf16[2,216,128]{2,1,0:T(8,128)(2,1)S(1)} %get-tuple-element.74), channel_id=1, source_target_pairs={{0,4},{1,5},{2,6},{3,7},{4,0},{5,1},{6,2},{7,3},{8,12},{9,13},{10,... | collective-permute-start | bytes 331784 | tf_op jit(solution)/shard_map/ppermute | solution.py:447
  51.5 6.1 %collective-permute-start.13 = (bf16[2,216,128]{2,1,0:T(8,128)(2,1)S(1)}, bf16[2,216,128]{2,1,0:T(8,128)(2,1)S(1)}, u32[]{:S(2)}, u32[]{:S(2)}) collective-permute-start(bf16[2,216,128]{2,1,0:T(8,128)(2,1)S(1)} %get-tuple-element.75), channel_id=1, source_target_pairs={{0,6},{1,7},{2,4},{3,5},{4,2},{5,3},{6,0},{7,1},{8,14},{9,15},{10,... | collective-permute-start | bytes 331784 | tf_op jit(solution)/shard_map/ppermute | solution.py:447
  57.7 5.8 %collective-permute-start.14 = (bf16[216,128]{1,0:T(8,128)(2,1)S(1)}, bf16[216,128]{1,0:T(8,128)(2,1)S(1)}, u32[]{:S(2)}, u32[]{:S(2)}) collective-permute-start(bf16[216,128]{1,0:T(8,128)(2,1)S(1)} %get-tuple-element.77), channel_id=1, source_target_pairs={{0,8},{1,9},{2,10},{3,11},{4,12},{5,13},{6,14},{7,15},{8,0},{9,1},... | collective-permute-start | bytes 165896 | tf_op jit(solution)/shard_map/ppermute | solution.py:447

commit v4 on v3

--- a/solution.py
+++ b/solution.py
@@ -133,12 +133,13 @@
     blocks = [received[c * quarter + k].at[side] for c in range(2) for side in range(2) for k in range(quarter)]
     (
         image_ref, halo_in_ref, halo_cr_ref, h_ref, wd_ref, att_hw_ref, wide_hw_ref, weight_ref, pass_ref, slope_ref, att_ref, rel_ref, codes_ref, wf_out,
-        meta_ref, plain_ref, table_ref, proj_ref, a_ref, picked_ref, row_ref, ahead_ref,
+        meta_ref, plain_ref, table_ref, proj_ref, a_ref, picked_ref, row_ref, density_ref,
     ) = refs[half + 1 :]
     rays = codes_ref.shape[1]
     segs = rel_ref.shape[0]
-    samples = weight_ref.shape[1]
+    samples = weight_ref.shape[0]
     feats = image_ref.shape[0]
+    hids = table_ref.shape[1]
     me = lax.axis_index("region")
     core = me & 1
     chip = lax.shift_right_logical(me, 1)
@@ -166,8 +167,7 @@
     rel = jnp.bitwise_xor(region & 1, core) * half + jnp.bitwise_xor(lax.shift_right_logical(region, 1), chip)
     rel_ref[...] = rel
     for k in range(segs):
-        for part in range(2):
-            row_ref[2 * k + part] = meta[6 + k : 7 + k, part * LANES : (part + 1) * LANES]
+        row_ref[:, k * rays : (k + 1) * rays] = meta[6 + k : 7 + k]
     wanted = [rel_ref[k : k + 1, :] for k in range(segs)]
     for r, block in enumerate(blocks):
         w_t = block[0:WF_AT]
@@ -189,41 +189,46 @@
                 a_ref[2 * k + part, rows, :] = choose(values, bits[k])
             return carry
 
-        lax.fori_loop(0, 16, pick_rows, 0)
+        lax.fori_loop(0, 16, pick_rows, 0, unroll=4)
     hot = seg_hot(wanted, regions).astype(BF16)
     hot2 = jnp.concatenate([hot, hot], axis=0)
     for tile in range(2 * segs):
         picked_ref[tile] = hot2[:, tile * LANES : (tile + 1) * LANES]
-    ahead_ref[...] = jnp.zeros(ahead_ref.shape, F32)
-    order = iota((samples, LANES), 0).astype(F32)
-
-    def step(tile, carry):
+
+    def densities(tile, carry):
         here = picked_ref[tile]
-        wd = dot(table_ref[samples], here)
-        wd_ref[tile] = wd
+        wd_ref[tile] = dot(table_ref[samples], here)
         sums = []
         for s in range(samples):
             h = jnp.maximum(a_ref[tile] + dot(table_ref[s], here), 0.0)
             h_ref[tile, s] = h
             sums.append(jnp.sum(h * wd_ref[tile], axis=0, keepdims=True))
-        density = jnp.concatenate(sums, axis=0)
-        part = tile & 1
-        live = order < row_ref[tile]
-        soft = jnp.maximum(density, 0.0) + jnp.log1p(jnp.exp(-jnp.abs(density)))
-        thick = jnp.where(live, STEP * soft, 0.0)
-        through = running_sum(thick)
-        passing = jnp.exp(-(through - thick))
-        keeping = jnp.exp(-thick)
-        weight = passing * (1.0 - keeping)
-        weight_ref[tile] = weight
-        pass_ref[tile] = passing * keeping
-        slope_ref[tile] = jnp.where(live, STEP / (1.0 + jnp.exp(-density)), 0.0)
-        before = ahead_ref[part]
-        att = jnp.exp(-before)
-        ahead_ref[part] = before + through[samples - 1 : samples, :]
-        att_ref[tile] = att
-        scale = [jnp.broadcast_to(weight[s : s + 1, :] * att, (8, LANES)) for s in range(samples)]
         lanes = pl.ds(pl.multiple_of(tile * LANES, LANES), LANES)
+        density_ref[:, lanes] = jnp.concatenate(sums, axis=0)
+        return carry
+
+    lax.fori_loop(0, 2 * segs, densities, 0, unroll=4)
+    density = density_ref[...]
+    live = iota(density.shape, 0).astype(F32) < row_ref[...]
+    soft = jnp.maximum(density, 0.0) + jnp.log1p(jnp.exp(-jnp.abs(density)))
+    thick = jnp.where(live, STEP * soft, 0.0)
+    through = running_sum(thick)
+    passing = jnp.exp(-(through - thick))
+    keeping = jnp.exp(-thick)
+    weight = passing * (1.0 - keeping)
+    weight_ref[...] = weight
+    pass_ref[...] = passing * keeping
+    slope_ref[...] = jnp.where(live, STEP / (1.0 + jnp.exp(-density)), 0.0)
+    ahead = jnp.zeros((1, rays), F32)
+    for k in range(segs):
+        att_ref[:, k * rays : (k + 1) * rays] = jnp.exp(-ahead)
+        ahead = ahead + through[samples - 1 : samples, k * rays : (k + 1) * rays]
+    density_ref[...] = weight * att_ref[...]
+
+    def compose(tile, carry):
+        lanes = pl.ds(pl.multiple_of(tile * LANES, LANES), LANES)
+        faded = density_ref[:, lanes]
+        scale = [jnp.broadcast_to(faded[s : s + 1, :], (8, LANES)) for s in range(samples)]
         for pair in range(8):
             both = []
             for ht in (2 * pair, 2 * pair + 1):
@@ -231,29 +236,32 @@
                 total = scale[0] * h_ref[tile, 0, rows, :]
                 for s in range(1, samples):
                     total = total + scale[s] * h_ref[tile, s, rows, :]
-                att_hw_ref[tile, rows, :] = total
                 both.append(total)
-            wide_hw_ref[pair * 16 : pair * 16 + 16, lanes] = jnp.concatenate(both, axis=0).astype(BF16)
+            both = jnp.concatenate(both, axis=0)
+            high, low = split(both)
+            att_hw_ref[pair * 16 : pair * 16 + 16, lanes] = both
+            wide_hw_ref[pair * 16 : pair * 16 + 16, lanes] = high
+            wide_hw_ref[hids + pair * 16 : hids + pair * 16 + 16, lanes] = low
         return carry
 
-    lax.fori_loop(0, 2 * segs, step, 0)
+    lax.fori_loop(0, 2 * segs, compose, 0, unroll=2)
     wf_twice = jnp.concatenate([wf_out[...], wf_out[...]], axis=1)
-    for part in range(2):
-        feat = [jnp.zeros((8, LANES), F32)] * (feats // 8)
-        for k in range(segs):
-            tile = 2 * k + part
-            high, low = split(att_hw_ref[tile])
-            proj_ref[0 : regions * feats // LANES, :, 0:LANES] = dot(wf_twice, jnp.concatenate([high, low], axis=0)).reshape(
-                regions * feats // LANES, LANES, LANES
-            )
-            bits = bits_of(wanted[k][:, part * LANES : (part + 1) * LANES], regions)
+    feat = [jnp.zeros((8, LANES), F32)] * (2 * (feats // 8))
+    for k in range(segs):
+        values = dot(wf_twice, wide_hw_ref[:, k * rays : (k + 1) * rays])
+        for r in range(regions * feats // LANES):
+            proj_ref[r] = values[r * LANES : (r + 1) * LANES]
+        for part in range(2):
+            lanes = slice(part * LANES, (part + 1) * LANES)
+            bits = bits_of(wanted[k][:, lanes], regions)
             for ft in range(feats // 8):
-                values = []
+                found = []
                 for r in range(regions):
                     at = r * feats + ft * 8
-                    values.append(proj_ref[at // LANES, at % LANES : at % LANES + 8, 0:LANES])
-                feat[ft] = feat[ft] + choose(values, bits)
-        image_ref[:, part * LANES : (part + 1) * LANES] = jnp.concatenate(feat, axis=0).astype(BF16)
+                    found.append(proj_ref[at // LANES, at % LANES : at % LANES + 8, lanes])
+                feat[2 * ft + part] = feat[2 * ft + part] + choose(found, bits)
+    for part in range(2):
+        image_ref[:, part * LANES : (part + 1) * LANES] = jnp.concatenate(feat[part::2], axis=0).astype(BF16)
     near, far = target_ref[:, :IW].astype(F32), target_ref[:, rays - IW :].astype(F32)
     for out_ref, row in ((halo_in_ref, jnp.where(core == 0, far, near)), (halo_cr_ref, jnp.where(core == 0, near, far))):
         out_ref[0:feats] = image_ref[...]
@@ -275,12 +283,14 @@
     half, own_ref, inner_ref, cross_ref, tgt_ref, dec_ref, dect_ref,
     h_in, wd_ref, att_hw_ref, wide_hw_ref, weight_ref, pass_ref, slope_ref, att_ref, rel_ref, codes_ref, wf_ref,
     mine_ref, other_ref,
-    patch_ref, masked_ref, q_ref, gp_ref, g1_ref, hd_ref, tail_ref, row_ref,
+    patch_ref, masked_ref, q_ref, gp_ref, g1_ref, hd_ref, tail_ref, row_ref, along_ref, hot_ref,
 ):
     regions = 2 * half
     feats, rays = own_ref.shape
     segs = rel_ref.shape[0]
-    samples = weight_ref.shape[1]
+    samples = weight_ref.shape[0]
+    hids = wd_ref.shape[1]
+    unroll = min(regions, 16)
     me = lax.axis_index("region")
     core = me & 1
     own = own_ref[...].astype(F32)
@@ -318,46 +328,61 @@
         image_rows.append(total)
     grad_ray = jnp.concatenate(image_rows, axis=1)
     wanted = [rel_ref[k : k + 1, :] for k in range(segs)]
+    hot = seg_hot(wanted, regions)
     for r in range(regions):
+        hot_ref[r] = jnp.broadcast_to(hot[r : r + 1], (16, segs * rays)).astype(BF16)
+    hot = hot.astype(BF16)
+    grad_narrow = grad_ray.astype(BF16)
+
+    def mask_grads(r, carry):
         for k in range(segs):
-            masked = jnp.where(wanted[k] == r, grad_ray, 0.0).astype(BF16)
-            masked_ref[r * feats : (r + 1) * feats, k * rays : (k + 1) * rays] = masked
-    raw = dot(wf_ref[...], masked_ref[...], 0, 0)
-    for tile in range(2 * segs):
-        q_ref[tile] = raw[:, tile * LANES : (tile + 1) * LANES]
-    feat_grad = dot(masked_ref[...], wide_hw_ref[...], 1, 1).astype(BF16)
+            mask = hot_ref[r, :, k * rays : (k + 1) * rays]
+            for at in range(0, feats, 16):
+                rows = pl.ds(pl.multiple_of(r * feats + at, 16), 16)
+                masked_ref[rows, k * rays : (k + 1) * rays] = grad_narrow[at : at + 16] * mask
+        return carry
+
+    lax.fori_loop(0, regions, mask_grads, 0, unroll=unroll)
+    q_ref[...] = dot(wf_ref[...], masked_ref[...], 0, 0)
+    feat_grad = dot(masked_ref[...], wide_hw_ref[0:hids], 1, 1).astype(BF16)
     for r in range(regions):
         out, to = (mine_ref, r) if r < half else (other_ref, r - half)
         out[to, WF_AT:G2_AT] = feat_grad[r * feats : (r + 1) * feats]
-    hot = seg_hot(wanted, regions).astype(BF16)
-    for part in range(2):
-        later = jnp.zeros((1, LANES), F32)
-        for k in reversed(range(segs)):
-            row_ref[2 * k + part] = -later
-            pulled = jnp.sum(att_hw_ref[2 * k + part] * q_ref[2 * k + part], axis=0, keepdims=True)
-            later = later + pulled
-
-    def step(tile, carry):
-        att = jnp.broadcast_to(att_ref[tile], (8, LANES))
+    later = jnp.zeros((1, rays), F32)
+    for k in reversed(range(segs)):
+        lanes = slice(k * rays, (k + 1) * rays)
+        row_ref[:, lanes] = -later
+        later = later + jnp.sum(att_hw_ref[:, lanes] * q_ref[:, lanes], axis=0, keepdims=True)
+
+    def project(tile, carry):
+        lanes = pl.ds(pl.multiple_of(tile * LANES, LANES), LANES)
+        att = jnp.broadcast_to(att_ref[:, lanes], (8, LANES))
         sums = [jnp.zeros((8, LANES), F32)] * samples
         for ht in range(16):
             rows = slice(ht * 8, ht * 8 + 8)
-            q = q_ref[tile, rows, :] * att
-            q_ref[tile, rows, :] = q
+            q = q_ref[rows, lanes] * att
+            q_ref[rows, lanes] = q
             for s in range(samples):
                 sums[s] = sums[s] + h_in[tile, s, rows, :] * q
-        along = jnp.concatenate([jnp.sum(v, axis=0, keepdims=True) for v in sums], axis=0)
-        weight = weight_ref[tile]
-        through = running_sum(along * weight)
-        later = through[samples - 1 : samples, :] - through
-        grad_thick = row_ref[tile] + along * pass_ref[tile] - later
-        grad_density = (grad_thick * slope_ref[tile]).astype(BF16).astype(F32)
+        along_ref[:, lanes] = jnp.concatenate([jnp.sum(v, axis=0, keepdims=True) for v in sums], axis=0)
+        return carry
+
+    lax.fori_loop(0, 2 * segs, project, 0)
+    along = along_ref[...]
+    through = running_sum(along * weight_ref[...])
+    later = through[samples - 1 : samples, :] - through
+    grad_thick = row_ref[...] + along * pass_ref[...] - later
+    along_ref[...] = (grad_thick * slope_ref[...]).astype(BF16).astype(F32)
+
+    def descend(tile, carry):
+        lanes = pl.ds(pl.multiple_of(tile * LANES, LANES), LANES)
+        weight = weight_ref[:, lanes]
+        grad_density = along_ref[:, lanes]
         scale = [jnp.broadcast_to(weight[s : s + 1, :], (8, LANES)) for s in range(samples)]
         slant = [jnp.broadcast_to(grad_density[s : s + 1, :], (8, LANES)) for s in range(samples)]
-        lanes = pl.ds(pl.multiple_of(tile * LANES, LANES), LANES)
         for pair in range(8):
             at = [slice((2 * pair + u) * 8, (2 * pair + u) * 8 + 8) for u in range(2)]
-            q = [q_ref[tile, rows, :] for rows in at]
+            q = [q_ref[rows, lanes] for rows in at]
             wd = [wd_ref[tile, rows, :] for rows in at]
             g1 = [jnp.zeros((8, LANES), F32)] * 2
             hd = [jnp.zeros((8, LANES), F32)] * 2
@@ -369,17 +394,17 @@
                     g1[u] = g1[u] + gp
                     hd[u] = hd[u] + slant[s] * h
                     both.append(gp)
-                gp_ref[s, 16 * pair : 16 * pair + 16, lanes] = jnp.concatenate(both, axis=0).astype(BF16)
+                gp_ref[s * hids + 16 * pair : s * hids + 16 * pair + 16, lanes] = jnp.concatenate(both, axis=0).astype(BF16)
             g1_ref[16 * pair : 16 * pair + 16, lanes] = jnp.concatenate(g1, axis=0).astype(BF16)
             hd_ref[16 * pair : 16 * pair + 16, lanes] = jnp.concatenate(hd, axis=0).astype(BF16)
         return carry
 
-    lax.fori_loop(0, 2 * segs, step, 0)
-    codes = codes_ref[...].astype(F32)
+    lax.fori_loop(0, 2 * segs, descend, 0)
     tail_ref[...] = jnp.zeros(tail_ref.shape, F32)
     for s in range(samples):
-        tail_ref[:, s, :] = dot(hot, gp_ref[s], 1, 1)
+        tail_ref[:, s, :] = dot(hot, gp_ref[s * hids : (s + 1) * hids], 1, 1)
     tail_ref[:, samples, :] = dot(hot, hd_ref[...], 1, 1)
+    codes = codes_ref[...].astype(F32)
     g1 = g1_ref[...]
     for r in range(regions):
         out, to = (mine_ref, r) if r < half else (other_ref, r - half)
@@ -388,7 +413,8 @@
         out[to, G2_AT:PART_ROWS] = tail_ref[r].astype(BF16)
 
 
-def flip_kernel(target_ref, decoder_ref, target_out, decoder_out, same_out):
+def flip_kernel(target_ref, decoder_ref, near_ref, target_out, decoder_out, same_out, near_out):
+    near_out[...] = near_ref[...]
     same_out[...] = decoder_ref[...]
     target_out[...] = target_ref[...].astype(F32).T.astype(BF16)
     decoder_out[...] = decoder_ref[...].astype(F32).T.astype(BF16)
@@ -476,11 +502,12 @@
             shape(dino_width, rays, kind=BF16),
             shape(*decoder.shape[::-1], kind=BF16),
             shape(*decoder.shape, kind=BF16),
+            shape(*near.shape, kind=BF16),
         ),
-        compiler_params=grant(8),
+        compiler_params=grant(8 + regions / 8),
         name="flip",
-    )(target, decoder)
-    far, (target_t, decoder_t, decoder) = lax.optimization_barrier((far, flipped))
+    )(target, decoder, near)
+    far, (target_t, decoder_t, decoder, near) = lax.optimization_barrier((far, flipped))
     blocks = to_half(
         pl.pallas_call(
             relay_kernel,
@@ -499,12 +526,12 @@
             shape(feat_width + dino_width // 2, rays, kind=BF16),
             shape(tiles, samples, hid_width, LANES),
             shape(tiles, hid_width, LANES),
-            shape(tiles, hid_width, LANES),
-            shape(hid_width, lanes, kind=BF16),
-            shape(tiles, samples, LANES),
-            shape(tiles, samples, LANES),
-            shape(tiles, samples, LANES),
-            shape(tiles, 1, LANES),
+            shape(hid_width, lanes),
+            shape(2 * hid_width, lanes, kind=BF16),
+            shape(samples, lanes),
+            shape(samples, lanes),
+            shape(samples, lanes),
+            shape(1, lanes),
             shape(segs, rays, kind=jnp.int32),
             shape(code_width, rays, kind=BF16),
             shape(regions * feat_width, hid_width, kind=BF16),
@@ -516,8 +543,8 @@
             pltpu.VMEM((regions, hid_width, rays), F32),
             pltpu.VMEM((tiles, hid_width, LANES), F32),
             pltpu.VMEM((tiles, 2 * regions, LANES), BF16),
-            pltpu.VMEM((tiles, 1, LANES), F32),
-            pltpu.VMEM((2, 1, LANES), F32),
+            pltpu.VMEM((1, lanes), F32),
+            pltpu.VMEM((samples, lanes), F32),
         ],
         compiler_params=grant(10 + regions / 4),
         name="forward",
@@ -533,14 +560,16 @@
         scratch_shapes=[
             pltpu.VMEM((decoder.shape[0], 4 * IW), BF16),
             pltpu.VMEM((regions * feat_width, lanes), BF16),
-            pltpu.VMEM((tiles, hid_width, LANES), F32),
-            pltpu.VMEM((samples, hid_width, lanes), BF16),
+            pltpu.VMEM((hid_width, lanes), F32),
+            pltpu.VMEM((samples * hid_width, lanes), BF16),
             pltpu.VMEM((hid_width, lanes), BF16),
             pltpu.VMEM((hid_width, lanes), BF16),
             pltpu.VMEM((regions, PART_ROWS - G2_AT, hid_width), F32),
-            pltpu.VMEM((tiles, 1, LANES), F32),
+            pltpu.VMEM((1, lanes), F32),
+            pltpu.VMEM((samples, lanes), F32),
+            pltpu.VMEM((regions, 16, lanes), BF16),
         ],
-        compiler_params=grant(16 + regions / 4),
+        compiler_params=grant(22 + regions / 4),
         name="backward",
     )(image, halo_in, halo_cr, target_t, decoder, decoder_t, *kept)
 

time: 64.6 us -> 61.8 us (0.957)
  Pallas kernels: 19.2 us -> 17.3 us
  waiting for transfers between devices: 20.2 us -> 19.2 us
    pallas_call x1, Pallas kernels: 6.83 us -> 4.99 us  [local(): pl.pallas_call(functools.partial(forward_kernel, half, group, room), out_...]
    ppermute x8, waiting for transfers between devices: 16.9 us -> 16 us  [to_chip(): lax.ppermute(block, 'region', [(i, i ^ 2 * k) for i in range(regions)])]
where the time goes in v4:
time: 61.8 us; the launch traced here: 61.5 us
  starting transfers between devices  21.3 us (34%)
  waiting for transfers between devices  19.2 us (31%)
  Pallas kernels  17.3 us (28%)
  local copies, waits for them, and re-layouts  2.9 us (5%)
  between operations  0.72 us (1%)
    ppermute x8, waiting for transfers between devices, to_chip(): lax.ppermute(block, 'region', [(i, i ^ 2 * k) for i in range(regions)])  16 us
    ppermute x8, starting transfers between devices, to_chip(): lax.ppermute(block, 'region', [(i, i ^ 2 * k) for i in range(regions)])  14.9 us
    pallas_call x1, Pallas kernels, local(): pl.pallas_call(functools.partial(backward_kernel, half), out_shape=(part,...  8.83 us
    ppermute x1, starting transfers between devices, local(): theirs = lax.ppermute(other, 'region', inner)  5.5 us
    pallas_call x1, Pallas kernels, local(): pl.pallas_call(functools.partial(forward_kernel, half, group, room), out_...  4.99 us
    unnamed x10, local copies, waits for them, and re-layouts  2.9 us
    pallas_call x1, Pallas kernels, local(): pl.pallas_call(functools.partial(pack_kernel, half, group, room), out_sha...  2.16 us
    ppermute x1, waiting for transfers between devices, local(): theirs = lax.ppermute(other, 'region', inner)  1.42 us
  transfers between devices with their start and end apart: 15, of which 11 were waited for; matrix products, arithmetic and copies ran while one was open for 0% of the time, Pallas kernels for 0%

profile of v4, /device:TPU:0, one launch (start us, length us, event | category | flops | bytes accessed | tf_op | source)
XLA Modules:
  0.0 61.5 jit_solution(9294926932580452662)
XLA Ops:
  0.6 0.0 copy-start.3
  0.6 0.0 copy-start.4
  0.7 2.2 %pack.1 = (bf16[4,256,128]{2,1,0:T(8,128)(2,1)}, bf16[400,128]{1,0:T(8,128)(2,1)}) custom-call(s32[1,256]{1,0:T(1,128)} %bitcast.8, s32[4,256]{1,0:T(4,128)} %bitcast.6, s32[4,256]{1,0:T(4,128)} %bitcast.7, bf16[256,128]{1,0:T(8,128)(2,1)} %refs_3_.1, bf16[1,16,128]{2,1,0:T(8,128)(2,1)} %samp_ref.1, bf16[1,128,128]{2,1,0:T(8,128)(2,1)} %wh_ref.1, ...), custom_call_target="tpu_custom_call" | custom-call | tf_op jit(solution)/shard_map/pack/pallas_call | solution.py:482
  2.8 4.1 %collective-permute-start = (bf16[400,128]{1,0:T(8,128)(2,1)}, bf16[400,128]{1,0:T(8,128)(2,1)S(1)}, u32[]{:S(2)}, u32[]{:S(2)}) collective-permute-start(bf16[400,128]{1,0:T(8,128)(2,1)} %get-tuple-element.45), channel_id=1, source_target_pairs={{0,8},{1,9},{2,10},{3,11},{4,12},{5,13},{6,14},{7,15},{8,0},{9,1},... | collective-permute-start | bytes 307208 | tf_op jit(solution)/shard_map/ppermute | solution.py:473
  6.9 0.0 copy-start
  6.9 1.0 %copy-done = bf16[576,384]{1,0:T(8,128)(2,1)S(1)} copy-done((bf16[576,384]{1,0:T(8,128)(2,1)S(1)}, bf16[576,384]{1,0:T(8,128)(2,1)}, u32[]{:S(2)}) %copy-start) | copy-done | bytes 442392
  7.9 0.0 copy-start.1
  7.9 0.9 %copy-done.1 = bf16[4,256,128]{2,1,0:T(8,128)(2,1)S(1)} copy-done((bf16[4,256,128]{2,1,0:T(8,128)(2,1)S(1)}, bf16[4,256,128]{2,1,0:T(8,128)(2,1)}, u32[]{:S(2)}) %copy-start.1) | copy-done | bytes 262168
  8.9 0.0 copy-start.2
  8.9 0.9 %copy-done.2 = bf16[256,384]{1,0:T(8,128)(2,1)S(1)} copy-done((bf16[256,384]{1,0:T(8,128)(2,1)S(1)}, bf16[256,384]{1,0:T(8,128)(2,1)}, u32[]{:S(2)}) %copy-start.2) | copy-done | bytes 196632
  9.8 0.3 flip.1
  10.1 2.1 %collective-permute-done.far_ref = bf16[400,128]{1,0:T(8,128)(2,1)S(1)} collective-permute-done((bf16[400,128]{1,0:T(8,128)(2,1)}, bf16[400,128]{1,0:T(8,128)(2,1)S(1)}, u32[]{:S(2)}, u32[]{:S(2)}) %collective-permute-start) | collective-permute-done | bytes 102432 | tf_op jit(solution)/shard_map/ppermute | solution.py:473
  12.3 1.6 %collective-permute-start.1 = (bf16[2,256,128]{2,1,0:T(8,128)(2,1)S(1)}, bf16[2,256,128]{2,1,0:T(8,128)(2,1)S(1)}, u32[]{:S(2)}, u32[]{:S(2)}) collective-permute-start(bf16[2,256,128]{2,1,0:T(8,128)(2,1)S(1)} %get-tuple-element.54), channel_id=1, source_target_pairs={{0,2},{1,3},{2,0},{3,1},{4,6},{5,7},{6,4},{7,5},{8,10},{9,11},{10,... | collective-permute-start | bytes 393224 | tf_op jit(solution)/shard_map/ppermute | solution.py:473
  13.9 0.8 %collective-permute-start.2 = (bf16[2,256,128]{2,1,0:T(8,128)(2,1)S(1)}, bf16[2,256,128]{2,1,0:T(8,128)(2,1)S(1)}, u32[]{:S(2)}, u32[]{:S(2)}) collective-permute-start(bf16[2,256,128]{2,1,0:T(8,128)(2,1)S(1)} %get-tuple-element.55), channel_id=1, source_target_pairs={{0,4},{1,5},{2,6},{3,7},{4,0},{5,1},{6,2},{7,3},{8,12},{9,13},{10,... | collective-permute-start | bytes 393224 | tf_op jit(solution)/shard_map/ppermute | solution.py:473
  14.6 1.2 %collective-permute-start.3 = (bf16[2,256,128]{2,1,0:T(8,128)(2,1)S(1)}, bf16[2,256,128]{2,1,0:T(8,128)(2,1)S(1)}, u32[]{:S(2)}, u32[]{:S(2)}) collective-permute-start(bf16[2,256,128]{2,1,0:T(8,128)(2,1)S(1)} %get-tuple-element.56), channel_id=1, source_target_pairs={{0,6},{1,7},{2,4},{3,5},{4,2},{5,3},{6,0},{7,1},{8,14},{9,15},{10,... | collective-permute-start | bytes 393224 | tf_op jit(solution)/shard_map/ppermute | solution.py:473
  15.8 0.0 collective-permute-start.4
  15.8 1.8 %collective-permute-done.1.refs_1_ = bf16[2,256,128]{2,1,0:T(8,128)(2,1)S(1)} collective-permute-done((bf16[2,256,128]{2,1,0:T(8,128)(2,1)S(1)}, bf16[2,256,128]{2,1,0:T(8,128)(2,1)S(1)}, u32[]{:S(2)}, u32[]{:S(2)}) %collective-permute-start.1) | collective-permute-done | bytes 131104 | tf_op jit(solution)/shard_map/ppermute | solution.py:473
  17.6 0.0 collective-permute-start.5
  17.6 1.8 %collective-permute-done.2.refs_2_ = bf16[2,256,128]{2,1,0:T(8,128)(2,1)S(1)} collective-permute-done((bf16[2,256,128]{2,1,0:T(8,128)(2,1)S(1)}, bf16[2,256,128]{2,1,0:T(8,128)(2,1)S(1)}, u32[]{:S(2)}, u32[]{:S(2)}) %collective-permute-start.2) | collective-permute-done | bytes 131104 | tf_op jit(solution)/shard_map/ppermute | solution.py:473
  19.5 0.0 collective-permute-start.6
  19.5 2.1 %collective-permute-done.3.refs_3_ = bf16[2,256,128]{2,1,0:T(8,128)(2,1)S(1)} collective-permute-done((bf16[2,256,128]{2,1,0:T(8,128)(2,1)S(1)}, bf16[2,256,128]{2,1,0:T(8,128)(2,1)S(1)}, u32[]{:S(2)}, u32[]{:S(2)}) %collective-permute-start.3) | collective-permute-done | bytes 131104 | tf_op jit(solution)/shard_map/ppermute | solution.py:473
  21.6 0.0 collective-permute-start.7
  21.6 0.0 collective-permute-done.4.refs_4_
  21.6 0.0 collective-permute-done.5.refs_5_
  21.6 0.0 collective-permute-done.6.refs_6_
  21.6 1.3 %collective-permute-done.7.refs_7_ = bf16[2,256,128]{2,1,0:T(8,128)(2,1)S(1)} collective-permute-done((bf16[2,256,128]{2,1,0:T(8,128)(2,1)S(1)}, bf16[2,256,128]{2,1,0:T(8,128)(2,1)S(1)}, u32[]{:S(2)}, u32[]{:S(2)}) %collective-permute-start.7) | collective-permute-done | bytes 131104 | tf_op jit(solution)/shard_map/ppermute | solution.py:519
  22.9 5.0 %forward.1 = (bf16[64,256]{1,0:T(8,128)(2,1)S(1)}, bf16[256,256]{1,0:T(8,128)(2,1)S(1)}, bf16[256,256]{1,0:T(8,128)(2,1)S(1)}, f32[8,16,128,128]{3,2,1,0:T(8,128...) custom-call(bf16[2,256,128]{2,1,0:T(8,128)(2,1)S(1)} %get-tuple-elem, ...), custom_call_target="tpu_custom_call" | custom-call | tf_op jit(solution)/shard_map/forward/pallas_call | solution.py:521
  27.9 0.2 collective-permute-start.8
  28.1 0.7 %collective-permute-start.9 = (bf16[256,256]{1,0:T(8,128)(2,1)S(1)}, bf16[256,256]{1,0:T(8,128)(2,1)S(1)}, u32[]{:S(2)}, u32[]{:S(2)}) collective-permute-start(bf16[256,256]{1,0:T(8,128)(2,1)S(1)} %get-tuple-element.60), channel_id=1, source_target_pairs={{1,2},{3,4},{5,6},{7,8},{9,10},{11,12},{13,14},{2,1},{4,3},{6,5},{... | collective-permute-start | bytes 393224 | tf_op jit(solution)/shard_map/ppermute | solution.py:554
  28.8 0.5 collective-permute-done.8.inner_ref
  29.3 0.0 collective-permute-done.9.cross_ref
  29.3 8.8 %backward.1 = (bf16[8,216,128]{2,1,0:T(8,128)(2,1)S(1)}, bf16[8,216,128]{2,1,0:T(8,128)(2,1)S(1)}) custom-call(bf16[64,256]{1,0:T(8,128)(2,1)S(1)} %get-tuple-element.58.own_ref, bf16[256,256]{1,0:T(8,128)(2,1)S(1)} %collective-permute-done.8.inner_ref, bf16[256,256]{1,0:T(8,128)(2,1)S(1)} %collective-permute-done.9.cross_ref, ...), custom_call_target="tpu_custom_call" | custom-call | tf_op jit(solution)/shard_map/backward/pallas_call | solution.py:557
  38.2 5.5 %collective-permute-start.10 = (bf16[8,216,128]{2,1,0:T(8,128)(2,1)S(1)}, bf16[8,216,128]{2,1,0:T(8,128)(2,1)S(1)}, u32[]{:S(2)}, u32[]{:S(2)}) collective-permute-start(bf16[8,216,128]{2,1,0:T(8,128)(2,1)S(1)} %get-tuple-element.75), channel_id=1, source_target_pairs={{0,1},{1,0},{2,3},{3,2},{4,5},{5,4},{6,7},{7,6},{8,9},{9,8},{10,11... | collective-permute-start | bytes 1327112 | tf_op jit(solution)/shard_map/ppermute | solution.py:576
  43.7 1.4 %collective-permute-done.10.theirs_ref = bf16[8,216,128]{2,1,0:T(8,128)(2,1)S(1)} collective-permute-done((bf16[8,216,128]{2,1,0:T(8,128)(2,1)S(1)}, bf16[8,216,128]{2,1,0:T(8,128)(2,1)S(1)}, u32[]{:S(2)}, u32[]{:S(2)}) %collective-permute-start.10) | collective-permute-done | bytes 442400 | tf_op jit(solution)/shard_map/ppermute | solution.py:576
  45.1 0.1 merge.1
  45.2 1.8 %collective-permute-start.11 = (bf16[2,216,128]{2,1,0:T(8,128)(2,1)S(1)}, bf16[2,216,128]{2,1,0:T(8,128)(2,1)S(1)}, u32[]{:S(2)}, u32[]{:S(2)}) collective-permute-start(bf16[2,216,128]{2,1,0:T(8,128)(2,1)S(1)} %get-tuple-element.77), channel_id=1, source_target_pairs={{0,2},{1,3},{2,0},{3,1},{4,6},{5,7},{6,4},{7,5},{8,10},{9,11},{10,... | collective-permute-start | bytes 331784 | tf_op jit(solution)/shard_map/ppermute | solution.py:473
  47.0 1.7 %collective-permute-start.12 = (bf16[2,216,128]{2,1,0:T(8,128)(2,1)S(1)}, bf16[2,216,128]{2,1,0:T(8,128)(2,1)S(1)}, u32[]{:S(2)}, u32[]{:S(2)}) collective-permute-start(bf16[2,216,128]{2,1,0:T(8,128)(2,1)S(1)} %get-tuple-element.78), channel_id=1, source_target_pairs={{0,4},{1,5},{2,6},{3,7},{4,0},{5,1},{6,2},{7,3},{8,12},{9,13},{10,... | collective-permute-start | bytes 331784 | tf_op jit(solution)/shard_map/ppermute | solution.py:473
  48.7 0.5 collective-permute-start.13
  49.1 1.5 %collective-permute-done.11.refs_1_ = bf16[2,216,128]{2,1,0:T(8,128)(2,1)S(1)} collective-permute-done((bf16[2,216,128]{2,1,0:T(8,128)(2,1)S(1)}, bf16[2,216,128]{2,1,0:T(8,128)(2,1)S(1)}, u32[]{:S(2)}, u32[]{:S(2)}) %collective-permute-start.11) | collective-permute-done | bytes 110624 | tf_op jit(solution)/shard_map/ppermute | solution.py:473
  50.6 1.9 %collective-permute-done.12.refs_2_ = bf16[2,216,128]{2,1,0:T(8,128)(2,1)S(1)} collective-permute-done((bf16[2,216,128]{2,1,0:T(8,128)(2,1)S(1)}, bf16[2,216,128]{2,1,0:T(8,128)(2,1)S(1)}, u32[]{:S(2)}, u32[]{:S(2)}) %collective-permute-start.12) | collective-permute-done | bytes 110624 | tf_op jit(solution)/shard_map/ppermute | solution.py:473
  52.5 2.3 %collective-permute-done.13.refs_3_ = bf16[2,216,128]{2,1,0:T(8,128)(2,1)S(1)} collective-permute-done((bf16[2,216,128]{2,1,0:T(8,128)(2,1)S(1)}, bf16[2,216,128]{2,1,0:T(8,128)(2,1)S(1)}, u32[]{:S(2)}, u32[]{:S(2)}) %collective-permute-start.13) | collective-permute-done | bytes 110624 | tf_op jit(solution)/shard_map/ppermute | solution.py:473
  54.8 0.1 reduce.1
  54.9 3.3 %collective-permute-start.14 = (bf16[216,128]{1,0:T(8,128)(2,1)S(1)}, bf16[216,128]{1,0:T(8,128)(2,1)S(1)}, u32[]{:S(2)}, u32[]{:S(2)}) collective-permute-start(bf16[216,128]{1,0:T(8,128)(2,1)S(1)} %get-tuple-element.81), channel_id=1, source_target_pairs={{0,8},{1,9},{2,10},{3,11},{4,12},{5,13},{6,14},{7,15},{8,0},{9,1},... | collective-permute-start | bytes 165896 | tf_op jit(solution)/shard_map/ppermute | solution.py:473
  58.2 2.4 %collective-permute-done.14.part_ref = bf16[216,128]{1,0:T(8,128)(2,1)S(1)} collective-permute-done((bf16[216,128]{1,0:T(8,128)(2,1)S(1)}, bf16[216,128]{1,0:T(8,128)(2,1)S(1)}, u32[]{:S(2)}, u32[]{:S(2)}) %collective-permute-start.14) | collective-permute-done | bytes 55328 | tf_op jit(solution)/shard_map/ppermute | solution.py:473
  60.7 0.0 copy-done.3
  60.7 0.0 copy-done.4
  60.7 0.8 %finish.1 = (f32[1,128,128]{2,1,0:T(8,128)}, f32[1,64,128]{2,1,0:T(8,128)}, f32[1,128]{1,0:T(1,128)}, f32[1,16,128]{2,1,0:T(8,128)}) custom-call(f32[216,128]{1,0:T(8,128)S(1)} %get-tuple-element.80.keep_ref, bf16[216,128]{1,0:T(8,128)(2,1)S(1)} %collective-permute-done.14.part_ref, bf16[1,16,128]{2,1,0:T(8,128)(2,1)S(1)} %copy-done.4, ...), custom_call_target="tpu_custom_call" | custom-call | tf_op jit(solution)/shard_map/finish/pallas_call | solution.py:589
  (1 shorter events, 0.0 us)
Async XLA Ops:
  0.6 60.0 %copy-start.3 = (bf16[1,128,128]{2,1,0:T(8,128)(2,1)S(1)}, bf16[1,128,128]{2,1,0:T(8,128)(2,1)}, u32[]{:S(2)}) copy-start(bf16[1,128,128]{2,1,0:T(8,128)(2,1)} %wh_ref.1) | copy-start | bytes 98308
  0.6 60.0 %copy-start.4 = (bf16[1,16,128]{2,1,0:T(8,128)(2,1)S(1)}, bf16[1,16,128]{2,1,0:T(8,128)(2,1)}, u32[]{:S(2)}) copy-start(bf16[1,16,128]{2,1,0:T(8,128)(2,1)} %samp_ref.1) | copy-start | bytes 12292
  2.8 9.4 %collective-permute-start = (bf16[400,128]{1,0:T(8,128)(2,1)}, bf16[400,128]{1,0:T(8,128)(2,1)S(1)}, u32[]{:S(2)}, u32[]{:S(2)}) collective-permute-start(bf16[400,128]{1,0:T(8,128)(2,1)} %get-tuple-element.45), channel_id=1, source_target_pairs={{0,8},{1,9},{2,10},{3,11},{4,12},{5,13},{6,14},{7,15},{8,0},{9,1},... | collective-permute-start | bytes 307208 | tf_op jit(solution)/shard_map/ppermute | solution.py:473
  6.9 1.0 %copy-start = (bf16[576,384]{1,0:T(8,128)(2,1)S(1)}, bf16[576,384]{1,0:T(8,128)(2,1)}, u32[]{:S(2)}) copy-start(bf16[576,384]{1,0:T(8,128)(2,1)} %decoder_ref.1) | copy-start | bytes 1327108
  7.9 0.9 %copy-start.1 = (bf16[4,256,128]{2,1,0:T(8,128)(2,1)S(1)}, bf16[4,256,128]{2,1,0:T(8,128)(2,1)}, u32[]{:S(2)}) copy-start(bf16[4,256,128]{2,1,0:T(8,128)(2,1)} %get-tuple-element.46.near_ref) | copy-start | bytes 786436
  8.9 0.9 %copy-start.2 = (bf16[256,384]{1,0:T(8,128)(2,1)S(1)}, bf16[256,384]{1,0:T(8,128)(2,1)}, u32[]{:S(2)}) copy-start(bf16[256,384]{1,0:T(8,128)(2,1)} %target_ref.1) | copy-start | bytes 589828
  12.3 5.4 %collective-permute-start.1 = (bf16[2,256,128]{2,1,0:T(8,128)(2,1)S(1)}, bf16[2,256,128]{2,1,0:T(8,128)(2,1)S(1)}, u32[]{:S(2)}, u32[]{:S(2)}) collective-permute-start(bf16[2,256,128]{2,1,0:T(8,128)(2,1)S(1)} %get-tuple-element.54), channel_id=1, source_target_pairs={{0,2},{1,3},{2,0},{3,1},{4,6},{5,7},{6,4},{7,5},{8,10},{9,11},{10,... | collective-permute-start | bytes 393224 | tf_op jit(solution)/shard_map/ppermute | solution.py:473
  13.9 5.6 %collective-permute-start.2 = (bf16[2,256,128]{2,1,0:T(8,128)(2,1)S(1)}, bf16[2,256,128]{2,1,0:T(8,128)(2,1)S(1)}, u32[]{:S(2)}, u32[]{:S(2)}) collective-permute-start(bf16[2,256,128]{2,1,0:T(8,128)(2,1)S(1)} %get-tuple-element.55), channel_id=1, source_target_pairs={{0,4},{1,5},{2,6},{3,7},{4,0},{5,1},{6,2},{7,3},{8,12},{9,13},{10,... | collective-permute-start | bytes 393224 | tf_op jit(solution)/shard_map/ppermute | solution.py:473
  14.6 6.9 %collective-permute-start.3 = (bf16[2,256,128]{2,1,0:T(8,128)(2,1)S(1)}, bf16[2,256,128]{2,1,0:T(8,128)(2,1)S(1)}, u32[]{:S(2)}, u32[]{:S(2)}) collective-permute-start(bf16[2,256,128]{2,1,0:T(8,128)(2,1)S(1)} %get-tuple-element.56), channel_id=1, source_target_pairs={{0,6},{1,7},{2,4},{3,5},{4,2},{5,3},{6,0},{7,1},{8,14},{9,15},{10,... | collective-permute-start | bytes 393224 | tf_op jit(solution)/shard_map/ppermute | solution.py:473
  15.8 5.8 %collective-permute-start.4 = (bf16[2,256,128]{2,1,0:T(8,128)(2,1)S(1)}, bf16[2,256,128]{2,1,0:T(8,128)(2,1)S(1)}, u32[]{:S(2)}, u32[]{:S(2)}) collective-permute-start(bf16[2,256,128]{2,1,0:T(8,128)(2,1)S(1)} %get-tuple-element.53.refs_0_), channel_id=1, source_target_pairs={{0,1},{1,0},{2,3},{3,2},{4,5},{5,4},{6,7},{7,6},{8,9},{9,8},{10,11... | collective-permute-start | bytes 393224 | tf_op jit(solution)/shard_map/ppermute | solution.py:519
  17.6 3.9 %collective-permute-start.5 = (bf16[2,256,128]{2,1,0:T(8,128)(2,1)S(1)}, bf16[2,256,128]{2,1,0:T(8,128)(2,1)S(1)}, u32[]{:S(2)}, u32[]{:S(2)}) collective-permute-start(bf16[2,256,128]{2,1,0:T(8,128)(2,1)S(1)} %collective-permute-done.1.refs_1_), channel_id=1, source_target_pairs={{0,1},{1,0},{2,3},{3,2},{4,5},{5,4},{6,7},{7,6},{8,9},{9,8},{10,11... | collective-permute-start | bytes 393224 | tf_op jit(solution)/shard_map/ppermute | solution.py:519
  19.5 2.1 %collective-permute-start.6 = (bf16[2,256,128]{2,1,0:T(8,128)(2,1)S(1)}, bf16[2,256,128]{2,1,0:T(8,128)(2,1)S(1)}, u32[]{:S(2)}, u32[]{:S(2)}) collective-permute-start(bf16[2,256,128]{2,1,0:T(8,128)(2,1)S(1)} %collective-permute-done.2.refs_2_), channel_id=1, source_target_pairs={{0,1},{1,0},{2,3},{3,2},{4,5},{5,4},{6,7},{7,6},{8,9},{9,8},{10,11... | collective-permute-start | bytes 393224 | tf_op jit(solution)/shard_map/ppermute | solution.py:519
  21.6 1.3 %collective-permute-start.7 = (bf16[2,256,128]{2,1,0:T(8,128)(2,1)S(1)}, bf16[2,256,128]{2,1,0:T(8,128)(2,1)S(1)}, u32[]{:S(2)}, u32[]{:S(2)}) collective-permute-start(bf16[2,256,128]{2,1,0:T(8,128)(2,1)S(1)} %collective-permute-done.3.refs_3_), channel_id=1, source_target_pairs={{0,1},{1,0},{2,3},{3,2},{4,5},{5,4},{6,7},{7,6},{8,9},{9,8},{10,11... | collective-permute-start | bytes 393224 | tf_op jit(solution)/shard_map/ppermute | solution.py:519
  27.9 1.4 %collective-permute-start.8 = (bf16[256,256]{1,0:T(8,128)(2,1)S(1)}, bf16[256,256]{1,0:T(8,128)(2,1)S(1)}, u32[]{:S(2)}, u32[]{:S(2)}) collective-permute-start(bf16[256,256]{1,0:T(8,128)(2,1)S(1)} %get-tuple-element.59), channel_id=1, source_target_pairs={{0,1},{1,0},{2,3},{3,2},{4,5},{5,4},{6,7},{7,6},{8,9},{9,8},{10,11... | collective-permute-start | bytes 393224 | tf_op jit(solution)/shard_map/ppermute | solution.py:553
  28.1 1.2 %collective-permute-start.9 = (bf16[256,256]{1,0:T(8,128)(2,1)S(1)}, bf16[256,256]{1,0:T(8,128)(2,1)S(1)}, u32[]{:S(2)}, u32[]{:S(2)}) collective-permute-start(bf16[256,256]{1,0:T(8,128)(2,1)S(1)} %get-tuple-element.60), channel_id=1, source_target_pairs={{1,2},{3,4},{5,6},{7,8},{9,10},{11,12},{13,14},{2,1},{4,3},{6,5},{... | collective-permute-start | bytes 393224 | tf_op jit(solution)/shard_map/ppermute | solution.py:554
  38.2 6.9 %collective-permute-start.10 = (bf16[8,216,128]{2,1,0:T(8,128)(2,1)S(1)}, bf16[8,216,128]{2,1,0:T(8,128)(2,1)S(1)}, u32[]{:S(2)}, u32[]{:S(2)}) collective-permute-start(bf16[8,216,128]{2,1,0:T(8,128)(2,1)S(1)} %get-tuple-element.75), channel_id=1, source_target_pairs={{0,1},{1,0},{2,3},{3,2},{4,5},{5,4},{6,7},{7,6},{8,9},{9,8},{10,11... | collective-permute-start | bytes 1327112 | tf_op jit(solution)/shard_map/ppermute | solution.py:576
  45.2 5.4 %collective-permute-start.11 = (bf16[2,216,128]{2,1,0:T(8,128)(2,1)S(1)}, bf16[2,216,128]{2,1,0:T(8,128)(2,1)S(1)}, u32[]{:S(2)}, u32[]{:S(2)}) collective-permute-start(bf16[2,216,128]{2,1,0:T(8,128)(2,1)S(1)} %get-tuple-element.77), channel_id=1, source_target_pairs={{0,2},{1,3},{2,0},{3,1},{4,6},{5,7},{6,4},{7,5},{8,10},{9,11},{10,... | collective-permute-start | bytes 331784 | tf_op jit(solution)/shard_map/ppermute | solution.py:473
  47.0 5.5 %collective-permute-start.12 = (bf16[2,216,128]{2,1,0:T(8,128)(2,1)S(1)}, bf16[2,216,128]{2,1,0:T(8,128)(2,1)S(1)}, u32[]{:S(2)}, u32[]{:S(2)}) collective-permute-start(bf16[2,216,128]{2,1,0:T(8,128)(2,1)S(1)} %get-tuple-element.78), channel_id=1, source_target_pairs={{0,4},{1,5},{2,6},{3,7},{4,0},{5,1},{6,2},{7,3},{8,12},{9,13},{10,... | collective-permute-start | bytes 331784 | tf_op jit(solution)/shard_map/ppermute | solution.py:473
  48.7 6.1 %collective-permute-start.13 = (bf16[2,216,128]{2,1,0:T(8,128)(2,1)S(1)}, bf16[2,216,128]{2,1,0:T(8,128)(2,1)S(1)}, u32[]{:S(2)}, u32[]{:S(2)}) collective-permute-start(bf16[2,216,128]{2,1,0:T(8,128)(2,1)S(1)} %get-tuple-element.79), channel_id=1, source_target_pairs={{0,6},{1,7},{2,4},{3,5},{4,2},{5,3},{6,0},{7,1},{8,14},{9,15},{10,... | collective-permute-start | bytes 331784 | tf_op jit(solution)/shard_map/ppermute | solution.py:473
  54.9 5.8 %collective-permute-start.14 = (bf16[216,128]{1,0:T(8,128)(2,1)S(1)}, bf16[216,128]{1,0:T(8,128)(2,1)S(1)}, u32[]{:S(2)}, u32[]{:S(2)}) collective-permute-start(bf16[216,128]{1,0:T(8,128)(2,1)S(1)} %get-tuple-element.81), channel_id=1, source_target_pairs={{0,8},{1,9},{2,10},{3,11},{4,12},{5,13},{6,14},{7,15},{8,0},{9,1},... | collective-permute-start | bytes 165896 | tf_op jit(solution)/shard_map/ppermute | solution.py:473

commit v5 on v4

--- a/solution.py
+++ b/solution.py
@@ -90,22 +90,21 @@
         codes = codes_ref[pl.ds(pl.multiple_of(chip * room, 16), room), :]
         return jnp.where(first, density, here).astype(BF16), codes
 
-    for ref in [near_ref.at[k] for k in range(half // 2)] + [far_ref]:
+    for side, ref in enumerate((near_ref, far_ref)):
         ref[0:WF_AT] = wh_t
         ref[WF_AT:SAMPLE_AT] = wf_ref[0]
         ref[SAMPLE_AT:META_AT] = samp_ref[0]
-    for k in range(half // 2):
-        near_ref[k, META_AT:RAYS_AT], near_ref[k, RAYS_AT:] = rays_for(k)
-        at = META_AT + k * (16 + room)
-        far_ref[at : at + 16], far_ref[at + 16 : at + 16 + room] = rays_for(k + half // 2)
+        for k in range(half // 2):
+            at = META_AT + k * (16 + room)
+            ref[at : at + 16], ref[at + 16 : at + 16 + room] = rays_for(k + side * (half // 2))
 
 
 def relay_kernel(near_ref, far_ref, *outs):
     for k, out in enumerate(outs):
-        out[0] = near_ref[k]
-        out[1, 0:META_AT] = far_ref[0:META_AT]
-        rows = near_ref.shape[1] - META_AT
-        out[1, META_AT:] = far_ref[META_AT + k * rows : META_AT + (k + 1) * rows]
+        rows = out.shape[1] - META_AT
+        for side, ref in enumerate((near_ref, far_ref)):
+            out[side, 0:META_AT] = ref[0:META_AT]
+            out[side, META_AT:] = ref[META_AT + k * rows : META_AT + (k + 1) * rows]
 
 
 def bits_of(row, regions):
@@ -118,6 +117,52 @@
     for bit in bits:
         values = [jnp.where(bit, values[i + 1], values[i]) for i in range(0, len(values), 2)]
     return values[0]
+
+
+def fold(source_ref, rel_ref, out_ref):
+    segs, rays = rel_ref.shape
+    regions = out_ref.shape[0]
+
+    def step(pair, carry):
+        rows = pl.ds(pl.multiple_of(pair * 16, 16), 16)
+        for part in range(rays // LANES):
+            lanes = slice(part * LANES, (part + 1) * LANES)
+            rel = [jnp.broadcast_to(rel_ref[k : k + 1, lanes], (16, LANES)) for k in range(segs)]
+            held = [source_ref[rows, k * rays + part * LANES : k * rays + (part + 1) * LANES] for k in range(segs)]
+            for r in range(regions):
+                total = jnp.where(rel[0] == r, held[0], 0.0)
+                for k in range(1, segs):
+                    total = jnp.where(rel[k] == r, held[k], total)
+                out_ref[r, rows, lanes] = total.astype(BF16)
+        return carry
+
+    lax.fori_loop(0, source_ref.shape[0] // 16, step, 0, unroll=2)
+
+
+def fold_kernel(source_ref, rel_ref, out_ref):
+    fold(source_ref, rel_ref, out_ref)
+
+
+def pick(source_ref, rel_ref, out_ref, first=0):
+    segs, rays = rel_ref.shape
+    regions = source_ref.shape[0]
+    for part in range(rays // LANES):
+        lanes = slice(part * LANES, (part + 1) * LANES)
+
+        def step(index, carry):
+            rows = pl.ds(pl.multiple_of(index * 8, 8), 8)
+            bits = [bits_of(rel_ref[k : k + 1, lanes], regions) for k in range(segs)]
+            values = [source_ref[r, rows, lanes] for r in range(regions)]
+            for k in range(segs):
+                found = choose(values, bits[k])
+                at = slice(k * rays + part * LANES, k * rays + (part + 1) * LANES)
+                if first > 0:
+                    here = lax.shift_right_logical(rel_ref[k : k + 1, lanes], len(bits[k])) == first // regions
+                    found = jnp.where(here, found, out_ref[rows, at])
+                out_ref[rows, at] = found
+            return carry
+
+        lax.fori_loop(0, source_ref.shape[1] // 8, step, 0, unroll=4)
 
 
 def seg_hot(wanted, regions):
@@ -132,8 +177,8 @@
     received, target_ref = refs[:half], refs[half]
     blocks = [received[c * quarter + k].at[side] for c in range(2) for side in range(2) for k in range(quarter)]
     (
-        image_ref, halo_in_ref, halo_cr_ref, h_ref, wd_ref, att_hw_ref, wide_hw_ref, weight_ref, pass_ref, slope_ref, att_ref, rel_ref, codes_ref, wf_out,
-        meta_ref, plain_ref, table_ref, proj_ref, a_ref, picked_ref, row_ref, density_ref,
+        image_ref, halo_in_ref, halo_cr_ref, h_ref, wd_ref, att_hw_ref, weight_ref, pass_ref, slope_ref, att_ref, rel_ref, codes_ref, wf_up,
+        wide_hw_ref, wf_out,        meta_ref, plain_ref, table_ref, proj_ref, a_ref, picked_ref, row_ref, density_ref,
     ) = refs[half + 1 :]
     rays = codes_ref.shape[1]
     segs = rel_ref.shape[0]
@@ -175,21 +220,11 @@
         plain_ref[0:samples, r, :] = dot(block[SAMPLE_AT:META_AT], w_t, 1, 1)
         plain_ref[samples, r : r + 1, :] = block[META_AT:RAYS_AT].astype(F32)[0:1, :]
         wf_out[r * feats : (r + 1) * feats] = block[WF_AT:SAMPLE_AT]
+        wf_up[r] = block[WF_AT:SAMPLE_AT].astype(F32).T.astype(BF16)
     for s in range(samples + 1):
         high, low = split(plain_ref[s])
         table_ref[s] = jnp.concatenate([high.astype(F32), low.astype(F32)], axis=0).T.astype(BF16)
-    for part in range(2):
-        lanes = slice(part * LANES, (part + 1) * LANES)
-
-        def pick_rows(index, carry):
-            rows = pl.ds(pl.multiple_of(index * 8, 8), 8)
-            bits = [bits_of(row[:, lanes], regions) for row in wanted]
-            values = [proj_ref[r, rows, lanes] for r in range(regions)]
-            for k in range(segs):
-                a_ref[2 * k + part, rows, :] = choose(values, bits[k])
-            return carry
-
-        lax.fori_loop(0, 16, pick_rows, 0, unroll=4)
+    pick(proj_ref, rel_ref, a_ref)
     hot = seg_hot(wanted, regions).astype(BF16)
     hot2 = jnp.concatenate([hot, hot], axis=0)
     for tile in range(2 * segs):
@@ -197,13 +232,13 @@
 
     def densities(tile, carry):
         here = picked_ref[tile]
+        lanes = pl.ds(pl.multiple_of(tile * LANES, LANES), LANES)
         wd_ref[tile] = dot(table_ref[samples], here)
         sums = []
         for s in range(samples):
-            h = jnp.maximum(a_ref[tile] + dot(table_ref[s], here), 0.0)
+            h = jnp.maximum(a_ref[:, lanes] + dot(table_ref[s], here), 0.0)
             h_ref[tile, s] = h
             sums.append(jnp.sum(h * wd_ref[tile], axis=0, keepdims=True))
-        lanes = pl.ds(pl.multiple_of(tile * LANES, LANES), LANES)
         density_ref[:, lanes] = jnp.concatenate(sums, axis=0)
         return carry
 
@@ -281,16 +316,15 @@
 
 def backward_kernel(
     half, own_ref, inner_ref, cross_ref, tgt_ref, dec_ref, dect_ref,
-    h_in, wd_ref, att_hw_ref, wide_hw_ref, weight_ref, pass_ref, slope_ref, att_ref, rel_ref, codes_ref, wf_ref,
+    folded_ref, h_in, wd_ref, att_hw_ref, weight_ref, pass_ref, slope_ref, att_ref, rel_ref, codes_ref, wf_ref,
     mine_ref, other_ref,
-    patch_ref, masked_ref, q_ref, gp_ref, g1_ref, hd_ref, tail_ref, row_ref, along_ref, hot_ref,
+    patch_ref, proj_ref, q_ref, gp_ref, g1_ref, held_ref, hd_ref, tail_ref, row_ref, along_ref,
 ):
     regions = 2 * half
     feats, rays = own_ref.shape
     segs = rel_ref.shape[0]
     samples = weight_ref.shape[0]
     hids = wd_ref.shape[1]
-    unroll = min(regions, 16)
     me = lax.axis_index("region")
     core = me & 1
     own = own_ref[...].astype(F32)
@@ -328,26 +362,15 @@
         image_rows.append(total)
     grad_ray = jnp.concatenate(image_rows, axis=1)
     wanted = [rel_ref[k : k + 1, :] for k in range(segs)]
-    hot = seg_hot(wanted, regions)
+    hot = seg_hot(wanted, regions).astype(BF16)
+    grad_narrow = grad_ray.astype(BF16)
+    group = proj_ref.shape[0]
     for r in range(regions):
-        hot_ref[r] = jnp.broadcast_to(hot[r : r + 1], (16, segs * rays)).astype(BF16)
-    hot = hot.astype(BF16)
-    grad_narrow = grad_ray.astype(BF16)
-
-    def mask_grads(r, carry):
-        for k in range(segs):
-            mask = hot_ref[r, :, k * rays : (k + 1) * rays]
-            for at in range(0, feats, 16):
-                rows = pl.ds(pl.multiple_of(r * feats + at, 16), 16)
-                masked_ref[rows, k * rays : (k + 1) * rays] = grad_narrow[at : at + 16] * mask
-        return carry
-
-    lax.fori_loop(0, regions, mask_grads, 0, unroll=unroll)
-    q_ref[...] = dot(wf_ref[...], masked_ref[...], 0, 0)
-    feat_grad = dot(masked_ref[...], wide_hw_ref[0:hids], 1, 1).astype(BF16)
-    for r in range(regions):
+        proj_ref[r % group] = dot(wf_ref[r], grad_narrow)
         out, to = (mine_ref, r) if r < half else (other_ref, r - half)
-        out[to, WF_AT:G2_AT] = feat_grad[r * feats : (r + 1) * feats]
+        out[to, WF_AT:G2_AT] = dot(grad_narrow, folded_ref[r], 1, 1).astype(BF16)
+        if (r + 1) % group == 0:
+            pick(proj_ref, rel_ref, q_ref, r + 1 - group)
     later = jnp.zeros((1, rays), F32)
     for k in reversed(range(segs)):
         lanes = slice(k * rays, (k + 1) * rays)
@@ -395,7 +418,7 @@
                     hd[u] = hd[u] + slant[s] * h
                     both.append(gp)
                 gp_ref[s * hids + 16 * pair : s * hids + 16 * pair + 16, lanes] = jnp.concatenate(both, axis=0).astype(BF16)
-            g1_ref[16 * pair : 16 * pair + 16, lanes] = jnp.concatenate(g1, axis=0).astype(BF16)
+            g1_ref[16 * pair : 16 * pair + 16, lanes] = jnp.concatenate(g1, axis=0)
             hd_ref[16 * pair : 16 * pair + 16, lanes] = jnp.concatenate(hd, axis=0).astype(BF16)
         return carry
 
@@ -404,12 +427,11 @@
     for s in range(samples):
         tail_ref[:, s, :] = dot(hot, gp_ref[s * hids : (s + 1) * hids], 1, 1)
     tail_ref[:, samples, :] = dot(hot, hd_ref[...], 1, 1)
-    codes = codes_ref[...].astype(F32)
-    g1 = g1_ref[...]
+    codes = codes_ref[...]
+    fold(g1_ref, rel_ref, held_ref)
     for r in range(regions):
         out, to = (mine_ref, r) if r < half else (other_ref, r - half)
-        held = jnp.concatenate([jnp.where(row == r, codes, 0.0).astype(BF16) for row in wanted], axis=1)
-        out[to, 0:WF_AT] = dot(held, g1, 1, 1).astype(BF16)
+        out[to, 0:WF_AT] = dot(codes, held_ref[r], 1, 1).astype(BF16)
         out[to, G2_AT:PART_ROWS] = tail_ref[r].astype(BF16)
 
 
@@ -482,7 +504,7 @@
     near, far = pl.pallas_call(
         functools.partial(pack_kernel, half, group, room),
         out_shape=(
-            shape(quarter, pack_rows, LANES, kind=BF16),
+            shape(META_AT + quarter * (16 + room), LANES, kind=BF16),
             shape(META_AT + quarter * (16 + room), LANES, kind=BF16),
         ),
         in_specs=[pl.BlockSpec(memory_space=pltpu.HBM)] * 8,
@@ -527,21 +549,22 @@
             shape(tiles, samples, hid_width, LANES),
             shape(tiles, hid_width, LANES),
             shape(hid_width, lanes),
-            shape(2 * hid_width, lanes, kind=BF16),
             shape(samples, lanes),
             shape(samples, lanes),
             shape(samples, lanes),
             shape(1, lanes),
             shape(segs, rays, kind=jnp.int32),
             shape(code_width, rays, kind=BF16),
-            shape(regions * feat_width, hid_width, kind=BF16),
+            shape(regions, hid_width, feat_width, kind=BF16),
         ),
         scratch_shapes=[
+            pltpu.VMEM((2 * hid_width, lanes), BF16),
+            pltpu.VMEM((regions * feat_width, hid_width), BF16),
             pltpu.VMEM((16, regions * room), F32),
             pltpu.VMEM((samples + 1, regions, hid_width), F32),
             pltpu.VMEM((samples + 1, hid_width, 2 * regions), BF16),
             pltpu.VMEM((regions, hid_width, rays), F32),
-            pltpu.VMEM((tiles, hid_width, LANES), F32),
+            pltpu.VMEM((hid_width, lanes), F32),
             pltpu.VMEM((tiles, 2 * regions, LANES), BF16),
             pltpu.VMEM((1, lanes), F32),
             pltpu.VMEM((samples, lanes), F32),
@@ -552,6 +575,12 @@
 
     halo_in = lax.ppermute(halo_in, "region", inner)
     halo_cr = lax.ppermute(halo_cr, "region", cross)
+    folded = pl.pallas_call(
+        fold_kernel,
+        out_shape=shape(regions, hid_width, rays, kind=BF16),
+        compiler_params=grant(8 + regions / 4),
+        name="fold",
+    )(kept[2], kept[7])
 
     part = shape(half, PART_ROWS, LANES, kind=BF16)
     mine, other = pl.pallas_call(
@@ -559,19 +588,19 @@
         out_shape=(part, part),
         scratch_shapes=[
             pltpu.VMEM((decoder.shape[0], 4 * IW), BF16),
-            pltpu.VMEM((regions * feat_width, lanes), BF16),
+            pltpu.VMEM((min(regions, 16), hid_width, rays), F32),
             pltpu.VMEM((hid_width, lanes), F32),
             pltpu.VMEM((samples * hid_width, lanes), BF16),
-            pltpu.VMEM((hid_width, lanes), BF16),
+            pltpu.VMEM((hid_width, lanes), F32),
+            pltpu.VMEM((regions, hid_width, rays), BF16),
             pltpu.VMEM((hid_width, lanes), BF16),
             pltpu.VMEM((regions, PART_ROWS - G2_AT, hid_width), F32),
             pltpu.VMEM((1, lanes), F32),
             pltpu.VMEM((samples, lanes), F32),
-            pltpu.VMEM((regions, 16, lanes), BF16),
         ],
         compiler_params=grant(22 + regions / 4),
         name="backward",
-    )(image, halo_in, halo_cr, target_t, decoder, decoder_t, *kept)
+    )(image, halo_in, halo_cr, target_t, decoder, decoder_t, folded, *kept)
 
     theirs = lax.ppermute(other, "region", inner)
     parts = pl.pallas_call(

time: 61.8 us -> 60.5 us (0.979)
  Pallas kernels: 17.3 us -> 16.6 us
    pallas_call x1, Pallas kernels: 8.83 us -> 7.71 us  [local(): pl.pallas_call(functools.partial(backward_kernel, half), out_shape=(part,...]
  transfers between devices with their start and end apart: 15 -> 15, of which waited for: 11 -> 10; matrix products, arithmetic and copies ran while one was open for 0% -> 0% of each run, Pallas kernels for 0% -> 1%
where the time goes in v5:
time: 60.5 us; the launch traced here: 60.2 us
  starting transfers between devices  21.3 us (35%)
  waiting for transfers between devices  18.8 us (31%)
  Pallas kernels  16.6 us (27%)
  local copies, waits for them, and re-layouts  2.84 us (5%)
  between operations  0.73 us (1%)
    ppermute x8, waiting for transfers between devices, to_chip(): lax.ppermute(block, 'region', [(i, i ^ 2 * k) for i in range(regions)])  16 us
    ppermute x8, starting transfers between devices, to_chip(): lax.ppermute(block, 'region', [(i, i ^ 2 * k) for i in range(regions)])  14.9 us
    pallas_call x1, Pallas kernels, local(): pl.pallas_call(functools.partial(backward_kernel, half), out_shape=(part,...  7.71 us
    ppermute x1, starting transfers between devices, local(): theirs = lax.ppermute(other, 'region', inner)  5.47 us
    pallas_call x1, Pallas kernels, local(): pl.pallas_call(functools.partial(forward_kernel, half, group, room), out_...  4.92 us
    unnamed x10, local copies, waits for them, and re-layouts  2.84 us
    pallas_call x1, Pallas kernels, local(): pl.pallas_call(functools.partial(pack_kernel, half, group, room), out_sha...  2.11 us
    ppermute x1, waiting for transfers between devices, local(): theirs = lax.ppermute(other, 'region', inner)  1.42 us
  transfers between devices with their start and end apart: 15, of which 10 were waited for; matrix products, arithmetic and copies ran while one was open for 0% of the time, Pallas kernels for 1%

profile of v5, /device:TPU:0, one launch (start us, length us, event | category | flops | bytes accessed | tf_op | source)
XLA Modules:
  0.0 60.2 jit_solution(13442477767297543999)
XLA Ops:
  0.6 2.1 %pack.1 = (bf16[400,128]{1,0:T(8,128)(2,1)}, bf16[400,128]{1,0:T(8,128)(2,1)}) custom-call(s32[1,256]{1,0:T(1,128)} %bitcast.8, s32[4,256]{1,0:T(4,128)} %bitcast.6, s32[4,256]{1,0:T(4,128)} %bitcast.7, bf16[256,128]{1,0:T(8,128)(2,1)} %refs_3_.1, bf16[1,16,128]{2,1,0:T(8,128)(2,1)} %samp_ref.1, bf16[1,128,128]{2,1,0:T(8,128)(2,1)} %wh_ref.1, ...), custom_call_target="tpu_custom_call" | custom-call | tf_op jit(solution)/shard_map/pack/pallas_call | solution.py:504
  2.7 4.1 %collective-permute-start = (bf16[400,128]{1,0:T(8,128)(2,1)}, bf16[400,128]{1,0:T(8,128)(2,1)S(1)}, u32[]{:S(2)}, u32[]{:S(2)}) collective-permute-start(bf16[400,128]{1,0:T(8,128)(2,1)} %get-tuple-element.44), channel_id=1, source_target_pairs={{0,8},{1,9},{2,10},{3,11},{4,12},{5,13},{6,14},{7,15},{8,0},{9,1},... | collective-permute-start | bytes 307208 | tf_op jit(solution)/shard_map/ppermute | solution.py:495
  6.8 0.0 copy-start
  6.9 1.0 %copy-done = bf16[576,384]{1,0:T(8,128)(2,1)S(1)} copy-done((bf16[576,384]{1,0:T(8,128)(2,1)S(1)}, bf16[576,384]{1,0:T(8,128)(2,1)}, u32[]{:S(2)}) %copy-start) | copy-done | bytes 442392
  7.9 0.0 copy-start.1
  7.9 0.9 %copy-done.1 = bf16[256,384]{1,0:T(8,128)(2,1)S(1)} copy-done((bf16[256,384]{1,0:T(8,128)(2,1)S(1)}, bf16[256,384]{1,0:T(8,128)(2,1)}, u32[]{:S(2)}) %copy-start.1) | copy-done | bytes 196632
  8.8 0.0 copy-start.3
  8.8 0.9 %copy-done.3 = bf16[400,128]{1,0:T(8,128)(2,1)S(1)} copy-done((bf16[400,128]{1,0:T(8,128)(2,1)S(1)}, bf16[400,128]{1,0:T(8,128)(2,1)}, u32[]{:S(2)}) %copy-start.3) | copy-done | bytes 102424
  9.7 0.3 flip.1
  10.0 2.2 %collective-permute-done.far_ref = bf16[400,128]{1,0:T(8,128)(2,1)S(1)} collective-permute-done((bf16[400,128]{1,0:T(8,128)(2,1)}, bf16[400,128]{1,0:T(8,128)(2,1)S(1)}, u32[]{:S(2)}, u32[]{:S(2)}) %collective-permute-start) | collective-permute-done | bytes 102432 | tf_op jit(solution)/shard_map/ppermute | solution.py:495
  12.1 0.1 relay.1
  12.2 1.6 %collective-permute-start.1 = (bf16[2,256,128]{2,1,0:T(8,128)(2,1)S(1)}, bf16[2,256,128]{2,1,0:T(8,128)(2,1)S(1)}, u32[]{:S(2)}, u32[]{:S(2)}) collective-permute-start(bf16[2,256,128]{2,1,0:T(8,128)(2,1)S(1)} %get-tuple-element.53), channel_id=1, source_target_pairs={{0,2},{1,3},{2,0},{3,1},{4,6},{5,7},{6,4},{7,5},{8,10},{9,11},{10,... | collective-permute-start | bytes 393224 | tf_op jit(solution)/shard_map/ppermute | solution.py:495
  13.8 0.8 %collective-permute-start.2 = (bf16[2,256,128]{2,1,0:T(8,128)(2,1)S(1)}, bf16[2,256,128]{2,1,0:T(8,128)(2,1)S(1)}, u32[]{:S(2)}, u32[]{:S(2)}) collective-permute-start(bf16[2,256,128]{2,1,0:T(8,128)(2,1)S(1)} %get-tuple-element.54), channel_id=1, source_target_pairs={{0,4},{1,5},{2,6},{3,7},{4,0},{5,1},{6,2},{7,3},{8,12},{9,13},{10,... | collective-permute-start | bytes 393224 | tf_op jit(solution)/shard_map/ppermute | solution.py:495
  14.6 1.2 %collective-permute-start.3 = (bf16[2,256,128]{2,1,0:T(8,128)(2,1)S(1)}, bf16[2,256,128]{2,1,0:T(8,128)(2,1)S(1)}, u32[]{:S(2)}, u32[]{:S(2)}) collective-permute-start(bf16[2,256,128]{2,1,0:T(8,128)(2,1)S(1)} %get-tuple-element.55), channel_id=1, source_target_pairs={{0,6},{1,7},{2,4},{3,5},{4,2},{5,3},{6,0},{7,1},{8,14},{9,15},{10,... | collective-permute-start | bytes 393224 | tf_op jit(solution)/shard_map/ppermute | solution.py:495
  15.8 0.0 copy-start.2
  15.8 0.0 copy-start.4
  15.8 0.0 collective-permute-start.4
  15.8 1.8 %collective-permute-done.1.refs_1_ = bf16[2,256,128]{2,1,0:T(8,128)(2,1)S(1)} collective-permute-done((bf16[2,256,128]{2,1,0:T(8,128)(2,1)S(1)}, bf16[2,256,128]{2,1,0:T(8,128)(2,1)S(1)}, u32[]{:S(2)}, u32[]{:S(2)}) %collective-permute-start.1) | collective-permute-done | bytes 131104 | tf_op jit(solution)/shard_map/ppermute | solution.py:495
  17.6 0.0 collective-permute-start.5
  17.6 1.8 %collective-permute-done.2.refs_2_ = bf16[2,256,128]{2,1,0:T(8,128)(2,1)S(1)} collective-permute-done((bf16[2,256,128]{2,1,0:T(8,128)(2,1)S(1)}, bf16[2,256,128]{2,1,0:T(8,128)(2,1)S(1)}, u32[]{:S(2)}, u32[]{:S(2)}) %collective-permute-start.2) | collective-permute-done | bytes 131104 | tf_op jit(solution)/shard_map/ppermute | solution.py:495
  19.4 0.0 collective-permute-start.6
  19.4 2.1 %collective-permute-done.3.refs_3_ = bf16[2,256,128]{2,1,0:T(8,128)(2,1)S(1)} collective-permute-done((bf16[2,256,128]{2,1,0:T(8,128)(2,1)S(1)}, bf16[2,256,128]{2,1,0:T(8,128)(2,1)S(1)}, u32[]{:S(2)}, u32[]{:S(2)}) %collective-permute-start.3) | collective-permute-done | bytes 131104 | tf_op jit(solution)/shard_map/ppermute | solution.py:495
  21.5 0.0 collective-permute-start.7
  21.5 0.0 collective-permute-done.4.refs_4_
  21.5 0.0 collective-permute-done.5.refs_5_
  21.5 0.0 collective-permute-done.6.refs_6_
  21.5 1.3 %collective-permute-done.7.refs_7_ = bf16[2,256,128]{2,1,0:T(8,128)(2,1)S(1)} collective-permute-done((bf16[2,256,128]{2,1,0:T(8,128)(2,1)S(1)}, bf16[2,256,128]{2,1,0:T(8,128)(2,1)S(1)}, u32[]{:S(2)}, u32[]{:S(2)}) %collective-permute-start.7) | collective-permute-done | bytes 131104 | tf_op jit(solution)/shard_map/ppermute | solution.py:541
  22.9 4.9 %forward.1 = (bf16[64,256]{1,0:T(8,128)(2,1)S(1)}, bf16[256,256]{1,0:T(8,128)(2,1)S(1)}, bf16[256,256]{1,0:T(8,128)(2,1)S(1)}, f32[8,16,128,128]{3,2,1,0:T(8,128...) custom-call(bf16[2,256,128]{2,1,0:T(8,128)(2,1)S(1)} %get-tuple-elem, ...), custom_call_target="tpu_custom_call" | custom-call | tf_op jit(solution)/shard_map/forward/pallas_call | solution.py:543
  27.8 0.2 collective-permute-start.8
  28.0 0.7 %collective-permute-start.9 = (bf16[256,256]{1,0:T(8,128)(2,1)S(1)}, bf16[256,256]{1,0:T(8,128)(2,1)S(1)}, u32[]{:S(2)}, u32[]{:S(2)}) collective-permute-start(bf16[256,256]{1,0:T(8,128)(2,1)S(1)} %get-tuple-element.59), channel_id=1, source_target_pairs={{1,2},{3,4},{5,6},{7,8},{9,10},{11,12},{13,14},{2,1},{4,3},{6,5},{... | collective-permute-start | bytes 393224 | tf_op jit(solution)/shard_map/ppermute | solution.py:577
  28.7 0.5 fold.1.folded_ref
  29.2 0.0 collective-permute-done.8.inner_ref
  29.2 0.0 collective-permute-done.9.cross_ref
  29.2 7.7 %backward.1 = (bf16[8,216,128]{2,1,0:T(8,128)(2,1)S(1)}, bf16[8,216,128]{2,1,0:T(8,128)(2,1)S(1)}) custom-call(bf16[64,256]{1,0:T(8,128)(2,1)S(1)} %get-tuple-element.57.own_ref, bf16[256,256]{1,0:T(8,128)(2,1)S(1)} %collective-permute-done.8.inner_ref, bf16[256,256]{1,0:T(8,128)(2,1)S(1)} %collective-permute-done.9.cross_ref, ...), custom_call_target="tpu_custom_call" | custom-call | tf_op jit(solution)/shard_map/backward/pallas_call | solution.py:586
  36.9 5.5 %collective-permute-start.10 = (bf16[8,216,128]{2,1,0:T(8,128)(2,1)S(1)}, bf16[8,216,128]{2,1,0:T(8,128)(2,1)S(1)}, u32[]{:S(2)}, u32[]{:S(2)}) collective-permute-start(bf16[8,216,128]{2,1,0:T(8,128)(2,1)S(1)} %get-tuple-element.73), channel_id=1, source_target_pairs={{0,1},{1,0},{2,3},{3,2},{4,5},{5,4},{6,7},{7,6},{8,9},{9,8},{10,11... | collective-permute-start | bytes 1327112 | tf_op jit(solution)/shard_map/ppermute | solution.py:605
  42.4 1.4 %collective-permute-done.10.theirs_ref = bf16[8,216,128]{2,1,0:T(8,128)(2,1)S(1)} collective-permute-done((bf16[8,216,128]{2,1,0:T(8,128)(2,1)S(1)}, bf16[8,216,128]{2,1,0:T(8,128)(2,1)S(1)}, u32[]{:S(2)}, u32[]{:S(2)}) %collective-permute-start.10) | collective-permute-done | bytes 442400 | tf_op jit(solution)/shard_map/ppermute | solution.py:605
  43.8 0.1 merge.1
  43.9 1.8 %collective-permute-start.11 = (bf16[2,216,128]{2,1,0:T(8,128)(2,1)S(1)}, bf16[2,216,128]{2,1,0:T(8,128)(2,1)S(1)}, u32[]{:S(2)}, u32[]{:S(2)}) collective-permute-start(bf16[2,216,128]{2,1,0:T(8,128)(2,1)S(1)} %get-tuple-element.75), channel_id=1, source_target_pairs={{0,2},{1,3},{2,0},{3,1},{4,6},{5,7},{6,4},{7,5},{8,10},{9,11},{10,... | collective-permute-start | bytes 331784 | tf_op jit(solution)/shard_map/ppermute | solution.py:495
  45.7 1.7 %collective-permute-start.12 = (bf16[2,216,128]{2,1,0:T(8,128)(2,1)S(1)}, bf16[2,216,128]{2,1,0:T(8,128)(2,1)S(1)}, u32[]{:S(2)}, u32[]{:S(2)}) collective-permute-start(bf16[2,216,128]{2,1,0:T(8,128)(2,1)S(1)} %get-tuple-element.76), channel_id=1, source_target_pairs={{0,4},{1,5},{2,6},{3,7},{4,0},{5,1},{6,2},{7,3},{8,12},{9,13},{10,... | collective-permute-start | bytes 331784 | tf_op jit(solution)/shard_map/ppermute | solution.py:495
  47.4 0.5 collective-permute-start.13
  47.9 1.5 %collective-permute-done.11.refs_1_ = bf16[2,216,128]{2,1,0:T(8,128)(2,1)S(1)} collective-permute-done((bf16[2,216,128]{2,1,0:T(8,128)(2,1)S(1)}, bf16[2,216,128]{2,1,0:T(8,128)(2,1)S(1)}, u32[]{:S(2)}, u32[]{:S(2)}) %collective-permute-start.11) | collective-permute-done | bytes 110624 | tf_op jit(solution)/shard_map/ppermute | solution.py:495
  49.3 1.8 %collective-permute-done.12.refs_2_ = bf16[2,216,128]{2,1,0:T(8,128)(2,1)S(1)} collective-permute-done((bf16[2,216,128]{2,1,0:T(8,128)(2,1)S(1)}, bf16[2,216,128]{2,1,0:T(8,128)(2,1)S(1)}, u32[]{:S(2)}, u32[]{:S(2)}) %collective-permute-start.12) | collective-permute-done | bytes 110624 | tf_op jit(solution)/shard_map/ppermute | solution.py:495
  51.2 2.4 %collective-permute-done.13.refs_3_ = bf16[2,216,128]{2,1,0:T(8,128)(2,1)S(1)} collective-permute-done((bf16[2,216,128]{2,1,0:T(8,128)(2,1)S(1)}, bf16[2,216,128]{2,1,0:T(8,128)(2,1)S(1)}, u32[]{:S(2)}, u32[]{:S(2)}) %collective-permute-start.13) | collective-permute-done | bytes 110624 | tf_op jit(solution)/shard_map/ppermute | solution.py:495
  53.5 0.1 reduce.1
  53.6 3.3 %collective-permute-start.14 = (bf16[216,128]{1,0:T(8,128)(2,1)S(1)}, bf16[216,128]{1,0:T(8,128)(2,1)S(1)}, u32[]{:S(2)}, u32[]{:S(2)}) collective-permute-start(bf16[216,128]{1,0:T(8,128)(2,1)S(1)} %get-tuple-element.79), channel_id=1, source_target_pairs={{0,8},{1,9},{2,10},{3,11},{4,12},{5,13},{6,14},{7,15},{8,0},{9,1},... | collective-permute-start | bytes 165896 | tf_op jit(solution)/shard_map/ppermute | solution.py:495
  56.9 2.5 %collective-permute-done.14.part_ref = bf16[216,128]{1,0:T(8,128)(2,1)S(1)} collective-permute-done((bf16[216,128]{1,0:T(8,128)(2,1)S(1)}, bf16[216,128]{1,0:T(8,128)(2,1)S(1)}, u32[]{:S(2)}, u32[]{:S(2)}) %collective-permute-start.14) | collective-permute-done | bytes 55328 | tf_op jit(solution)/shard_map/ppermute | solution.py:495
  59.4 0.0 copy-done.2
  59.4 0.0 copy-done.4
  59.4 0.8 %finish.1 = (f32[1,128,128]{2,1,0:T(8,128)}, f32[1,64,128]{2,1,0:T(8,128)}, f32[1,128]{1,0:T(1,128)}, f32[1,16,128]{2,1,0:T(8,128)}) custom-call(f32[216,128]{1,0:T(8,128)S(1)} %get-tuple-element.78.keep_ref, bf16[216,128]{1,0:T(8,128)(2,1)S(1)} %collective-permute-done.14.part_ref, bf16[1,16,128]{2,1,0:T(8,128)(2,1)S(1)} %copy-done.4, ...), custom_call_target="tpu_custom_call" | custom-call | tf_op jit(solution)/shard_map/finish/pallas_call | solution.py:618
Async XLA Ops:
  2.7 9.4 %collective-permute-start = (bf16[400,128]{1,0:T(8,128)(2,1)}, bf16[400,128]{1,0:T(8,128)(2,1)S(1)}, u32[]{:S(2)}, u32[]{:S(2)}) collective-permute-start(bf16[400,128]{1,0:T(8,128)(2,1)} %get-tuple-element.44), channel_id=1, source_target_pairs={{0,8},{1,9},{2,10},{3,11},{4,12},{5,13},{6,14},{7,15},{8,0},{9,1},... | collective-permute-start | bytes 307208 | tf_op jit(solution)/shard_map/ppermute | solution.py:495
  6.8 1.0 %copy-start = (bf16[576,384]{1,0:T(8,128)(2,1)S(1)}, bf16[576,384]{1,0:T(8,128)(2,1)}, u32[]{:S(2)}) copy-start(bf16[576,384]{1,0:T(8,128)(2,1)} %decoder_ref.1) | copy-start | bytes 1327108
  7.9 0.9 %copy-start.1 = (bf16[256,384]{1,0:T(8,128)(2,1)S(1)}, bf16[256,384]{1,0:T(8,128)(2,1)}, u32[]{:S(2)}) copy-start(bf16[256,384]{1,0:T(8,128)(2,1)} %target_ref.1) | copy-start | bytes 589828
  8.8 0.9 %copy-start.3 = (bf16[400,128]{1,0:T(8,128)(2,1)S(1)}, bf16[400,128]{1,0:T(8,128)(2,1)}, u32[]{:S(2)}) copy-start(bf16[400,128]{1,0:T(8,128)(2,1)} %get-tuple-element.45.near_ref) | copy-start | bytes 307204
  12.2 5.4 %collective-permute-start.1 = (bf16[2,256,128]{2,1,0:T(8,128)(2,1)S(1)}, bf16[2,256,128]{2,1,0:T(8,128)(2,1)S(1)}, u32[]{:S(2)}, u32[]{:S(2)}) collective-permute-start(bf16[2,256,128]{2,1,0:T(8,128)(2,1)S(1)} %get-tuple-element.53), channel_id=1, source_target_pairs={{0,2},{1,3},{2,0},{3,1},{4,6},{5,7},{6,4},{7,5},{8,10},{9,11},{10,... | collective-permute-start | bytes 393224 | tf_op jit(solution)/shard_map/ppermute | solution.py:495
  13.8 5.6 %collective-permute-start.2 = (bf16[2,256,128]{2,1,0:T(8,128)(2,1)S(1)}, bf16[2,256,128]{2,1,0:T(8,128)(2,1)S(1)}, u32[]{:S(2)}, u32[]{:S(2)}) collective-permute-start(bf16[2,256,128]{2,1,0:T(8,128)(2,1)S(1)} %get-tuple-element.54), channel_id=1, source_target_pairs={{0,4},{1,5},{2,6},{3,7},{4,0},{5,1},{6,2},{7,3},{8,12},{9,13},{10,... | collective-permute-start | bytes 393224 | tf_op jit(solution)/shard_map/ppermute | solution.py:495
  14.6 6.9 %collective-permute-start.3 = (bf16[2,256,128]{2,1,0:T(8,128)(2,1)S(1)}, bf16[2,256,128]{2,1,0:T(8,128)(2,1)S(1)}, u32[]{:S(2)}, u32[]{:S(2)}) collective-permute-start(bf16[2,256,128]{2,1,0:T(8,128)(2,1)S(1)} %get-tuple-element.55), channel_id=1, source_target_pairs={{0,6},{1,7},{2,4},{3,5},{4,2},{5,3},{6,0},{7,1},{8,14},{9,15},{10,... | collective-permute-start | bytes 393224 | tf_op jit(solution)/shard_map/ppermute | solution.py:495
  15.8 43.6 %copy-start.2 = (bf16[1,128,128]{2,1,0:T(8,128)(2,1)S(1)}, bf16[1,128,128]{2,1,0:T(8,128)(2,1)}, u32[]{:S(2)}) copy-start(bf16[1,128,128]{2,1,0:T(8,128)(2,1)} %wh_ref.1) | copy-start | bytes 98308
  15.8 43.6 %copy-start.4 = (bf16[1,16,128]{2,1,0:T(8,128)(2,1)S(1)}, bf16[1,16,128]{2,1,0:T(8,128)(2,1)}, u32[]{:S(2)}) copy-start(bf16[1,16,128]{2,1,0:T(8,128)(2,1)} %samp_ref.1) | copy-start | bytes 12292
  15.8 5.8 %collective-permute-start.4 = (bf16[2,256,128]{2,1,0:T(8,128)(2,1)S(1)}, bf16[2,256,128]{2,1,0:T(8,128)(2,1)S(1)}, u32[]{:S(2)}, u32[]{:S(2)}) collective-permute-start(bf16[2,256,128]{2,1,0:T(8,128)(2,1)S(1)} %get-tuple-element.52.refs_0_), channel_id=1, source_target_pairs={{0,1},{1,0},{2,3},{3,2},{4,5},{5,4},{6,7},{7,6},{8,9},{9,8},{10,11... | collective-permute-start | bytes 393224 | tf_op jit(solution)/shard_map/ppermute | solution.py:541
  17.6 3.9 %collective-permute-start.5 = (bf16[2,256,128]{2,1,0:T(8,128)(2,1)S(1)}, bf16[2,256,128]{2,1,0:T(8,128)(2,1)S(1)}, u32[]{:S(2)}, u32[]{:S(2)}) collective-permute-start(bf16[2,256,128]{2,1,0:T(8,128)(2,1)S(1)} %collective-permute-done.1.refs_1_), channel_id=1, source_target_pairs={{0,1},{1,0},{2,3},{3,2},{4,5},{5,4},{6,7},{7,6},{8,9},{9,8},{10,11... | collective-permute-start | bytes 393224 | tf_op jit(solution)/shard_map/ppermute | solution.py:541
  19.4 2.1 %collective-permute-start.6 = (bf16[2,256,128]{2,1,0:T(8,128)(2,1)S(1)}, bf16[2,256,128]{2,1,0:T(8,128)(2,1)S(1)}, u32[]{:S(2)}, u32[]{:S(2)}) collective-permute-start(bf16[2,256,128]{2,1,0:T(8,128)(2,1)S(1)} %collective-permute-done.2.refs_2_), channel_id=1, source_target_pairs={{0,1},{1,0},{2,3},{3,2},{4,5},{5,4},{6,7},{7,6},{8,9},{9,8},{10,11... | collective-permute-start | bytes 393224 | tf_op jit(solution)/shard_map/ppermute | solution.py:541
  21.5 1.3 %collective-permute-start.7 = (bf16[2,256,128]{2,1,0:T(8,128)(2,1)S(1)}, bf16[2,256,128]{2,1,0:T(8,128)(2,1)S(1)}, u32[]{:S(2)}, u32[]{:S(2)}) collective-permute-start(bf16[2,256,128]{2,1,0:T(8,128)(2,1)S(1)} %collective-permute-done.3.refs_3_), channel_id=1, source_target_pairs={{0,1},{1,0},{2,3},{3,2},{4,5},{5,4},{6,7},{7,6},{8,9},{9,8},{10,11... | collective-permute-start | bytes 393224 | tf_op jit(solution)/shard_map/ppermute | solution.py:541
  27.8 1.4 %collective-permute-start.8 = (bf16[256,256]{1,0:T(8,128)(2,1)S(1)}, bf16[256,256]{1,0:T(8,128)(2,1)S(1)}, u32[]{:S(2)}, u32[]{:S(2)}) collective-permute-start(bf16[256,256]{1,0:T(8,128)(2,1)S(1)} %get-tuple-element.58), channel_id=1, source_target_pairs={{0,1},{1,0},{2,3},{3,2},{4,5},{5,4},{6,7},{7,6},{8,9},{9,8},{10,11... | collective-permute-start | bytes 393224 | tf_op jit(solution)/shard_map/ppermute | solution.py:576
  28.0 1.2 %collective-permute-start.9 = (bf16[256,256]{1,0:T(8,128)(2,1)S(1)}, bf16[256,256]{1,0:T(8,128)(2,1)S(1)}, u32[]{:S(2)}, u32[]{:S(2)}) collective-permute-start(bf16[256,256]{1,0:T(8,128)(2,1)S(1)} %get-tuple-element.59), channel_id=1, source_target_pairs={{1,2},{3,4},{5,6},{7,8},{9,10},{11,12},{13,14},{2,1},{4,3},{6,5},{... | collective-permute-start | bytes 393224 | tf_op jit(solution)/shard_map/ppermute | solution.py:577
  36.9 6.9 %collective-permute-start.10 = (bf16[8,216,128]{2,1,0:T(8,128)(2,1)S(1)}, bf16[8,216,128]{2,1,0:T(8,128)(2,1)S(1)}, u32[]{:S(2)}, u32[]{:S(2)}) collective-permute-start(bf16[8,216,128]{2,1,0:T(8,128)(2,1)S(1)} %get-tuple-element.73), channel_id=1, source_target_pairs={{0,1},{1,0},{2,3},{3,2},{4,5},{5,4},{6,7},{7,6},{8,9},{9,8},{10,11... | collective-permute-start | bytes 1327112 | tf_op jit(solution)/shard_map/ppermute | solution.py:605
  43.9 5.4 %collective-permute-start.11 = (bf16[2,216,128]{2,1,0:T(8,128)(2,1)S(1)}, bf16[2,216,128]{2,1,0:T(8,128)(2,1)S(1)}, u32[]{:S(2)}, u32[]{:S(2)}) collective-permute-start(bf16[2,216,128]{2,1,0:T(8,128)(2,1)S(1)} %get-tuple-element.75), channel_id=1, source_target_pairs={{0,2},{1,3},{2,0},{3,1},{4,6},{5,7},{6,4},{7,5},{8,10},{9,11},{10,... | collective-permute-start | bytes 331784 | tf_op jit(solution)/shard_map/ppermute | solution.py:495
  45.7 5.5 %collective-permute-start.12 = (bf16[2,216,128]{2,1,0:T(8,128)(2,1)S(1)}, bf16[2,216,128]{2,1,0:T(8,128)(2,1)S(1)}, u32[]{:S(2)}, u32[]{:S(2)}) collective-permute-start(bf16[2,216,128]{2,1,0:T(8,128)(2,1)S(1)} %get-tuple-element.76), channel_id=1, source_target_pairs={{0,4},{1,5},{2,6},{3,7},{4,0},{5,1},{6,2},{7,3},{8,12},{9,13},{10,... | collective-permute-start | bytes 331784 | tf_op jit(solution)/shard_map/ppermute | solution.py:495
  47.4 6.2 %collective-permute-start.13 = (bf16[2,216,128]{2,1,0:T(8,128)(2,1)S(1)}, bf16[2,216,128]{2,1,0:T(8,128)(2,1)S(1)}, u32[]{:S(2)}, u32[]{:S(2)}) collective-permute-start(bf16[2,216,128]{2,1,0:T(8,128)(2,1)S(1)} %get-tuple-element.77), channel_id=1, source_target_pairs={{0,6},{1,7},{2,4},{3,5},{4,2},{5,3},{6,0},{7,1},{8,14},{9,15},{10,... | collective-permute-start | bytes 331784 | tf_op jit(solution)/shard_map/ppermute | solution.py:495
  53.6 5.8 %collective-permute-start.14 = (bf16[216,128]{1,0:T(8,128)(2,1)S(1)}, bf16[216,128]{1,0:T(8,128)(2,1)S(1)}, u32[]{:S(2)}, u32[]{:S(2)}) collective-permute-start(bf16[216,128]{1,0:T(8,128)(2,1)S(1)} %get-tuple-element.79), channel_id=1, source_target_pairs={{0,8},{1,9},{2,10},{3,11},{4,12},{5,13},{6,14},{7,15},{8,0},{9,1},... | collective-permute-start | bytes 165896 | tf_op jit(solution)/shard_map/ppermute | solution.py:495

commit v6 on v5

--- a/solution.py
+++ b/solution.py
@@ -435,10 +435,13 @@
         out[to, G2_AT:PART_ROWS] = tail_ref[r].astype(BF16)
 
 
-def flip_kernel(target_ref, decoder_ref, near_ref, target_out, decoder_out, same_out, near_out):
+def flip_target_kernel(target_ref, near_ref, target_out, near_out):
     near_out[...] = near_ref[...]
+    target_out[...] = target_ref[...].astype(F32).T.astype(BF16)
+
+
+def flip_decoder_kernel(decoder_ref, decoder_out, same_out):
     same_out[...] = decoder_ref[...]
-    target_out[...] = target_ref[...].astype(F32).T.astype(BF16)
     decoder_out[...] = decoder_ref[...].astype(F32).T.astype(BF16)
 
 
@@ -495,7 +498,8 @@
         return lax.ppermute(block, "region", [(i, i ^ (2 * k)) for i in range(regions)])
 
     def to_half(blocks):
-        return [blocks[0]] + [to_chip(blocks[k], k) for k in range(1, quarter)]
+        sent = {k: to_chip(blocks[k], k) for k in reversed(range(1, quarter))}
+        return [blocks[0]] + [sent[k] for k in range(1, quarter)]
 
     pack_args = (
         pixel_of_ray.reshape(1, rays), seg_region.T, seg_count.T,
@@ -519,17 +523,12 @@
     )(*pack_args)
     far = to_chip(far, quarter)
     flipped = pl.pallas_call(
-        flip_kernel,
-        out_shape=(
-            shape(dino_width, rays, kind=BF16),
-            shape(*decoder.shape[::-1], kind=BF16),
-            shape(*decoder.shape, kind=BF16),
-            shape(*near.shape, kind=BF16),
-        ),
+        flip_target_kernel,
+        out_shape=(shape(dino_width, rays, kind=BF16), shape(*near.shape, kind=BF16)),
         compiler_params=grant(8 + regions / 8),
-        name="flip",
-    )(target, decoder, near)
-    far, (target_t, decoder_t, decoder, near) = lax.optimization_barrier((far, flipped))
+        name="flip_target",
+    )(target, near)
+    far, (target_t, near) = lax.optimization_barrier((far, flipped))
     blocks = to_half(
         pl.pallas_call(
             relay_kernel,
@@ -575,12 +574,19 @@
 
     halo_in = lax.ppermute(halo_in, "region", inner)
     halo_cr = lax.ppermute(halo_cr, "region", cross)
+    decoder, sums = lax.optimization_barrier((decoder, kept[2]))
+    decoder_t, decoder = pl.pallas_call(
+        flip_decoder_kernel,
+        out_shape=(shape(*decoder.shape[::-1], kind=BF16), shape(*decoder.shape, kind=BF16)),
+        compiler_params=grant(8),
+        name="flip_decoder",
+    )(decoder)
     folded = pl.pallas_call(
         fold_kernel,
         out_shape=shape(regions, hid_width, rays, kind=BF16),
         compiler_params=grant(8 + regions / 4),
         name="fold",
-    )(kept[2], kept[7])
+    )(sums, kept[7])
 
     part = shape(half, PART_ROWS, LANES, kind=BF16)
     mine, other = pl.pallas_call(

time: 60.5 us -> 60.5 us (level)
  starting transfers between devices: 21.3 us -> 20.1 us
  waiting for transfers between devices: 18.8 us -> 19.9 us
    ppermute x1, starting transfers between devices: 5.47 us -> 4.24 us  [local(): theirs = lax.ppermute(other, 'region', inner)]
    ppermute x8, waiting for transfers between devices: 16 us -> 17.2 us  [to_chip(): lax.ppermute(block, 'region', [(i, i ^ 2 * k) for i in range(regions)])]
where the time goes in v6:
time: 60.5 us; the launch traced here: 60.2 us
  starting transfers between devices  20.1 us (33%)
  waiting for transfers between devices  19.9 us (33%)
  Pallas kernels  16.6 us (27%)
  local copies, waits for them, and re-layouts  2.84 us (5%)
  between operations  0.74 us (1%)
    ppermute x8, waiting for transfers between devices, to_chip(): lax.ppermute(block, 'region', [(i, i ^ 2 * k) for i in range(regions)])  17.2 us
    ppermute x8, starting transfers between devices, to_chip(): lax.ppermute(block, 'region', [(i, i ^ 2 * k) for i in range(regions)])  15 us
    pallas_call x1, Pallas kernels, local(): pl.pallas_call(functools.partial(backward_kernel, half), out_shape=(part,...  7.71 us
    pallas_call x1, Pallas kernels, local(): pl.pallas_call(functools.partial(forward_kernel, half, group, room), out_...  4.9 us
    ppermute x1, starting transfers between devices, local(): theirs = lax.ppermute(other, 'region', inner)  4.24 us
    unnamed x10, local copies, waits for them, and re-layouts  2.84 us
    pallas_call x1, Pallas kernels, local(): pl.pallas_call(functools.partial(pack_kernel, half, group, room), out_sha...  2.11 us
    ppermute x1, waiting for transfers between devices, local(): theirs = lax.ppermute(other, 'region', inner)  1.42 us
  transfers between devices with their start and end apart: 15, of which 10 were waited for; matrix products, arithmetic and copies ran while one was open for 0% of the time, Pallas kernels for 1%

profile of v6, /device:TPU:0, one launch (start us, length us, event | category | flops | bytes accessed | tf_op | source)
XLA Modules:
  0.0 60.2 jit_solution(10935104933914579843)
XLA Ops:
  0.6 2.1 %pack.1 = (bf16[400,128]{1,0:T(8,128)(2,1)}, bf16[400,128]{1,0:T(8,128)(2,1)}) custom-call(s32[1,256]{1,0:T(1,128)} %bitcast.8, s32[4,256]{1,0:T(4,128)} %bitcast.6, s32[4,256]{1,0:T(4,128)} %bitcast.7, bf16[256,128]{1,0:T(8,128)(2,1)} %refs_3_.1, bf16[1,16,128]{2,1,0:T(8,128)(2,1)} %samp_ref.1, bf16[1,128,128]{2,1,0:T(8,128)(2,1)} %wh_ref.1, ...), custom_call_target="tpu_custom_call" | custom-call | tf_op jit(solution)/shard_map/pack/pallas_call | solution.py:508
  2.8 4.1 %collective-permute-start = (bf16[400,128]{1,0:T(8,128)(2,1)}, bf16[400,128]{1,0:T(8,128)(2,1)S(1)}, u32[]{:S(2)}, u32[]{:S(2)}) collective-permute-start(bf16[400,128]{1,0:T(8,128)(2,1)} %get-tuple-element.44), channel_id=1, source_target_pairs={{0,8},{1,9},{2,10},{3,11},{4,12},{5,13},{6,14},{7,15},{8,0},{9,1},... | collective-permute-start | bytes 307208 | tf_op jit(solution)/shard_map/ppermute | solution.py:498
  6.9 0.0 copy-start.1
  6.9 0.9 %copy-done.1 = bf16[256,384]{1,0:T(8,128)(2,1)S(1)} copy-done((bf16[256,384]{1,0:T(8,128)(2,1)S(1)}, bf16[256,384]{1,0:T(8,128)(2,1)}, u32[]{:S(2)}) %copy-start.1) | copy-done | bytes 196632
  7.8 0.0 copy-start.3
  7.8 0.9 %copy-done.3 = bf16[400,128]{1,0:T(8,128)(2,1)S(1)} copy-done((bf16[400,128]{1,0:T(8,128)(2,1)S(1)}, bf16[400,128]{1,0:T(8,128)(2,1)}, u32[]{:S(2)}) %copy-start.3) | copy-done | bytes 102424
  8.7 0.1 flip_target.1
  8.8 3.3 %collective-permute-done.far_ref = bf16[400,128]{1,0:T(8,128)(2,1)S(1)} collective-permute-done((bf16[400,128]{1,0:T(8,128)(2,1)}, bf16[400,128]{1,0:T(8,128)(2,1)S(1)}, u32[]{:S(2)}, u32[]{:S(2)}) %collective-permute-start) | collective-permute-done | bytes 102432 | tf_op jit(solution)/shard_map/ppermute | solution.py:498
  12.1 0.1 relay.1
  12.2 1.6 %collective-permute-start.1 = (bf16[2,256,128]{2,1,0:T(8,128)(2,1)S(1)}, bf16[2,256,128]{2,1,0:T(8,128)(2,1)S(1)}, u32[]{:S(2)}, u32[]{:S(2)}) collective-permute-start(bf16[2,256,128]{2,1,0:T(8,128)(2,1)S(1)} %get-tuple-element.51), channel_id=1, source_target_pairs={{0,2},{1,3},{2,0},{3,1},{4,6},{5,7},{6,4},{7,5},{8,10},{9,11},{10,... | collective-permute-start | bytes 393224 | tf_op jit(solution)/shard_map/ppermute | solution.py:498
  13.8 0.8 %collective-permute-start.2 = (bf16[2,256,128]{2,1,0:T(8,128)(2,1)S(1)}, bf16[2,256,128]{2,1,0:T(8,128)(2,1)S(1)}, u32[]{:S(2)}, u32[]{:S(2)}) collective-permute-start(bf16[2,256,128]{2,1,0:T(8,128)(2,1)S(1)} %get-tuple-element.52), channel_id=1, source_target_pairs={{0,4},{1,5},{2,6},{3,7},{4,0},{5,1},{6,2},{7,3},{8,12},{9,13},{10,... | collective-permute-start | bytes 393224 | tf_op jit(solution)/shard_map/ppermute | solution.py:498
  14.6 1.2 %collective-permute-start.3 = (bf16[2,256,128]{2,1,0:T(8,128)(2,1)S(1)}, bf16[2,256,128]{2,1,0:T(8,128)(2,1)S(1)}, u32[]{:S(2)}, u32[]{:S(2)}) collective-permute-start(bf16[2,256,128]{2,1,0:T(8,128)(2,1)S(1)} %get-tuple-element.53), channel_id=1, source_target_pairs={{0,6},{1,7},{2,4},{3,5},{4,2},{5,3},{6,0},{7,1},{8,14},{9,15},{10,... | collective-permute-start | bytes 393224 | tf_op jit(solution)/shard_map/ppermute | solution.py:498
  15.8 0.0 copy-start.2
  15.8 0.0 copy-start.4
  15.8 0.0 collective-permute-start.4
  15.8 1.8 %collective-permute-done.1.refs_1_ = bf16[2,256,128]{2,1,0:T(8,128)(2,1)S(1)} collective-permute-done((bf16[2,256,128]{2,1,0:T(8,128)(2,1)S(1)}, bf16[2,256,128]{2,1,0:T(8,128)(2,1)S(1)}, u32[]{:S(2)}, u32[]{:S(2)}) %collective-permute-start.1) | collective-permute-done | bytes 131104 | tf_op jit(solution)/shard_map/ppermute | solution.py:498
  17.6 0.0 collective-permute-start.5
  17.6 1.8 %collective-permute-done.2.refs_2_ = bf16[2,256,128]{2,1,0:T(8,128)(2,1)S(1)} collective-permute-done((bf16[2,256,128]{2,1,0:T(8,128)(2,1)S(1)}, bf16[2,256,128]{2,1,0:T(8,128)(2,1)S(1)}, u32[]{:S(2)}, u32[]{:S(2)}) %collective-permute-start.2) | collective-permute-done | bytes 131104 | tf_op jit(solution)/shard_map/ppermute | solution.py:498
  19.4 0.0 collective-permute-start.6
  19.4 2.1 %collective-permute-done.3.refs_3_ = bf16[2,256,128]{2,1,0:T(8,128)(2,1)S(1)} collective-permute-done((bf16[2,256,128]{2,1,0:T(8,128)(2,1)S(1)}, bf16[2,256,128]{2,1,0:T(8,128)(2,1)S(1)}, u32[]{:S(2)}, u32[]{:S(2)}) %collective-permute-start.3) | collective-permute-done | bytes 131104 | tf_op jit(solution)/shard_map/ppermute | solution.py:498
  21.5 0.0 collective-permute-start.7
  21.5 0.0 collective-permute-done.4.refs_4_
  21.5 0.0 collective-permute-done.5.refs_5_
  21.5 0.0 collective-permute-done.6.refs_6_
  21.5 1.3 %collective-permute-done.7.refs_7_ = bf16[2,256,128]{2,1,0:T(8,128)(2,1)S(1)} collective-permute-done((bf16[2,256,128]{2,1,0:T(8,128)(2,1)S(1)}, bf16[2,256,128]{2,1,0:T(8,128)(2,1)S(1)}, u32[]{:S(2)}, u32[]{:S(2)}) %collective-permute-start.7) | collective-permute-done | bytes 131104 | tf_op jit(solution)/shard_map/ppermute | solution.py:540
  22.9 4.9 %forward.1 = (bf16[64,256]{1,0:T(8,128)(2,1)S(1)}, bf16[256,256]{1,0:T(8,128)(2,1)S(1)}, bf16[256,256]{1,0:T(8,128)(2,1)S(1)}, f32[8,16,128,128]{3,2,1,0:T(8,128...) custom-call(bf16[2,256,128]{2,1,0:T(8,128)(2,1)S(1)} %get-tuple-elem, ...), custom_call_target="tpu_custom_call" | custom-call | tf_op jit(solution)/shard_map/forward/pallas_call | solution.py:542
  27.8 0.2 collective-permute-start.8
  28.0 0.7 %collective-permute-start.9 = (bf16[256,256]{1,0:T(8,128)(2,1)S(1)}, bf16[256,256]{1,0:T(8,128)(2,1)S(1)}, u32[]{:S(2)}, u32[]{:S(2)}) collective-permute-start(bf16[256,256]{1,0:T(8,128)(2,1)S(1)} %get-tuple-element.57), channel_id=1, source_target_pairs={{1,2},{3,4},{5,6},{7,8},{9,10},{11,12},{13,14},{2,1},{4,3},{6,5},{... | collective-permute-start | bytes 393224 | tf_op jit(solution)/shard_map/ppermute | solution.py:576
  28.6 0.0 copy-start
  28.7 1.0 %copy-done = bf16[576,384]{1,0:T(8,128)(2,1)S(1)} copy-done((bf16[576,384]{1,0:T(8,128)(2,1)S(1)}, bf16[576,384]{1,0:T(8,128)(2,1)}, u32[]{:S(2)}) %copy-start) | copy-done | bytes 442392
  29.7 0.2 flip_decoder.1
  29.9 0.5 fold.1.folded_ref
  30.4 0.0 collective-permute-done.8.inner_ref
  30.4 0.0 collective-permute-done.9.cross_ref
  30.4 7.7 %backward.1 = (bf16[8,216,128]{2,1,0:T(8,128)(2,1)S(1)}, bf16[8,216,128]{2,1,0:T(8,128)(2,1)S(1)}) custom-call(bf16[64,256]{1,0:T(8,128)(2,1)S(1)} %get-tuple-element.55.own_ref, bf16[256,256]{1,0:T(8,128)(2,1)S(1)} %collective-permute-done.8.inner_ref, bf16[256,256]{1,0:T(8,128)(2,1)S(1)} %collective-permute-done.9.cross_ref, ...), custom_call_target="tpu_custom_call" | custom-call | tf_op jit(solution)/shard_map/backward/pallas_call | solution.py:592
  38.1 4.2 %collective-permute-start.10 = (bf16[8,216,128]{2,1,0:T(8,128)(2,1)S(1)}, bf16[8,216,128]{2,1,0:T(8,128)(2,1)S(1)}, u32[]{:S(2)}, u32[]{:S(2)}) collective-permute-start(bf16[8,216,128]{2,1,0:T(8,128)(2,1)S(1)} %get-tuple-element.73), channel_id=1, source_target_pairs={{0,1},{1,0},{2,3},{3,2},{4,5},{5,4},{6,7},{7,6},{8,9},{9,8},{10,11... | collective-permute-start | bytes 1327112 | tf_op jit(solution)/shard_map/ppermute | solution.py:611
  42.4 1.4 %collective-permute-done.10.theirs_ref = bf16[8,216,128]{2,1,0:T(8,128)(2,1)S(1)} collective-permute-done((bf16[8,216,128]{2,1,0:T(8,128)(2,1)S(1)}, bf16[8,216,128]{2,1,0:T(8,128)(2,1)S(1)}, u32[]{:S(2)}, u32[]{:S(2)}) %collective-permute-start.10) | collective-permute-done | bytes 442400 | tf_op jit(solution)/shard_map/ppermute | solution.py:611
  43.8 0.1 merge.1
  43.9 1.8 %collective-permute-start.11 = (bf16[2,216,128]{2,1,0:T(8,128)(2,1)S(1)}, bf16[2,216,128]{2,1,0:T(8,128)(2,1)S(1)}, u32[]{:S(2)}, u32[]{:S(2)}) collective-permute-start(bf16[2,216,128]{2,1,0:T(8,128)(2,1)S(1)} %get-tuple-element.75), channel_id=1, source_target_pairs={{0,2},{1,3},{2,0},{3,1},{4,6},{5,7},{6,4},{7,5},{8,10},{9,11},{10,... | collective-permute-start | bytes 331784 | tf_op jit(solution)/shard_map/ppermute | solution.py:498
  45.7 1.7 %collective-permute-start.12 = (bf16[2,216,128]{2,1,0:T(8,128)(2,1)S(1)}, bf16[2,216,128]{2,1,0:T(8,128)(2,1)S(1)}, u32[]{:S(2)}, u32[]{:S(2)}) collective-permute-start(bf16[2,216,128]{2,1,0:T(8,128)(2,1)S(1)} %get-tuple-element.76), channel_id=1, source_target_pairs={{0,4},{1,5},{2,6},{3,7},{4,0},{5,1},{6,2},{7,3},{8,12},{9,13},{10,... | collective-permute-start | bytes 331784 | tf_op jit(solution)/shard_map/ppermute | solution.py:498
  47.4 0.5 collective-permute-start.13
  47.9 1.4 %collective-permute-done.11.refs_1_ = bf16[2,216,128]{2,1,0:T(8,128)(2,1)S(1)} collective-permute-done((bf16[2,216,128]{2,1,0:T(8,128)(2,1)S(1)}, bf16[2,216,128]{2,1,0:T(8,128)(2,1)S(1)}, u32[]{:S(2)}, u32[]{:S(2)}) %collective-permute-start.11) | collective-permute-done | bytes 110624 | tf_op jit(solution)/shard_map/ppermute | solution.py:498
  49.3 1.9 %collective-permute-done.12.refs_2_ = bf16[2,216,128]{2,1,0:T(8,128)(2,1)S(1)} collective-permute-done((bf16[2,216,128]{2,1,0:T(8,128)(2,1)S(1)}, bf16[2,216,128]{2,1,0:T(8,128)(2,1)S(1)}, u32[]{:S(2)}, u32[]{:S(2)}) %collective-permute-start.12) | collective-permute-done | bytes 110624 | tf_op jit(solution)/shard_map/ppermute | solution.py:498
  51.2 2.4 %collective-permute-done.13.refs_3_ = bf16[2,216,128]{2,1,0:T(8,128)(2,1)S(1)} collective-permute-done((bf16[2,216,128]{2,1,0:T(8,128)(2,1)S(1)}, bf16[2,216,128]{2,1,0:T(8,128)(2,1)S(1)}, u32[]{:S(2)}, u32[]{:S(2)}) %collective-permute-start.13) | collective-permute-done | bytes 110624 | tf_op jit(solution)/shard_map/ppermute | solution.py:498
  53.5 0.1 reduce.1
  53.6 3.3 %collective-permute-start.14 = (bf16[216,128]{1,0:T(8,128)(2,1)S(1)}, bf16[216,128]{1,0:T(8,128)(2,1)S(1)}, u32[]{:S(2)}, u32[]{:S(2)}) collective-permute-start(bf16[216,128]{1,0:T(8,128)(2,1)S(1)} %get-tuple-element.79), channel_id=1, source_target_pairs={{0,8},{1,9},{2,10},{3,11},{4,12},{5,13},{6,14},{7,15},{8,0},{9,1},... | collective-permute-start | bytes 165896 | tf_op jit(solution)/shard_map/ppermute | solution.py:498
  57.0 2.5 %collective-permute-done.14.part_ref = bf16[216,128]{1,0:T(8,128)(2,1)S(1)} collective-permute-done((bf16[216,128]{1,0:T(8,128)(2,1)S(1)}, bf16[216,128]{1,0:T(8,128)(2,1)S(1)}, u32[]{:S(2)}, u32[]{:S(2)}) %collective-permute-start.14) | collective-permute-done | bytes 55328 | tf_op jit(solution)/shard_map/ppermute | solution.py:498
  59.4 0.0 copy-done.2
  59.4 0.0 copy-done.4
  59.4 0.8 %finish.1 = (f32[1,128,128]{2,1,0:T(8,128)}, f32[1,64,128]{2,1,0:T(8,128)}, f32[1,128]{1,0:T(1,128)}, f32[1,16,128]{2,1,0:T(8,128)}) custom-call(f32[216,128]{1,0:T(8,128)S(1)} %get-tuple-element.78.keep_ref, bf16[216,128]{1,0:T(8,128)(2,1)S(1)} %collective-permute-done.14.part_ref, bf16[1,16,128]{2,1,0:T(8,128)(2,1)S(1)} %copy-done.4, ...), custom_call_target="tpu_custom_call" | custom-call | tf_op jit(solution)/shard_map/finish/pallas_call | solution.py:624
Async XLA Ops:
  2.8 9.4 %collective-permute-start = (bf16[400,128]{1,0:T(8,128)(2,1)}, bf16[400,128]{1,0:T(8,128)(2,1)S(1)}, u32[]{:S(2)}, u32[]{:S(2)}) collective-permute-start(bf16[400,128]{1,0:T(8,128)(2,1)} %get-tuple-element.44), channel_id=1, source_target_pairs={{0,8},{1,9},{2,10},{3,11},{4,12},{5,13},{6,14},{7,15},{8,0},{9,1},... | collective-permute-start | bytes 307208 | tf_op jit(solution)/shard_map/ppermute | solution.py:498
  6.9 0.9 %copy-start.1 = (bf16[256,384]{1,0:T(8,128)(2,1)S(1)}, bf16[256,384]{1,0:T(8,128)(2,1)}, u32[]{:S(2)}) copy-start(bf16[256,384]{1,0:T(8,128)(2,1)} %target_ref.1) | copy-start | bytes 589828
  7.8 0.9 %copy-start.3 = (bf16[400,128]{1,0:T(8,128)(2,1)S(1)}, bf16[400,128]{1,0:T(8,128)(2,1)}, u32[]{:S(2)}) copy-start(bf16[400,128]{1,0:T(8,128)(2,1)} %get-tuple-element.45.near_ref) | copy-start | bytes 307204
  12.2 5.4 %collective-permute-start.1 = (bf16[2,256,128]{2,1,0:T(8,128)(2,1)S(1)}, bf16[2,256,128]{2,1,0:T(8,128)(2,1)S(1)}, u32[]{:S(2)}, u32[]{:S(2)}) collective-permute-start(bf16[2,256,128]{2,1,0:T(8,128)(2,1)S(1)} %get-tuple-element.51), channel_id=1, source_target_pairs={{0,2},{1,3},{2,0},{3,1},{4,6},{5,7},{6,4},{7,5},{8,10},{9,11},{10,... | collective-permute-start | bytes 393224 | tf_op jit(solution)/shard_map/ppermute | solution.py:498
  13.8 5.6 %collective-permute-start.2 = (bf16[2,256,128]{2,1,0:T(8,128)(2,1)S(1)}, bf16[2,256,128]{2,1,0:T(8,128)(2,1)S(1)}, u32[]{:S(2)}, u32[]{:S(2)}) collective-permute-start(bf16[2,256,128]{2,1,0:T(8,128)(2,1)S(1)} %get-tuple-element.52), channel_id=1, source_target_pairs={{0,4},{1,5},{2,6},{3,7},{4,0},{5,1},{6,2},{7,3},{8,12},{9,13},{10,... | collective-permute-start | bytes 393224 | tf_op jit(solution)/shard_map/ppermute | solution.py:498
  14.6 6.9 %collective-permute-start.3 = (bf16[2,256,128]{2,1,0:T(8,128)(2,1)S(1)}, bf16[2,256,128]{2,1,0:T(8,128)(2,1)S(1)}, u32[]{:S(2)}, u32[]{:S(2)}) collective-permute-start(bf16[2,256,128]{2,1,0:T(8,128)(2,1)S(1)} %get-tuple-element.53), channel_id=1, source_target_pairs={{0,6},{1,7},{2,4},{3,5},{4,2},{5,3},{6,0},{7,1},{8,14},{9,15},{10,... | collective-permute-start | bytes 393224 | tf_op jit(solution)/shard_map/ppermute | solution.py:498
  15.8 43.6 %copy-start.2 = (bf16[1,128,128]{2,1,0:T(8,128)(2,1)S(1)}, bf16[1,128,128]{2,1,0:T(8,128)(2,1)}, u32[]{:S(2)}) copy-start(bf16[1,128,128]{2,1,0:T(8,128)(2,1)} %wh_ref.1) | copy-start | bytes 98308
  15.8 43.6 %copy-start.4 = (bf16[1,16,128]{2,1,0:T(8,128)(2,1)S(1)}, bf16[1,16,128]{2,1,0:T(8,128)(2,1)}, u32[]{:S(2)}) copy-start(bf16[1,16,128]{2,1,0:T(8,128)(2,1)} %samp_ref.1) | copy-start | bytes 12292
  15.8 5.8 %collective-permute-start.4 = (bf16[2,256,128]{2,1,0:T(8,128)(2,1)S(1)}, bf16[2,256,128]{2,1,0:T(8,128)(2,1)S(1)}, u32[]{:S(2)}, u32[]{:S(2)}) collective-permute-start(bf16[2,256,128]{2,1,0:T(8,128)(2,1)S(1)} %get-tuple-element.50.refs_0_), channel_id=1, source_target_pairs={{0,1},{1,0},{2,3},{3,2},{4,5},{5,4},{6,7},{7,6},{8,9},{9,8},{10,11... | collective-permute-start | bytes 393224 | tf_op jit(solution)/shard_map/ppermute | solution.py:540
  17.6 3.9 %collective-permute-start.5 = (bf16[2,256,128]{2,1,0:T(8,128)(2,1)S(1)}, bf16[2,256,128]{2,1,0:T(8,128)(2,1)S(1)}, u32[]{:S(2)}, u32[]{:S(2)}) collective-permute-start(bf16[2,256,128]{2,1,0:T(8,128)(2,1)S(1)} %collective-permute-done.1.refs_1_), channel_id=1, source_target_pairs={{0,1},{1,0},{2,3},{3,2},{4,5},{5,4},{6,7},{7,6},{8,9},{9,8},{10,11... | collective-permute-start | bytes 393224 | tf_op jit(solution)/shard_map/ppermute | solution.py:540
  19.4 2.1 %collective-permute-start.6 = (bf16[2,256,128]{2,1,0:T(8,128)(2,1)S(1)}, bf16[2,256,128]{2,1,0:T(8,128)(2,1)S(1)}, u32[]{:S(2)}, u32[]{:S(2)}) collective-permute-start(bf16[2,256,128]{2,1,0:T(8,128)(2,1)S(1)} %collective-permute-done.2.refs_2_), channel_id=1, source_target_pairs={{0,1},{1,0},{2,3},{3,2},{4,5},{5,4},{6,7},{7,6},{8,9},{9,8},{10,11... | collective-permute-start | bytes 393224 | tf_op jit(solution)/shard_map/ppermute | solution.py:540
  21.5 1.3 %collective-permute-start.7 = (bf16[2,256,128]{2,1,0:T(8,128)(2,1)S(1)}, bf16[2,256,128]{2,1,0:T(8,128)(2,1)S(1)}, u32[]{:S(2)}, u32[]{:S(2)}) collective-permute-start(bf16[2,256,128]{2,1,0:T(8,128)(2,1)S(1)} %collective-permute-done.3.refs_3_), channel_id=1, source_target_pairs={{0,1},{1,0},{2,3},{3,2},{4,5},{5,4},{6,7},{7,6},{8,9},{9,8},{10,11... | collective-permute-start | bytes 393224 | tf_op jit(solution)/shard_map/ppermute | solution.py:540
  27.8 2.6 %collective-permute-start.8 = (bf16[256,256]{1,0:T(8,128)(2,1)S(1)}, bf16[256,256]{1,0:T(8,128)(2,1)S(1)}, u32[]{:S(2)}, u32[]{:S(2)}) collective-permute-start(bf16[256,256]{1,0:T(8,128)(2,1)S(1)} %get-tuple-element.56), channel_id=1, source_target_pairs={{0,1},{1,0},{2,3},{3,2},{4,5},{5,4},{6,7},{7,6},{8,9},{9,8},{10,11... | collective-permute-start | bytes 393224 | tf_op jit(solution)/shard_map/ppermute | solution.py:575
  28.0 2.4 %collective-permute-start.9 = (bf16[256,256]{1,0:T(8,128)(2,1)S(1)}, bf16[256,256]{1,0:T(8,128)(2,1)S(1)}, u32[]{:S(2)}, u32[]{:S(2)}) collective-permute-start(bf16[256,256]{1,0:T(8,128)(2,1)S(1)} %get-tuple-element.57), channel_id=1, source_target_pairs={{1,2},{3,4},{5,6},{7,8},{9,10},{11,12},{13,14},{2,1},{4,3},{6,5},{... | collective-permute-start | bytes 393224 | tf_op jit(solution)/shard_map/ppermute | solution.py:576
  28.6 1.0 %copy-start = (bf16[576,384]{1,0:T(8,128)(2,1)S(1)}, bf16[576,384]{1,0:T(8,128)(2,1)}, u32[]{:S(2)}) copy-start(bf16[576,384]{1,0:T(8,128)(2,1)} %decoder_ref) | copy-start | bytes 1327108
  38.1 5.7 %collective-permute-start.10 = (bf16[8,216,128]{2,1,0:T(8,128)(2,1)S(1)}, bf16[8,216,128]{2,1,0:T(8,128)(2,1)S(1)}, u32[]{:S(2)}, u32[]{:S(2)}) collective-permute-start(bf16[8,216,128]{2,1,0:T(8,128)(2,1)S(1)} %get-tuple-element.73), channel_id=1, source_target_pairs={{0,1},{1,0},{2,3},{3,2},{4,5},{5,4},{6,7},{7,6},{8,9},{9,8},{10,11... | collective-permute-start | bytes 1327112 | tf_op jit(solution)/shard_map/ppermute | solution.py:611
  43.9 5.4 %collective-permute-start.11 = (bf16[2,216,128]{2,1,0:T(8,128)(2,1)S(1)}, bf16[2,216,128]{2,1,0:T(8,128)(2,1)S(1)}, u32[]{:S(2)}, u32[]{:S(2)}) collective-permute-start(bf16[2,216,128]{2,1,0:T(8,128)(2,1)S(1)} %get-tuple-element.75), channel_id=1, source_target_pairs={{0,2},{1,3},{2,0},{3,1},{4,6},{5,7},{6,4},{7,5},{8,10},{9,11},{10,... | collective-permute-start | bytes 331784 | tf_op jit(solution)/shard_map/ppermute | solution.py:498
  45.7 5.5 %collective-permute-start.12 = (bf16[2,216,128]{2,1,0:T(8,128)(2,1)S(1)}, bf16[2,216,128]{2,1,0:T(8,128)(2,1)S(1)}, u32[]{:S(2)}, u32[]{:S(2)}) collective-permute-start(bf16[2,216,128]{2,1,0:T(8,128)(2,1)S(1)} %get-tuple-element.76), channel_id=1, source_target_pairs={{0,4},{1,5},{2,6},{3,7},{4,0},{5,1},{6,2},{7,3},{8,12},{9,13},{10,... | collective-permute-start | bytes 331784 | tf_op jit(solution)/shard_map/ppermute | solution.py:498
  47.4 6.1 %collective-permute-start.13 = (bf16[2,216,128]{2,1,0:T(8,128)(2,1)S(1)}, bf16[2,216,128]{2,1,0:T(8,128)(2,1)S(1)}, u32[]{:S(2)}, u32[]{:S(2)}) collective-permute-start(bf16[2,216,128]{2,1,0:T(8,128)(2,1)S(1)} %get-tuple-element.77), channel_id=1, source_target_pairs={{0,6},{1,7},{2,4},{3,5},{4,2},{5,3},{6,0},{7,1},{8,14},{9,15},{10,... | collective-permute-start | bytes 331784 | tf_op jit(solution)/shard_map/ppermute | solution.py:498
  53.6 5.8 %collective-permute-start.14 = (bf16[216,128]{1,0:T(8,128)(2,1)S(1)}, bf16[216,128]{1,0:T(8,128)(2,1)S(1)}, u32[]{:S(2)}, u32[]{:S(2)}) collective-permute-start(bf16[216,128]{1,0:T(8,128)(2,1)S(1)} %get-tuple-element.79), channel_id=1, source_target_pairs={{0,8},{1,9},{2,10},{3,11},{4,12},{5,13},{6,14},{7,15},{8,0},{9,1},... | collective-permute-start | bytes 165896 | tf_op jit(solution)/shard_map/ppermute | solution.py:498
